TPU v7x, 256 devices: a whole 4x4x8 slice. The times are simulated.
256 devices in a mesh: dp: 16 (over z_hi, x, core), space: 16 (over z_lo, y).
Axes of the slice: x: 4, y: 4, z: 8 (z_hi: 2, z_lo: 4; z = z_hi * 4 + z_lo), core: 2. Of those that a mesh axis runs over, the one named last changes fastest.
Arguments:
- volume: bfloat16 [16, 4, 128, 8, 256], P('dp', None, 'space'), may hold values from -6 to 6
- first_filters: bfloat16 [16, 4, 3, 3, 3], replicated, may hold values from -0.625 to 0.625
- first_biases: float32 [16], replicated, may hold values from -0.5 to 0.5
- second_filters: bfloat16 [32, 16, 3, 3, 3], replicated, may hold values from -0.3125 to 0.3125
- second_biases: float32 [32], replicated, may hold values from -0.5 to 0.5
- cotangent: bfloat16 [16, 32, 64, 4, 128], P('dp', None, 'space'), may hold values from -12 to 12
Outputs:
- activations: bfloat16 [16, 32, 64, 4, 128], P('dp', None, 'space')
- pooled_grad: bfloat16 [16, 16, 64, 4, 128], P('dp', None, 'space')
- gradient_one: float32 [16, 4, 3, 3, 3], replicated
- shift_one: float32 [16], replicated
- gradient_two: float32 [32, 16, 3, 3, 3], replicated
- shift_two: float32 [32], replicated
All inputs are finite; a program needn't handle non-finite values.
Results may differ from a plain program's by a relative error of at most 0.015.
The roundings to bfloat16 on the way count: a program that leaves them out, or rounds other values in their place, can miss the bound.
Values may be sent and summed in bfloat16 or wider, within the bound.
No kernel may reach another device: no remote copies, remote signals or barrier semaphores. Data moves between devices by JAX's collectives and lax.ppermute only.
A program may use at most 128 MiB of HBM per device.

v0:
```python
import math

import jax
import jax.numpy as jnp
from jax import lax
from jax.sharding import PartitionSpec as P


def with_halo(block, sides, width):
    for axis, dim in sides:
        count = lax.axis_size(axis)
        forward = [(i, i + 1) for i in range(count - 1)]
        backward = [(target, source) for source, target in forward]
        low = lax.ppermute(
            lax.slice_in_dim(block, block.shape[dim] - width, None, axis=dim), axis, forward
        )
        high = lax.ppermute(lax.slice_in_dim(block, 0, width, axis=dim), axis, backward)
        block = jnp.concatenate([low, block, high], axis=dim)
    return block


def convolve(padded, kernel):
    return lax.conv_general_dilated(
        padded[None],
        kernel,
        (1, 1, 1),
        "VALID",
        dimension_numbers=("NCDHW", "OIDHW", "NCDHW"),
        preferred_element_type=jnp.float32,
    )[0]


def kernel_grad(padded, errors):
    result = lax.conv_general_dilated(
        padded[:, None],
        errors[:, None],
        (1, 1, 1),
        "VALID",
        dimension_numbers=("NCDHW", "OIDHW", "NCDHW"),
        preferred_element_type=jnp.float32,
    )
    return result.transpose(1, 0, 2, 3, 4)


def pad_plane(values):
    return jnp.pad(values, ((0, 0), (0, 0), (1, 1), (1, 1)))


def leaky_rectify(values):
    return jnp.where(values > 0, values, 0.3 * values)


def rectify_slope(values):
    return jnp.where(values > 0, 1.0, 0.3)


def mean_pool(values):
    extent = values.shape
    blocks = values.reshape(extent[0], extent[1] // 2, 2, extent[2] // 2, 2, extent[3] // 2, 2)
    return jnp.sum(blocks, axis=(2, 4, 6)) * 0.125


def spread_up(values):
    extent = values.shape
    grown = jnp.broadcast_to(
        values[:, :, None, :, None, :, None], (extent[0], extent[1], 2, extent[2], 2, extent[3], 2)
    )
    return grown.reshape(extent[0], 2 * extent[1], 2 * extent[2], 2 * extent[3])


def shards(volume, first_filters, first_biases, second_filters, second_biases, cotangent):
    sample = volume[0]
    target = cotangent[0]
    planes = sample.shape[1]
    rim_depth = 1
    haloed = with_halo(sample, (("space", 1),), 1)
    first_in = pad_plane(haloed)
    linear_one = convolve(first_in, first_filters) + first_biases[:, None, None, None]
    pooled = mean_pool(leaky_rectify(linear_one)).astype(jnp.bfloat16)
    pooled_ext = with_halo(pooled, (("space", 1),), rim_depth)
    second_in = pad_plane(pooled_ext)
    linear_wide = convolve(second_in, second_filters) + second_biases[:, None, None, None]
    delta_two = (target.astype(jnp.float32) * rectify_slope(linear_wide)).astype(jnp.bfloat16)
    delta_ext = with_halo(delta_two, (("space", 1),), 1)
    activations = leaky_rectify(linear_wide).astype(jnp.bfloat16)
    second_terms = (
        kernel_grad(second_in, delta_two),
        jnp.sum(delta_two.astype(jnp.float32), axis=(1, 2, 3)),
    )
    second_terms = lax.psum((second_terms[0], second_terms[1]), ("dp", "space"))
    flipped = jnp.flip(second_filters, (2, 3, 4)).transpose(1, 0, 2, 3, 4)
    pooled_grad = convolve(pad_plane(delta_ext), flipped).astype(jnp.bfloat16)
    stored_grad = lax.optimization_barrier(pooled_grad)
    delta_one = (
        spread_up(stored_grad.astype(jnp.float32)) * 0.125 * rectify_slope(linear_one)
    ).astype(jnp.bfloat16)
    first_terms = (
        kernel_grad(first_in, delta_one),
        jnp.sum(delta_one.astype(jnp.float32), axis=(1, 2, 3)),
    )
    first_terms = lax.psum((first_terms[0], first_terms[1]), ("dp", "space"))
    totals = (first_terms[0], first_terms[1], second_terms[0], second_terms[1])
    count_one = (
        lax.axis_size("dp") * lax.axis_size("space") * planes * sample.shape[2] * sample.shape[3]
    )
    scale_one = 1.0 / math.sqrt(count_one)
    scale_two = 1.0 / math.sqrt(count_one / 8)
    return (
        activations[None],
        pooled_grad[None],
        totals[0] * scale_one,
        totals[1] * scale_one,
        totals[2] * scale_two,
        totals[3] * scale_two,
    )


def solution(mesh):
    placed = (
        P("dp", None, "space", None, None),
        P(),
        P(),
        P(),
        P(),
        P("dp", None, "space", None, None),
    )
    return jax.shard_map(
        shards,
        mesh=mesh,
        in_specs=placed,
        out_specs=(
            P("dp", None, "space", None, None),
            P("dp", None, "space", None, None),
            P(),
            P(),
            P(),
            P(),
        ),
        check_vma=False,
    )
```

profile of v0, /device:TPU:1, one launch (start us, length us, event | category | flops | bytes accessed | tf_op | source)
XLA Modules:
  0.0 488.8 jit_solution(2869849680273263854)
XLA Ops:
  0.6 0.8 fusion.76
  1.4 4.0 collective-permute-start
  5.4 1.3 collective-permute-start.1
  6.7 1.3 copy.164
  8.1 1.8 collective-permute-done.1
  9.9 1.3 fusion.79
  11.3 0.8 reshape.137
  12.1 4.3 copy.155
  16.5 1.1 slice.34
  17.6 25.4 %fusion = (f32[8,8,8,33,16]{4,2,3,1,0:T(8,128)}, f32[8,8,8,33,16]{4,2,3,1,0:T(8,128)}) fusion(f32[16]{0:T(128)S(1)} %copy-done.12, bf16[16,4,3,3,3]{0,1,4,3,2:T(4,128)(2,1)S(1)} %copy-done.16, bf16[4,10,10,1,7,2]{4,0,5,2,1,3:T(4,128)(2,1)S(1)} %slice.34, bf16[4,10,10,1,8,33]{4,0,5,2,1,3:T(4,128)(2,1)} %copy.155, pred[8,33]{0,1:T(8,128)(4,1)S(1)} %copy-done.17), kind=kOutput, calls=%fused_computation.2 | convolution fusion | flops 60145920 | bytes 2388872 | tf_op jit(solution)/shard_map/conv_general_dilated | solution.py:23
  43.0 8.5 %copy.156 = f32[8,8,8,33,16]{3,2,4,1,0:T(8,128)} copy(f32[8,8,8,33,16]{4,2,3,1,0:T(8,128)} %get-tuple-element.65) | data formatting | bytes 2162688 | tf_op jit(solution)/shard_map/conv_general_dilated | solution.py:23
  51.5 3.5 reshape.99
  55.1 4.8 copy.157
  60.0 12.8 %fusion.2 = f32[16,4,4,128]{0,3,2,1:T(8,128)S(1)} fusion(f32[16,4,2,4,2,128,2]{0,6,5,4,3,2,1:T(2,128)} %bitcast.110, f32[16]{0:T(128)S(1)} %copy-done.12), kind=kLoop, calls=%fused_computation.6 | loop fusion | flops 1277952 | bytes 1179712 | tf_op jit(solution)/shard_map/reduce_sum | solution.py:60
  73.6 3.9 collective-permute-start.2
  77.5 1.3 collective-permute-start.3
  78.8 1.2 fusion.80
  80.1 9.0 %copy.178 = f32[8,8,8,33,16]{3,2,4,1,0:T(8,128)} copy(f32[8,8,8,33,16]{4,2,3,1,0:T(8,128)} %get-tuple-element.64) | data formatting | bytes 2162688 | tf_op jit(solution)/shard_map/jit(_where)/select_n | solution.py:54
  89.2 3.5 reshape.117
  92.8 4.6 copy.190
  97.3 29.6 %copy.176 = bf16[4,1,10,10,258]{0,1,4,3,2:T(2,128)(2,1)} copy(bf16[4,1,10,10,258]{4,3,2,0,1:T(8,128)(2,1)S(1)} %copy-done.6) | data formatting | bytes 412800 | tf_op jit(solution)/shard_map/broadcast_in_dim | solution.py:35
  127.0 1.0 copy.158
  128.2 0.9 fusion.78
  129.1 0.8 reshape.102
  129.9 2.0 copy.162
  132.1 2.8 fusion.36
  135.2 1.2 fusion.40
  136.4 1.1 convert_reduce_fusion.1
  137.5 2.5 copy.180
  140.2 4.0 collective-permute-start.4
  144.2 1.5 collective-permute-start.5
  145.7 1.3 copy.163
  146.9 16.5 %fusion.44 = f32[32,16,3,3,3]{0,1,4,3,2:T(8,128)} fusion(bf16[16,1,6,6,130]{0,1,4,3,2:T(2,128)(2,1)S(1)} %copy.180, bf16[32,1,4,4,128]{0,3,4,2,1:T(4,128)(2,1)} %fusion.40), kind=kOutput, calls=%fused_computation.64 | convolution fusion | flops 56623104 | bytes 336128 | tf_op jit(solution)/shard_map/transpose | solution.py:42
  163.9 0.9 copy.182
  165.4 1.7 reshape.111
  167.2 3.0 copy.170
  170.1 1.0 slice.43
  171.1 3.2 fusion.18
  174.4 0.9 copy.171
  175.4 0.9 copy.186
  176.5 1.0 slice_bitcast_fusion.2
  177.7 7.4 %broadcast_in_dim.50 = f32[16,4,2,4,2,128,2]{0,6,5,4,3,2,1:T(2,128)} broadcast(f32[16,4,4,128]{0,3,2,1:T(8,128)S(1)} %convert_multiply_fusion), dimensions={0,1,3,5} | broadcast | bytes 1179648 | tf_op jit(solution)/shard_map/broadcast_in_dim | solution.py:65
  185.1 5.2 %copy.175 = f32[16,1,8,8,256]{4,0,3,2,1:T(8,128)S(1)} copy(f32[16,1,8,8,256]{0,4,3,2,1:T(8,128)} %bitcast.108) | data formatting | bytes 2097152 | tf_op jit(solution)/shard_map/mul | solution.py:95
  190.6 14.3 %copy.177 = bf16[16,1,8,8,256]{0,1,4,3,2:T(2,128)(2,1)} copy(bf16[16,1,8,8,256]{4,0,3,2,1:T(8,128)(2,1)S(1)} %multiply_convert_fusion) | data formatting | bytes 1048576 | tf_op jit(solution)/shard_map/convert_element_type | solution.py:96
  204.9 8.6 %convert_reduce_fusion = f32[16]{0:T(128)} fusion(f32[1,16,8,8,256]{1,4,3,2,0:T(8,128)} %bitcast.109, f32[8,8,1,256,16]{4,3,1,0,2:T(8,128)} %copy.190), kind=kLoop, calls=%fused_computation.5 | loop fusion | flops 1048560 | bytes 2097216 | tf_op jit(solution)/shard_map/reduce_sum | solution.py:99
  213.6 183.3 %fusion.81 = f32[16,4,3,3,3]{0,1,4,3,2:T(4,128)S(1)} fusion(bf16[4,1,10,10,258]{0,1,4,3,2:T(2,128)(2,1)} %copy.176, bf16[16,1,8,8,256]{0,1,4,3,2:T(2,128)(2,1)S(1)} %copy-done.4), kind=kOutput, calls=%fused_computation.118 | convolution fusion | flops 56623104 | bytes 737600 | tf_op jit(solution)/shard_map/transpose | solution.py:42
  396.9 88.3 %all-reduce.3 = (f32[16,4,3,3,3]{0,1,4,3,2:T(4,128)S(1)}, f32[16]{0:T(128)S(1)}, f32[32,16,3,3,3]{0,1,4,3,2:T(8,128)S(1)}, f32[32]{0:T(128)S(1)}) all-reduce(f32[16,4,3,3,3]{0,1,4,3,2:T(4,128)S(1)} %fusion.81, f32[16]{0:T(128)S(1)} %copy-done.10, ...), channel_id=1, replica_groups=mesh['dp'=16,'space'=16] {'dp','space'}, use_global_device_ids=true, to_apply=%region_1.2 | all-reduce | flops 15600 | bytes 124800 | tf_op jit(solution)/shard_map/psum | solution.py:101
  487.6 0.9 copy.183
  (69 shorter events, 6.2 us)
Async XLA Ops:
  0.6 131.4 %copy-start = (bf16[32,16,3,3,3]{0,1,4,3,2:T(8,128)(2,1)S(1)}, bf16[32,16,3,3,3]{0,1,4,3,2:T(8,128)(2,1)}, u32[]{:S(2)}) copy-start(bf16[32,16,3,3,3]{0,1,4,3,2:T(8,128)(2,1)} %param.9) | copy-start | bytes 82948
  1.4 6.7 %collective-permute-start = (bf16[4,1,8,256]{3,2,1,0:T(8,128)(2,1)S(1)}, bf16[4,1,8,256]{3,2,1,0:T(8,128)(2,1)S(1)}, u32[]{:S(2)}, u32[]{:S(2)}) collective-permute-start(bf16[4,1,8,256]{3,2,1,0:T(8,128)(2,1)S(1)} %get-tuple-element.60), channel_id=1, source_target_pairs={{0,1},{1,2},{2,3},{3,4},{4,5},{5,6},{6,7},{7,8},{8,9},{9,10},{10,1... | collective-permute-start | bytes 49160 | tf_op jit(solution)/shard_map/ppermute | solution.py:14
  5.4 4.5 collective-permute-start.1
  11.3 6.3 %copy-start.12 = (f32[16]{0:T(128)S(1)}, f32[16]{0:T(128)}, u32[]{:S(2)}) copy-start(f32[16]{0:T(128)} %param.8) | copy-start | bytes 196
  11.3 6.3 %copy-start.16 = (bf16[16,4,3,3,3]{0,1,4,3,2:T(4,128)(2,1)S(1)}, bf16[16,4,3,3,3]{0,1,4,3,2:T(4,128)(2,1)}, u32[]{:S(2)}) copy-start(bf16[16,4,3,3,3]{0,1,4,3,2:T(4,128)(2,1)} %param.7) | copy-start | bytes 10372
  11.3 6.3 %copy-start.17 = (pred[8,33]{0,1:T(8,128)(4,1)S(1)}, pred[8,33]{0,1:T(8,128)(4,1)}, u32[]{:S(2)}) copy-start(pred[8,33]{0,1:T(8,128)(4,1)} %constant.43) | copy-start | bytes 796
  55.0 4.9 %copy-start.2 = (f32[8,8,1,264,16]{3,4,1,0,2:T(8,128)}, f32[8,8,1,264,16]{3,4,1,0,2:T(8,128)S(1)}, u32[]{:S(2)}) copy-start(f32[8,8,1,264,16]{3,4,1,0,2:T(8,128)S(1)} %reshape.99) | copy-start | bytes 3244036
  59.9 18.8 %copy-start.8 = (bf16[1,4,8,8,256]{4,3,2,1,0:T(8,128)(2,1)S(1)}, bf16[1,4,8,8,256]{4,3,2,1,0:T(8,128)(2,1)}, u32[]{:S(2)}) copy-start(bf16[1,4,8,8,256]{4,3,2,1,0:T(8,128)(2,1)} %param.6) | copy-start | bytes 393220
  73.6 53.4 %collective-permute-start.2 = (bf16[16,1,4,128]{0,3,2,1:T(8,128)(2,1)}, bf16[16,1,4,128]{0,3,2,1:T(8,128)(2,1)}, u32[]{:S(2)}, u32[]{:S(2)}) collective-permute-start(bf16[16,1,4,128]{0,3,2,1:T(8,128)(2,1)} %get-tuple-element.58), channel_id=1, source_target_pairs={{0,1},{1,2},{2,3},{3,4},{4,5},{5,6},{6,7},{7,8},{8,9},{9,10},{10,1... | collective-permute-start | bytes 49160 | tf_op jit(solution)/shard_map/ppermute | solution.py:14
  77.5 50.5 %collective-permute-start.3 = (bf16[16,1,4,128]{0,3,2,1:T(8,128)(2,1)}, bf16[16,1,4,128]{0,3,2,1:T(8,128)(2,1)S(1)}, u32[]{:S(2)}, u32[]{:S(2)}) collective-permute-start(bf16[16,1,4,128]{0,3,2,1:T(8,128)(2,1)} %get-tuple-element.59), channel_id=1, source_target_pairs={{1,0},{2,1},{3,2},{4,3},{5,4},{6,5},{7,6},{8,7},{9,8},{10,9},{11,1... | collective-permute-start | bytes 49160 | tf_op jit(solution)/shard_map/ppermute | solution.py:17
  92.7 4.6 copy-start.6
  128.0 4.0 copy-start.11
  128.0 4.0 copy-start.18
  134.9 2.7 copy-start.7
  140.2 24.7 %collective-permute-start.4 = (bf16[32,1,4,128]{0,2,3,1:T(4,128)(2,1)S(1)}, bf16[32,1,4,128]{0,2,3,1:T(4,128)(2,1)S(1)}, u32[]{:S(2)}, u32[]{:S(2)}) collective-permute-start(bf16[32,1,4,128]{0,2,3,1:T(4,128)(2,1)S(1)} %get-tuple-element.56), channel_id=1, source_target_pairs={{0,1},{1,2},{2,3},{3,4},{4,5},{5,6},{6,7},{7,8},{8,9},{9,10},{10,1... | collective-permute-start | bytes 98312 | tf_op jit(solution)/shard_map/ppermute | solution.py:14
  144.2 20.8 %collective-permute-start.5 = (bf16[32,1,4,128]{0,2,3,1:T(4,128)(2,1)S(1)}, bf16[32,1,4,128]{0,2,3,1:T(4,128)(2,1)S(1)}, u32[]{:S(2)}, u32[]{:S(2)}) collective-permute-start(bf16[32,1,4,128]{0,2,3,1:T(4,128)(2,1)S(1)} %get-tuple-element.57), channel_id=1, source_target_pairs={{1,0},{2,1},{3,2},{4,3},{5,4},{6,5},{7,6},{8,7},{9,8},{10,9},{11,1... | collective-permute-start | bytes 98312 | tf_op jit(solution)/shard_map/ppermute | solution.py:17
  171.1 4.1 copy-start.15
  185.1 5.2 %copy-start.3 = (f32[8,8,1,264,16]{3,4,1,0,2:T(8,128)S(1)}, f32[8,8,1,264,16]{3,4,1,0,2:T(8,128)}, u32[]{:S(2)}) copy-start(f32[8,8,1,264,16]{3,4,1,0,2:T(8,128)} %copy-done.2) | copy-start | bytes 3244036
  185.1 5.2 %copy-start.13 = (f32[16]{0:T(128)S(1)}, f32[16]{0:T(128)}, u32[]{:S(2)}) copy-start(f32[16]{0:T(128)} %param.8) | copy-start | bytes 196
  204.9 8.7 %copy-start.4 = (bf16[16,1,8,8,256]{0,1,4,3,2:T(2,128)(2,1)S(1)}, bf16[16,1,8,8,256]{0,1,4,3,2:T(2,128)(2,1)}, u32[]{:S(2)}) copy-start(bf16[16,1,8,8,256]{0,1,4,3,2:T(2,128)(2,1)} %copy.177) | copy-start | bytes 1572868
  213.5 183.4 %copy-start.9 = (f32[32,16,3,3,3]{0,1,4,3,2:T(8,128)S(1)}, f32[32,16,3,3,3]{0,1,4,3,2:T(8,128)}, u32[]{:S(2)}) copy-start(f32[32,16,3,3,3]{0,1,4,3,2:T(8,128)} %fusion.44) | copy-start | bytes 165892
  213.5 183.4 %copy-start.10 = (f32[16]{0:T(128)S(1)}, f32[16]{0:T(128)}, u32[]{:S(2)}) copy-start(f32[16]{0:T(128)} %convert_reduce_fusion) | copy-start | bytes 196
  213.5 183.4 %copy-start.14 = (f32[32]{0:T(128)S(1)}, f32[32]{0:T(128)}, u32[]{:S(2)}) copy-start(f32[32]{0:T(128)} %get-tuple-element.52) | copy-start | bytes 388
  213.5 274.0 %copy-start.5 = (bf16[1,16,4,4,128]{1,4,3,2,0:T(8,128)(2,1)S(1)}, bf16[1,16,4,4,128]{1,4,3,2,0:T(8,128)(2,1)}, u32[]{:S(2)}) copy-start(bf16[1,16,4,4,128]{1,4,3,2,0:T(8,128)(2,1)} %get-tuple-element.55) | copy-start | bytes 196612
  213.5 274.9 %copy-start.1 = (bf16[32,16,3,3,3]{0,1,4,3,2:T(8,128)(2,1)S(1)}, bf16[32,16,3,3,3]{0,1,4,3,2:T(8,128)(2,1)}, u32[]{:S(2)}) copy-start(bf16[32,16,3,3,3]{0,1,4,3,2:T(8,128)(2,1)} %param.9) | copy-start | bytes 82948
where the time goes:
time: 497 us; the launch traced here: 489 us
  matrix products  231 us (46%)
  local copies, waits for them, and re-layouts  120 us (24%)
  blocking collectives  88.3 us (18%)
  other arithmetic  30.4 us (6%)
  starting transfers between devices  15.9 us (3%)
    transpose x2, matrix products, kernel_grad(): return result.transpose(1, 0, 2, 3, 4)  200 us
    psum x1, blocking collectives, shards(): first_terms = lax.psum((first_terms[0], first_terms[1]), ('dp', 'space'))  88.3 us
    conv_general_dilated x15, local copies, waits for them, and re-layouts, convolve(): lax.conv_general_dilated(padded[None], kernel, (1, 1, 1), 'VALID', dimens...  32.9 us
    broadcast_in_dim x2, local copies, waits for them, and re-layouts, kernel_grad(): padded[:, None]  32.2 us
    conv_general_dilated x3, matrix products, convolve(): lax.conv_general_dilated(padded[None], kernel, (1, 1, 1), 'VALID', dimens...  31.4 us
    convert_element_type x1, local copies, waits for them, and re-layouts, shards(): delta_one = (spread_up(stored_grad.astype(jnp.float32)) * 0.125 * rectify...  14.3 us
    reduce_sum x1, other arithmetic, mean_pool(): return jnp.sum(blocks, axis=(2, 4, 6)) * 0.125  12.8 us
    select_n x3, local copies, waits for them, and re-layouts, rectify_slope(): return jnp.where(values > 0, 1.0, 0.3)  12.6 us
  transfers between devices with their start and end apart: 6, of which 1 were waited for; matrix products, arithmetic and copies ran while one was open for 14% of the time, Pallas kernels for 0%

commit v1 on v0

v1 whole, which is shorter than its diff:
```python
import math

import jax
import jax.numpy as jnp
from jax import lax
from jax.experimental import pallas as pl
from jax.experimental.pallas import tpu as pltpu
from jax.sharding import PartitionSpec as P

F32 = jnp.float32
BF16 = jnp.bfloat16
HALO = 5
PLANES = 8
LEAK = 0.3


def lanes_dot(left, right):
    return lax.dot_general(left, right, (((1,), (1,)), ((), ())), preferred_element_type=F32)


def plain_dot(left, right):
    return jnp.dot(left, right, preferred_element_type=F32)


def both_shifts(values):
    lane = lax.broadcasted_iota(jnp.int32, values.shape, 1)
    before = jnp.where(lane == 0, 0.0, pltpu.roll(values, 1, 1))
    after = jnp.where(lane == 127, 0.0, pltpu.roll(values, 127, 1))
    return before.astype(BF16), values.astype(BF16), after.astype(BF16)


def layers(
    flags, vol, vol_lo, vol_hi, cot, cot_lo, cot_hi, w1, b1, w2, b2, w3,
    act, pooled_grad, grads,
    split, x1, x2, x3, slope, delta_one, cot_all, cot_below, cot_above, act_all, grad_all, band, thin,
):
    row = lax.broadcasted_iota(jnp.int32, (256, 512), 0)
    col = lax.broadcasted_iota(jnp.int32, (256, 512), 1)
    kind = col // 128
    offset = jnp.where(kind == 0, 0, jnp.where(kind == 1, 1, jnp.where(kind == 2, -1, 2)))
    pick = (row == 2 * (col % 128) + offset).astype(F32).astype(BF16)
    for ci in range(4):
        planes = jnp.concatenate(
            [
                vol_lo[ci].astype(F32),
                vol[ci].astype(F32),
                vol_hi[ci].astype(F32),
                jnp.zeros((2, 8, 256), F32),
            ],
            axis=0,
        )
        parts = plain_dot(planes.reshape(160, 256).astype(BF16), pick)
        for group in range(5):
            for kind_n in range(4):
                split[kind_n, (group * 4 + ci) * 32 : (group * 4 + ci + 1) * 32, :] = parts[
                    group * 32 : group * 32 + 32, kind_n * 128 : kind_n * 128 + 128
                ]
    homes = {0: ((0, 1), (1, 0)), 1: ((0, 2), (1, 1)), 2: ((0, 0),), 3: ((1, 2),)}
    for group in range(5):
        base = group * 144
        x1[base : base + 48, 0:256] = jnp.zeros((48, 256), BF16)
        x1[base + 96 : base + 144, 1792:2048] = jnp.zeros((48, 256), BF16)
    for height in range(8):
        for kind_n in range(4):
            tile = split[kind_n, pl.ds(height, 80, stride=8), :].astype(BF16)
            for kh in range(3):
                out_h = height - kh + 1
                if not 0 <= out_h < 8:
                    continue
                for parity, kw in homes[kind_n]:
                    lane0 = out_h * 256 + parity * 128
                    for group in range(5):
                        row0 = group * 144 + (kh * 3 + kw) * 16
                        x1[row0 : row0 + 16, lane0 : lane0 + 128] = tile[
                            group * 16 : group * 16 + 16
                        ]
    for plane in range(8):
        base = plane * 144
        x2[base : base + 48, 0:128] = jnp.zeros((48, 128), BF16)
        x2[base + 96 : base + 144, 384:512] = jnp.zeros((48, 128), BF16)
    weights_one = w1[...]
    bias_one = b1[...]
    for group in range(4):
        for high in range(4):
            linear = plain_dot(
                weights_one, x1[group * 144 : group * 144 + 288, high * 512 : high * 512 + 512]
            )
            linear = linear + bias_one
            positive = linear > 0
            if group in (1, 2):
                slope[(group - 1) * 64 : group * 64, high * 512 : high * 512 + 512] = jnp.where(
                    positive, 0.125, 0.125 * LEAK
                )
            leaky = jnp.where(positive, linear, LEAK * linear)
            for pair in range(2):
                both = leaky[pair * 32 : pair * 32 + 16] + leaky[pair * 32 + 16 : pair * 32 + 32]
                mean = (
                    (both[:, 0:128] + both[:, 128:256]) + (both[:, 256:384] + both[:, 384:512])
                ) * 0.125
                plane = group * 2 + pair
                if plane < 2:
                    mean = mean * flags[0]
                if plane >= 6:
                    mean = mean * flags[1]
                for kw, moved in enumerate(both_shifts(mean)):
                    for kh in range(3):
                        out_h = high - kh + 1
                        if 0 <= out_h < 4:
                            row0 = plane * 144 + (kh * 3 + kw) * 16
                            x2[row0 : row0 + 16, out_h * 128 : out_h * 128 + 128] = moved
    cot_all[0:512, :] = cot[...].astype(F32)
    cot_below[0:128, :] = cot_lo[...].astype(F32)
    cot_above[0:128, :] = cot_hi[...].astype(F32)
    for plane in range(6):
        base = plane * 288
        x3[base : base + 96, 0:128] = jnp.zeros((96, 128), BF16)
        x3[base + 192 : base + 288, 384:512] = jnp.zeros((96, 128), BF16)
    weights_two = w2[...]
    bias_two = b2[...]
    for plane in range(6):
        linear = plain_dot(weights_two, x2[plane * 144 : plane * 144 + 432, :]) + bias_two
        positive = linear > 0
        factor = jnp.where(positive, 1.0, LEAK)
        leaky = jnp.where(positive, linear, LEAK * linear)
        for high in range(4):
            lanes = slice(high * 128, high * 128 + 128)
            if plane == 0:
                target = cot_below[pl.ds(high, 32, stride=4), :]
            elif plane == 5:
                target = cot_above[pl.ds(high, 32, stride=4), :]
            else:
                at = (plane - 1) * 4 + high
                target = cot_all[pl.ds(at, 32, stride=16), :]
                act_all[pl.ds(at, 32, stride=16), :] = leaky[:, lanes]
            delta = target * factor[:, lanes]
            for kw, moved in enumerate(both_shifts(delta)):
                for kh in range(3):
                    out_h = high - kh + 1
                    if 0 <= out_h < 4:
                        row0 = plane * 288 + (kh * 3 + kw) * 32
                        x3[row0 : row0 + 32, out_h * 128 : out_h * 128 + 128] = moved
    act[...] = act_all[0:512, :].astype(BF16)
    weights_three = w3[...]
    for plane in range(4):
        total = plain_dot(weights_three, x3[plane * 288 : plane * 288 + 864, :])
        for high in range(4):
            tile = total[:, high * 128 : high * 128 + 128].astype(BF16).astype(F32)
            grad_all[pl.ds(plane * 4 + high, 16, stride=16), :] = tile
            for row0 in (plane * 32, plane * 32 + 16):
                for part in range(4):
                    lane0 = high * 512 + part * 128
                    delta_one[row0 : row0 + 16, lane0 : lane0 + 128] = (
                        tile * slope[row0 : row0 + 16, lane0 : lane0 + 128]
                    ).astype(BF16)
    pooled_grad[...] = grad_all[0:256, :].astype(BF16)
    second = jnp.zeros((432, 128), F32)
    shift_two = jnp.zeros((16, 128), F32)
    for plane in range(4):
        delta = jnp.concatenate(
            [x3[(plane + 1) * 288 + 128 : (plane + 1) * 288 + 160, :], jnp.zeros((96, 512), BF16)],
            axis=0,
        )
        second = second + lanes_dot(x2[(plane + 1) * 144 : (plane + 1) * 144 + 432, :], delta)
        shift_two = shift_two + lanes_dot(jnp.ones((16, 512), BF16), delta)
    three = (
        second[0:112] + pltpu.roll(second[112:224], 32, 1) + pltpu.roll(second[224:336], 64, 1)
    )
    grads[0:96, :] = three[0:96] + pltpu.roll(second[336:432], 96, 1)
    grads[96:112, :] = three[96:112]
    first = jnp.zeros((288, 128), F32)
    shift_one = jnp.zeros((16, 128), F32)
    for group in (1, 2):
        delta = jnp.concatenate(
            [delta_one[(group - 1) * 64 : group * 64, :], jnp.zeros((64, 2048), BF16)], axis=0
        )
        first = first + lanes_dot(x1[group * 144 : group * 144 + 288, :], delta)
        shift_one = shift_one + lanes_dot(jnp.ones((16, 2048), BF16), delta)
    band[0:288, :] = first
    lane36 = lax.broadcasted_iota(jnp.int32, (36, 128), 1)
    packed = jnp.zeros((36, 128), F32)
    for kd in range(3):
        total = jnp.zeros((36, 128), F32)
        for plane in range(4):
            at = (plane + kd) // 4 * 144 + (plane + kd) % 4
            piece = band[pl.ds(at, 36, stride=4), :]
            lane0 = (128 + 16 * (kd - plane)) % 128
            total = total + (pltpu.roll(piece, lane0, 1) if lane0 else piece)
        packed = packed + jnp.where((lane36 >= 16 * kd) & (lane36 < 16 * kd + 16), total, 0.0)
    thin[...] = jnp.zeros((48, 128), F32)
    thin[0:36, :] = packed
    grads[112:136, :] = thin[0:24, :] + pltpu.roll(thin[24:48, :], 48, 1)
    lane = lax.broadcasted_iota(jnp.int32, (8, 128), 1)
    ones = shift_one[0:8]
    ones = (
        ones + pltpu.roll(ones, 112, 1) + pltpu.roll(ones, 96, 1) + pltpu.roll(ones, 80, 1)
    )
    ones = jnp.where((lane >= 32) & (lane < 48), pltpu.roll(ones, 32, 1), 0.0)
    grads[136:144, :] = jnp.where(lane < 32, shift_two[0:8], ones)


def unpack(scales, mine, other, grad_one, shift_one, grad_two, shift_two, whole):
    scale_one, scale_two = scales[1], scales[2]
    low = scales[0] > 0
    whole[0:72, :] = jnp.where(low, mine[...], other[...])
    whole[72:144, :] = jnp.where(low, other[...], mine[...])
    for group in range(4):
        rows = whole[0:112, :] * scale_two
        if group:
            rows = pltpu.roll(rows, 128 - 32 * group, 1)
        count = 7 if group < 3 else 6
        for tap in range(count):
            grad_two[group * 7 + tap] = rows[tap * 16 : tap * 16 + 16, 0:32]
    for kd in range(3):
        for tap in range(9):
            at, lane0 = (tap, 0) if tap < 6 else (tap - 6, 48)
            piece = whole[112 + at * 4 : 116 + at * 4, :] * scale_one
            lane0 += 16 * kd
            if lane0:
                piece = pltpu.roll(piece, 128 - lane0, 1)
            grad_one[kd * 9 + tap] = piece[:, 0:16]
    row = whole[136:144, :]
    shift_two[...] = row[0:1, 0:32] * scale_two
    shift_one[...] = pltpu.roll(row, 96, 1)[0:1, 0:16] * scale_one


def in_vmem(count):
    return [pl.BlockSpec(memory_space=pltpu.VMEM)] * count


def run_layers(flags, *arrays):
    return pl.pallas_call(
        layers,
        out_shape=(
            jax.ShapeDtypeStruct((512, 128), BF16),
            jax.ShapeDtypeStruct((256, 128), BF16),
            jax.ShapeDtypeStruct((144, 128), F32),
        ),
        in_specs=[pl.BlockSpec(memory_space=pltpu.SMEM)] + in_vmem(len(arrays)),
        out_specs=tuple(in_vmem(3)),
        scratch_shapes=[
            pltpu.VMEM((4, 648, 128), F32),
            pltpu.VMEM((720, 2048), BF16),
            pltpu.VMEM((1152, 512), BF16),
            pltpu.VMEM((1728, 512), BF16),
            pltpu.VMEM((128, 2048), F32),
            pltpu.VMEM((128, 2048), BF16),
            pltpu.VMEM((528, 128), F32),
            pltpu.VMEM((136, 128), F32),
            pltpu.VMEM((136, 128), F32),
            pltpu.VMEM((528, 128), F32),
            pltpu.VMEM((272, 128), F32),
            pltpu.VMEM((304, 128), F32),
            pltpu.VMEM((48, 128), F32),
        ],
        compiler_params=pltpu.CompilerParams(vmem_limit_bytes=40 << 20),
        name="layers",
    )(flags, *arrays)


def run_unpack(scales, mine, other):
    return pl.pallas_call(
        unpack,
        out_shape=(
            jax.ShapeDtypeStruct((27, 4, 16), F32),
            jax.ShapeDtypeStruct((1, 16), F32),
            jax.ShapeDtypeStruct((27, 16, 32), F32),
            jax.ShapeDtypeStruct((1, 32), F32),
        ),
        in_specs=[pl.BlockSpec(memory_space=pltpu.SMEM)] + in_vmem(2),
        out_specs=tuple(in_vmem(4)),
        scratch_shapes=[pltpu.VMEM((144, 128), F32)],
        name="unpack",
    )(scales, mine, other)


def banded(first_filters):
    taps = first_filters.transpose(2, 3, 4, 1, 0).reshape(3, 9, 4, 16)
    shifted = [jnp.pad(taps, ((j, 5 - j), (0, 0), (0, 0), (0, 0))) for j in range(4)]
    wide = jnp.stack(shifted, 0).reshape(4, 2, 4, 9, 4, 16)
    return wide.transpose(0, 5, 1, 3, 4, 2).reshape(64, 288)


def device_exchanges():
    def place(index):
        dp, space = divmod(index, 16)
        return [dp & 1, (dp >> 1) & 3, space & 3, (dp >> 3) * 4 + (space >> 2)]

    def index_of(core, x, y, z):
        return ((z >> 2) * 8 + x * 2 + core) * 16 + (z & 3) * 4 + y

    def pairing(which, mask):
        pairs = []
        for index in range(256):
            spot = place(index)
            spot[which] ^= mask
            pairs.append((index, index_of(*spot)))
        return pairs

    core = pairing(0, 1)
    others = [pairing(*step) for step in ((2, 1), (2, 3), (1, 1), (1, 3), (3, 1), (3, 2), (3, 7))]
    return core, others


def add_up(grads, core_index):
    axes = ("dp", "space")
    core, others = device_exchanges()
    low = core_index == 0
    top, bottom = grads[:72], grads[72:]
    mine = jnp.where(low, top, bottom) + lax.ppermute(jnp.where(low, bottom, top), axes, core)
    for pairs in others:
        mine = mine + lax.ppermute(mine, axes, pairs)
    return mine, lax.ppermute(mine, axes, core)


def shards(volume, first_filters, first_biases, second_filters, second_biases, cotangent):
    sample, target = volume[0], cotangent[0]
    slabs = lax.axis_size("space")
    here = lax.axis_index("space")
    forward = [(i, i + 1) for i in range(slabs - 1)]
    backward = [(i + 1, i) for i in range(slabs - 1)]
    vol_lo = lax.ppermute(sample[:, PLANES - HALO :], "space", forward)
    vol_hi = lax.ppermute(sample[:, :HALO], "space", backward)
    cot_lo = lax.ppermute(target[:, 3].reshape(128, 128), "space", forward)
    cot_hi = lax.ppermute(target[:, 0].reshape(128, 128), "space", backward)
    w1 = banded(first_filters)
    b1 = jnp.tile(first_biases, 4)[:, None]
    w2 = second_filters.transpose(0, 2, 3, 4, 1).reshape(32, 432)
    w3 = jnp.flip(second_filters, (2, 3, 4)).transpose(1, 2, 3, 4, 0).reshape(16, 864)
    flags = jnp.stack([here > 0, here < slabs - 1]).astype(F32)
    act, pooled_grad, grads = run_layers(
        flags, sample, vol_lo, vol_hi, target.reshape(512, 128), cot_lo, cot_hi,
        w1, b1, w2, second_biases[:, None], w3,
    )
    core_index = lax.axis_index("dp") % 2
    mine, other = add_up(grads, core_index)
    count_one = (
        lax.axis_size("dp") * slabs * PLANES * sample.shape[2] * sample.shape[3]
    )
    scales = jnp.stack(
        [
            (core_index == 0).astype(F32),
            jnp.float32(1.0 / math.sqrt(count_one)),
            jnp.float32(1.0 / math.sqrt(count_one / 8)),
        ]
    )
    grad_one, shift_one, grad_two, shift_two = run_unpack(scales, mine, other)
    return (
        act.reshape(1, 32, 4, 4, 128),
        pooled_grad.reshape(1, 16, 4, 4, 128),
        grad_one.reshape(3, 3, 3, 4, 16).transpose(4, 3, 0, 1, 2),
        shift_one[0],
        grad_two.reshape(3, 3, 3, 16, 32).transpose(4, 3, 0, 1, 2),
        shift_two[0],
    )


def solution(mesh):
    slab = P("dp", None, "space", None, None)
    return jax.shard_map(
        shards,
        mesh=mesh,
        in_specs=(slab, P(), P(), P(), P(), slab),
        out_specs=(slab, slab, P(), P(), P(), P()),
        check_vma=False,
    )
```

time: 497 us -> 67.5 us (0.14); the launches traced: 489 us -> 67.1 us
  matrix products: 231 us -> 0 us
  local copies, waits for them, and re-layouts: 120 us -> 4.58 us
  blocking collectives: 88.3 us -> 0 us
  other arithmetic: 30.4 us -> 1.11 us
  starting transfers between devices: 15.9 us -> 42.8 us
  waiting for transfers between devices: 1.83 us -> 11.2 us
  Pallas kernels: 0 us -> 6.57 us
    transpose x2 -> x0, matrix products: 200 us -> none  [kernel_grad(): return result.transpose(1, 0, 2, 3, 4)]
    psum x1 -> x0, blocking collectives: 88.3 us -> none  [shards(): first_terms = lax.psum((first_terms[0], first_terms[1]), ('dp', 'space'))]
    broadcast_in_dim x6 -> x1, local copies, waits for them, and re-layouts: 39.8 us -> 0.09 us  [shards(): second_biases[:, None]]
    conv_general_dilated x15 -> x0, local copies, waits for them, and re-layouts: 32.9 us -> none  [convolve(): lax.conv_general_dilated(padded[None], kernel, (1, 1, 1), 'VALID', dimens...]
    conv_general_dilated x3 -> x0, matrix products: 31.4 us -> none  [convolve(): lax.conv_general_dilated(padded[None], kernel, (1, 1, 1), 'VALID', dimens...]
    ppermute x6 -> x13, starting transfers between devices: 15.9 us -> 42.8 us  [the longest x7 21.4 us: add_up(): mine = mine + lax.ppermute(mine, axes, pairs)]
    reduce_sum x3 -> x0, other arithmetic: 22.6 us -> none  [the longest x1 12.8 us: mean_pool(): return jnp.sum(blocks, axis=(2, 4, 6)) * 0.125]
    convert_element_type x8 -> x0, local copies, waits for them, and re-layouts: 18.4 us -> none  [the longest x1 14.3 us: shards(): delta_one = (spread_up(stored_grad.astype(jnp.float32)) * 0.125 * rectify...]
  transfers between devices with their start and end apart: 6 -> 13, of which waited for: 1 -> 9; matrix products, arithmetic and copies ran while one was open for 14% -> 3% of each run, Pallas kernels for 0% -> 0%
where the time goes in v1:
time: 67.5 us; the launch traced here: 67.1 us
  starting transfers between devices  42.8 us (63%)
  waiting for transfers between devices  11.2 us (17%)
  Pallas kernels  6.57 us (10%)
  local copies, waits for them, and re-layouts  4.58 us (7%)
  other arithmetic  1.11 us (2%)
  between operations  0.86 us (1%)
    ppermute x7, starting transfers between devices, add_up(): mine = mine + lax.ppermute(mine, axes, pairs)  21.4 us
    ppermute x7, waiting for transfers between devices, add_up(): mine = mine + lax.ppermute(mine, axes, pairs)  10.1 us
    ppermute x1, starting transfers between devices, add_up(): return (mine, lax.ppermute(mine, axes, core))  8.17 us
    pallas_call x1, Pallas kernels, run_layers(): pl.pallas_call(layers, out_shape=(jax.ShapeDtypeStruct((512, 128), BF16),...  4.96 us
    ppermute x1, starting transfers between devices, shards(): vol_lo = lax.ppermute(sample[:, PLANES - HALO:], 'space', forward)  4.03 us
    ppermute x1, starting transfers between devices, shards(): cot_lo = lax.ppermute(target[:, 3].reshape(128, 128), 'space', forward)  3.99 us
    ppermute x1, starting transfers between devices, add_up(): lax.ppermute(jnp.where(low, bottom, top), axes, core)  2.63 us
    unnamed x16, local copies, waits for them, and re-layouts  2.59 us
  transfers between devices with their start and end apart: 13, of which 9 were waited for; matrix products, arithmetic and copies ran while one was open for 3% of the time, Pallas kernels for 0%

profile of v1, /device:TPU:1, one launch (start us, length us, event | category | flops | bytes accessed | tf_op | source)
XLA Modules:
  0.0 67.1 jit_solution(8270052534501672937)
XLA Ops:
  0.6 1.0 %fusion.1 = (bf16[4,5,8,256]{3,2,1,0:T(8,128)(2,1)S(1)}, bf16[4,5,8,256]{3,2,1,0:T(8,128)(2,1)S(1)}) fusion(bf16[4,8,8,256]{3,2,1,0:T(8,128)(2,1)} %bitcast.34), kind=kLoop, calls=%fused_computation.7 | loop fusion | bytes 327680 | tf_op jit(solution)/shard_map/slice | solution.py:322
  1.6 4.0 %collective-permute-start = (bf16[4,5,8,256]{3,2,1,0:T(8,128)(2,1)S(1)}, bf16[4,5,8,256]{3,2,1,0:T(8,128)(2,1)S(1)}, u32[]{:S(2)}, u32[]{:S(2)}) collective-permute-start(bf16[4,5,8,256]{3,2,1,0:T(8,128)(2,1)S(1)} %get-tuple-element.23), channel_id=1, source_target_pairs={{0,1},{1,2},{2,3},{3,4},{4,5},{5,6},{6,7},{7,8},{8,9},{9,10},{10,1... | collective-permute-start | bytes 245768 | tf_op jit(solution)/shard_map/ppermute | solution.py:321
  5.7 1.3 %collective-permute-start.1 = (bf16[4,5,8,256]{3,2,1,0:T(8,128)(2,1)S(1)}, bf16[4,5,8,256]{3,2,1,0:T(8,128)(2,1)S(1)}, u32[]{:S(2)}, u32[]{:S(2)}) collective-permute-start(bf16[4,5,8,256]{3,2,1,0:T(8,128)(2,1)S(1)} %get-tuple-element.22), channel_id=1, source_target_pairs={{1,0},{2,1},{3,2},{4,3},{5,4},{6,5},{7,6},{8,7},{9,8},{10,9},{11,1... | collective-permute-start | bytes 245768 | tf_op jit(solution)/shard_map/ppermute | solution.py:322
  7.0 0.0 copy-start.5
  7.0 4.0 %collective-permute-start.2 = (bf16[128,128]{1,0:T(8,128)(2,1)S(1)}, bf16[128,128]{1,0:T(8,128)(2,1)S(1)}, u32[]{:S(2)}, u32[]{:S(2)}) collective-permute-start(bf16[128,128]{1,0:T(8,128)(2,1)S(1)} %bitcast.45), channel_id=1, source_target_pairs={{0,1},{1,2},{2,3},{3,4},{4,5},{5,6},{6,7},{7,8},{8,9},{9,10},{10,1... | collective-permute-start | bytes 98312 | tf_op jit(solution)/shard_map/ppermute | solution.py:323
  11.0 1.3 %collective-permute-start.3 = (bf16[128,128]{1,0:T(8,128)(2,1)S(1)}, bf16[128,128]{1,0:T(8,128)(2,1)S(1)}, u32[]{:S(2)}, u32[]{:S(2)}) collective-permute-start(bf16[128,128]{1,0:T(8,128)(2,1)S(1)} %bitcast.44), channel_id=1, source_target_pairs={{1,0},{2,1},{3,2},{4,3},{5,4},{6,5},{7,6},{8,7},{9,8},{10,9},{11,1... | collective-permute-start | bytes 98312 | tf_op jit(solution)/shard_map/ppermute | solution.py:324
  12.4 0.0 copy-start.2
  12.4 0.1 fusion.2
  12.5 0.8 %copy-done.2 = bf16[32,16,3,3,3]{0,1,4,3,2:T(8,128)(2,1)S(1)} copy-done((bf16[32,16,3,3,3]{0,1,4,3,2:T(8,128)(2,1)S(1)}, bf16[32,16,3,3,3]{0,1,4,3,2:T(8,128)(2,1)}, u32[]{:S(2)}) %copy-start.2) | copy-done | bytes 27672
  13.3 0.3 maximum_bitcast_fusion
  13.6 0.1 add_convert_fusion.flags
  13.7 0.2 copy.17
  13.8 0.2 reshape.47
  14.0 0.1 copy.19.w1
  14.1 0.1 copy.18
  14.2 0.0 copy-start.6
  14.2 0.1 reshape.49.w3
  14.3 0.5 copy-done.6
  14.8 0.1 broadcast_in_dim_tile.4.b1
  14.9 0.1 copy.21.w2
  15.0 0.0 copy-start.7
  15.0 0.6 copy-done.7
  15.7 0.1 copy.22.b2
  15.8 0.0 collective-permute-done.2.cot_lo
  15.8 0.0 collective-permute-done.3.cot_hi
  15.8 0.0 collective-permute-done.vol_lo
  15.8 5.0 %layers.1 = (bf16[512,128]{1,0:T(8,128)(2,1)}, bf16[256,128]{1,0:T(8,128)(2,1)}, f32[144,128]{1,0:T(8,128)S(1)}) custom-call(f32[2]{0:T(128)S(1)} %add_convert_fusion.flags, bf16[4,8,8,256]{3,2,1,0:T(8,128)(2,1)S(1)} %bitcast.35, bf16[4,5,8,256]{3,2,1,0:T(8,128)(2,1)S(1)} %collective-permute-done.vol_lo, ...), custom_call_target="tpu_custom_call" | custom-call | tf_op jit(solution)/shard_map/layers/pallas_call | solution.py:231
  20.8 2.6 %collective-permute-start.4 = (f32[72,128]{1,0:T(8,128)S(1)}, f32[72,128]{1,0:T(8,128)S(1)}, u32[]{:S(2)}, u32[]{:S(2)}) collective-permute-start(f32[72,128]{1,0:T(8,128)S(1)} %slice_select_fusion), channel_id=1, source_target_pairs={{0,16},{1,17},{2,18},{3,19},{4,20},{5,21},{6,22},{7,23},{8,24},{9,... | collective-permute-start | bytes 110600 | tf_op jit(solution)/shard_map/ppermute | solution.py:309
  23.4 0.9 %collective-permute-done.4 = f32[72,128]{1,0:T(8,128)S(1)} collective-permute-done((f32[72,128]{1,0:T(8,128)S(1)}, f32[72,128]{1,0:T(8,128)S(1)}, u32[]{:S(2)}, u32[]{:S(2)}) %collective-permute-start.4) | collective-permute-done | bytes 36896 | tf_op jit(solution)/shard_map/ppermute | solution.py:309
  24.3 1.4 %collective-permute-start.5 = (f32[72,128]{1,0:T(8,128)S(1)}, f32[72,128]{1,0:T(8,128)S(1)}, u32[]{:S(2)}, u32[]{:S(2)}) collective-permute-start(f32[72,128]{1,0:T(8,128)S(1)} %select_add_fusion), channel_id=1, source_target_pairs={{0,1},{1,0},{2,3},{3,2},{4,5},{5,4},{6,7},{7,6},{8,9},{9,8},{10,11... | collective-permute-start | bytes 110600 | tf_op jit(solution)/shard_map/ppermute | solution.py:311
  25.7 1.5 %collective-permute-done.5 = f32[72,128]{1,0:T(8,128)S(1)} collective-permute-done((f32[72,128]{1,0:T(8,128)S(1)}, f32[72,128]{1,0:T(8,128)S(1)}, u32[]{:S(2)}, u32[]{:S(2)}) %collective-permute-start.5) | collective-permute-done | bytes 36896 | tf_op jit(solution)/shard_map/ppermute | solution.py:311
  27.1 7.0 %collective-permute-start.6 = (f32[72,128]{1,0:T(8,128)S(1)}, f32[72,128]{1,0:T(8,128)S(1)}, u32[]{:S(2)}, u32[]{:S(2)}) collective-permute-start(f32[72,128]{1,0:T(8,128)S(1)} %add.38), channel_id=1, source_target_pairs={{0,3},{1,2},{2,1},{3,0},{4,7},{5,6},{6,5},{7,4},{8,11},{9,10},{10,... | collective-permute-start | bytes 110600 | tf_op jit(solution)/shard_map/ppermute | solution.py:311
  34.1 1.3 %collective-permute-done.6 = f32[72,128]{1,0:T(8,128)S(1)} collective-permute-done((f32[72,128]{1,0:T(8,128)S(1)}, f32[72,128]{1,0:T(8,128)S(1)}, u32[]{:S(2)}, u32[]{:S(2)}) %collective-permute-start.6) | collective-permute-done | bytes 36896 | tf_op jit(solution)/shard_map/ppermute | solution.py:311
  35.5 1.2 %collective-permute-start.7 = (f32[72,128]{1,0:T(8,128)S(1)}, f32[72,128]{1,0:T(8,128)S(1)}, u32[]{:S(2)}, u32[]{:S(2)}) collective-permute-start(f32[72,128]{1,0:T(8,128)S(1)} %add.39), channel_id=1, source_target_pairs={{0,32},{1,33},{2,34},{3,35},{4,36},{5,37},{6,38},{7,39},{8,40},{9,... | collective-permute-start | bytes 110600 | tf_op jit(solution)/shard_map/ppermute | solution.py:311
  36.7 1.6 %collective-permute-done.7 = f32[72,128]{1,0:T(8,128)S(1)} collective-permute-done((f32[72,128]{1,0:T(8,128)S(1)}, f32[72,128]{1,0:T(8,128)S(1)}, u32[]{:S(2)}, u32[]{:S(2)}) %collective-permute-start.7) | collective-permute-done | bytes 36896 | tf_op jit(solution)/shard_map/ppermute | solution.py:311
  38.3 2.5 %collective-permute-start.8 = (f32[72,128]{1,0:T(8,128)S(1)}, f32[72,128]{1,0:T(8,128)S(1)}, u32[]{:S(2)}, u32[]{:S(2)}) collective-permute-start(f32[72,128]{1,0:T(8,128)S(1)} %add.40), channel_id=1, source_target_pairs={{0,96},{1,97},{2,98},{3,99},{4,100},{5,101},{6,102},{7,103},{8,104... | collective-permute-start | bytes 110600 | tf_op jit(solution)/shard_map/ppermute | solution.py:311
  40.8 1.5 %collective-permute-done.8 = f32[72,128]{1,0:T(8,128)S(1)} collective-permute-done((f32[72,128]{1,0:T(8,128)S(1)}, f32[72,128]{1,0:T(8,128)S(1)}, u32[]{:S(2)}, u32[]{:S(2)}) %collective-permute-start.8) | collective-permute-done | bytes 36896 | tf_op jit(solution)/shard_map/ppermute | solution.py:311
  42.3 1.6 %collective-permute-start.9 = (f32[72,128]{1,0:T(8,128)S(1)}, f32[72,128]{1,0:T(8,128)S(1)}, u32[]{:S(2)}, u32[]{:S(2)}) collective-permute-start(f32[72,128]{1,0:T(8,128)S(1)} %add.41), channel_id=1, source_target_pairs={{0,4},{1,5},{2,6},{3,7},{4,0},{5,1},{6,2},{7,3},{8,12},{9,13},{10,... | collective-permute-start | bytes 110600 | tf_op jit(solution)/shard_map/ppermute | solution.py:311
  43.9 1.3 %collective-permute-done.9 = f32[72,128]{1,0:T(8,128)S(1)} collective-permute-done((f32[72,128]{1,0:T(8,128)S(1)}, f32[72,128]{1,0:T(8,128)S(1)}, u32[]{:S(2)}, u32[]{:S(2)}) %collective-permute-start.9) | collective-permute-done | bytes 36896 | tf_op jit(solution)/shard_map/ppermute | solution.py:311
  45.3 3.0 %collective-permute-start.10 = (f32[72,128]{1,0:T(8,128)S(1)}, f32[72,128]{1,0:T(8,128)S(1)}, u32[]{:S(2)}, u32[]{:S(2)}) collective-permute-start(f32[72,128]{1,0:T(8,128)S(1)} %add.42), channel_id=1, source_target_pairs={{0,8},{1,9},{2,10},{3,11},{4,12},{5,13},{6,14},{7,15},{8,0},{9,1},... | collective-permute-start | bytes 110600 | tf_op jit(solution)/shard_map/ppermute | solution.py:311
  48.3 1.3 %collective-permute-done.10 = f32[72,128]{1,0:T(8,128)S(1)} collective-permute-done((f32[72,128]{1,0:T(8,128)S(1)}, f32[72,128]{1,0:T(8,128)S(1)}, u32[]{:S(2)}, u32[]{:S(2)}) %collective-permute-start.10) | collective-permute-done | bytes 36896 | tf_op jit(solution)/shard_map/ppermute | solution.py:311
  49.6 4.8 %collective-permute-start.11 = (f32[72,128]{1,0:T(8,128)S(1)}, f32[72,128]{1,0:T(8,128)S(1)}, u32[]{:S(2)}, u32[]{:S(2)}) collective-permute-start(f32[72,128]{1,0:T(8,128)S(1)} %add.43), channel_id=1, source_target_pairs={{0,140},{1,141},{2,142},{3,143},{4,136},{5,137},{6,138},{7,139},{8... | collective-permute-start | bytes 110600 | tf_op jit(solution)/shard_map/ppermute | solution.py:311
  54.4 1.5 %collective-permute-done.11 = f32[72,128]{1,0:T(8,128)S(1)} collective-permute-done((f32[72,128]{1,0:T(8,128)S(1)}, f32[72,128]{1,0:T(8,128)S(1)}, u32[]{:S(2)}, u32[]{:S(2)}) %collective-permute-start.11) | collective-permute-done | bytes 36896 | tf_op jit(solution)/shard_map/ppermute | solution.py:311
  55.9 8.2 %collective-permute-start.12 = (f32[72,128]{1,0:T(8,128)S(1)}, f32[72,128]{1,0:T(8,128)S(1)}, u32[]{:S(2)}, u32[]{:S(2)}) collective-permute-start(f32[72,128]{1,0:T(8,128)S(1)} %add.44.mine), channel_id=1, source_target_pairs={{0,16},{1,17},{2,18},{3,19},{4,20},{5,21},{6,22},{7,23},{8,24},{9,... | collective-permute-start | bytes 110600 | tf_op jit(solution)/shard_map/ppermute | solution.py:312
  64.0 0.7 pad_maximum_fusion.scales
  64.7 0.2 collective-permute-done.12.other
  64.9 0.6 copy-done.4
  65.5 1.6 %unpack.1 = (f32[27,4,16]{2,1,0:T(4,128)}, f32[1,16]{1,0:T(1,128)}, f32[27,16,32]{2,1,0:T(8,128)}, f32[1,32]{1,0:T(1,128)}) custom-call(f32[3]{0:T(128)} %pad_maximum_fusion.scales, f32[72,128]{1,0:T(8,128)} %copy-done.3, f32[72,128]{1,0:T(8,128)} %copy-done.4), custom_call_target="tpu_custom_call" | custom-call | tf_op jit(solution)/shard_map/unpack/pallas_call | solution.py:261
  (22 shorter events, 0.1 us)
Async XLA Ops:
  0.6 6.3 %copy-start.1 = (bf16[1,32,4,4,128]{4,3,2,1,0:T(4,128)(2,1)S(1)}, bf16[1,32,4,4,128]{4,3,2,1,0:T(4,128)(2,1)}, u32[]{:S(2)}) copy-start(bf16[1,32,4,4,128]{4,3,2,1,0:T(4,128)(2,1)} %param.11) | copy-start | bytes 393220
  1.6 14.2 %collective-permute-start = (bf16[4,5,8,256]{3,2,1,0:T(8,128)(2,1)S(1)}, bf16[4,5,8,256]{3,2,1,0:T(8,128)(2,1)S(1)}, u32[]{:S(2)}, u32[]{:S(2)}) collective-permute-start(bf16[4,5,8,256]{3,2,1,0:T(8,128)(2,1)S(1)} %get-tuple-element.23), channel_id=1, source_target_pairs={{0,1},{1,2},{2,3},{3,4},{4,5},{5,6},{6,7},{7,8},{8,9},{9,10},{10,1... | collective-permute-start | bytes 245768 | tf_op jit(solution)/shard_map/ppermute | solution.py:321
  5.7 10.1 %collective-permute-start.1 = (bf16[4,5,8,256]{3,2,1,0:T(8,128)(2,1)S(1)}, bf16[4,5,8,256]{3,2,1,0:T(8,128)(2,1)S(1)}, u32[]{:S(2)}, u32[]{:S(2)}) collective-permute-start(bf16[4,5,8,256]{3,2,1,0:T(8,128)(2,1)S(1)} %get-tuple-element.22), channel_id=1, source_target_pairs={{1,0},{2,1},{3,2},{4,3},{5,4},{6,5},{7,6},{8,7},{9,8},{10,9},{11,1... | collective-permute-start | bytes 245768 | tf_op jit(solution)/shard_map/ppermute | solution.py:322
  7.0 5.3 %copy-start.5 = (bf16[16,4,3,3,3]{0,1,4,3,2:T(4,128)(2,1)S(1)}, bf16[16,4,3,3,3]{0,1,4,3,2:T(4,128)(2,1)}, u32[]{:S(2)}) copy-start(bf16[16,4,3,3,3]{0,1,4,3,2:T(4,128)(2,1)} %param.7) | copy-start | bytes 10372
  7.0 8.7 %collective-permute-start.2 = (bf16[128,128]{1,0:T(8,128)(2,1)S(1)}, bf16[128,128]{1,0:T(8,128)(2,1)S(1)}, u32[]{:S(2)}, u32[]{:S(2)}) collective-permute-start(bf16[128,128]{1,0:T(8,128)(2,1)S(1)} %bitcast.45), channel_id=1, source_target_pairs={{0,1},{1,2},{2,3},{3,4},{4,5},{5,6},{6,7},{7,8},{8,9},{9,10},{10,1... | collective-permute-start | bytes 98312 | tf_op jit(solution)/shard_map/ppermute | solution.py:323
  11.0 4.8 %collective-permute-start.3 = (bf16[128,128]{1,0:T(8,128)(2,1)S(1)}, bf16[128,128]{1,0:T(8,128)(2,1)S(1)}, u32[]{:S(2)}, u32[]{:S(2)}) collective-permute-start(bf16[128,128]{1,0:T(8,128)(2,1)S(1)} %bitcast.44), channel_id=1, source_target_pairs={{1,0},{2,1},{3,2},{4,3},{5,4},{6,5},{7,6},{8,7},{9,8},{10,9},{11,1... | collective-permute-start | bytes 98312 | tf_op jit(solution)/shard_map/ppermute | solution.py:324
  12.4 0.9 %copy-start.2 = (bf16[32,16,3,3,3]{0,1,4,3,2:T(8,128)(2,1)S(1)}, bf16[32,16,3,3,3]{0,1,4,3,2:T(8,128)(2,1)}, u32[]{:S(2)}) copy-start(bf16[32,16,3,3,3]{0,1,4,3,2:T(8,128)(2,1)} %param.9) | copy-start | bytes 82948
  14.2 0.7 copy-start.6
  14.8 1.0 %copy-start = (bf16[1,4,8,8,256]{4,3,2,1,0:T(8,128)(2,1)S(1)}, bf16[1,4,8,8,256]{4,3,2,1,0:T(8,128)(2,1)}, u32[]{:S(2)}) copy-start(bf16[1,4,8,8,256]{4,3,2,1,0:T(8,128)(2,1)} %param.6) | copy-start | bytes 393220
  15.0 0.7 copy-start.7
  20.8 3.5 %collective-permute-start.4 = (f32[72,128]{1,0:T(8,128)S(1)}, f32[72,128]{1,0:T(8,128)S(1)}, u32[]{:S(2)}, u32[]{:S(2)}) collective-permute-start(f32[72,128]{1,0:T(8,128)S(1)} %slice_select_fusion), channel_id=1, source_target_pairs={{0,16},{1,17},{2,18},{3,19},{4,20},{5,21},{6,22},{7,23},{8,24},{9,... | collective-permute-start | bytes 110600 | tf_op jit(solution)/shard_map/ppermute | solution.py:309
  24.3 2.8 %collective-permute-start.5 = (f32[72,128]{1,0:T(8,128)S(1)}, f32[72,128]{1,0:T(8,128)S(1)}, u32[]{:S(2)}, u32[]{:S(2)}) collective-permute-start(f32[72,128]{1,0:T(8,128)S(1)} %select_add_fusion), channel_id=1, source_target_pairs={{0,1},{1,0},{2,3},{3,2},{4,5},{5,4},{6,7},{7,6},{8,9},{9,8},{10,11... | collective-permute-start | bytes 110600 | tf_op jit(solution)/shard_map/ppermute | solution.py:311
  27.1 8.3 %collective-permute-start.6 = (f32[72,128]{1,0:T(8,128)S(1)}, f32[72,128]{1,0:T(8,128)S(1)}, u32[]{:S(2)}, u32[]{:S(2)}) collective-permute-start(f32[72,128]{1,0:T(8,128)S(1)} %add.38), channel_id=1, source_target_pairs={{0,3},{1,2},{2,1},{3,0},{4,7},{5,6},{6,5},{7,4},{8,11},{9,10},{10,... | collective-permute-start | bytes 110600 | tf_op jit(solution)/shard_map/ppermute | solution.py:311
  35.5 2.8 %collective-permute-start.7 = (f32[72,128]{1,0:T(8,128)S(1)}, f32[72,128]{1,0:T(8,128)S(1)}, u32[]{:S(2)}, u32[]{:S(2)}) collective-permute-start(f32[72,128]{1,0:T(8,128)S(1)} %add.39), channel_id=1, source_target_pairs={{0,32},{1,33},{2,34},{3,35},{4,36},{5,37},{6,38},{7,39},{8,40},{9,... | collective-permute-start | bytes 110600 | tf_op jit(solution)/shard_map/ppermute | solution.py:311
  38.3 4.0 %collective-permute-start.8 = (f32[72,128]{1,0:T(8,128)S(1)}, f32[72,128]{1,0:T(8,128)S(1)}, u32[]{:S(2)}, u32[]{:S(2)}) collective-permute-start(f32[72,128]{1,0:T(8,128)S(1)} %add.40), channel_id=1, source_target_pairs={{0,96},{1,97},{2,98},{3,99},{4,100},{5,101},{6,102},{7,103},{8,104... | collective-permute-start | bytes 110600 | tf_op jit(solution)/shard_map/ppermute | solution.py:311
  42.3 3.0 %collective-permute-start.9 = (f32[72,128]{1,0:T(8,128)S(1)}, f32[72,128]{1,0:T(8,128)S(1)}, u32[]{:S(2)}, u32[]{:S(2)}) collective-permute-start(f32[72,128]{1,0:T(8,128)S(1)} %add.41), channel_id=1, source_target_pairs={{0,4},{1,5},{2,6},{3,7},{4,0},{5,1},{6,2},{7,3},{8,12},{9,13},{10,... | collective-permute-start | bytes 110600 | tf_op jit(solution)/shard_map/ppermute | solution.py:311
  45.3 4.3 %collective-permute-start.10 = (f32[72,128]{1,0:T(8,128)S(1)}, f32[72,128]{1,0:T(8,128)S(1)}, u32[]{:S(2)}, u32[]{:S(2)}) collective-permute-start(f32[72,128]{1,0:T(8,128)S(1)} %add.42), channel_id=1, source_target_pairs={{0,8},{1,9},{2,10},{3,11},{4,12},{5,13},{6,14},{7,15},{8,0},{9,1},... | collective-permute-start | bytes 110600 | tf_op jit(solution)/shard_map/ppermute | solution.py:311
  49.6 6.3 %collective-permute-start.11 = (f32[72,128]{1,0:T(8,128)S(1)}, f32[72,128]{1,0:T(8,128)S(1)}, u32[]{:S(2)}, u32[]{:S(2)}) collective-permute-start(f32[72,128]{1,0:T(8,128)S(1)} %add.43), channel_id=1, source_target_pairs={{0,140},{1,141},{2,142},{3,143},{4,136},{5,137},{6,138},{7,139},{8... | collective-permute-start | bytes 110600 | tf_op jit(solution)/shard_map/ppermute | solution.py:311
  55.9 9.0 %copy-start.3 = (f32[72,128]{1,0:T(8,128)}, f32[72,128]{1,0:T(8,128)S(1)}, u32[]{:S(2)}) copy-start(f32[72,128]{1,0:T(8,128)S(1)} %add.44.mine) | copy-start | bytes 110596
  55.9 9.0 %collective-permute-start.12 = (f32[72,128]{1,0:T(8,128)S(1)}, f32[72,128]{1,0:T(8,128)S(1)}, u32[]{:S(2)}, u32[]{:S(2)}) collective-permute-start(f32[72,128]{1,0:T(8,128)S(1)} %add.44.mine), channel_id=1, source_target_pairs={{0,16},{1,17},{2,18},{3,19},{4,20},{5,21},{6,22},{7,23},{8,24},{9,... | collective-permute-start | bytes 110600 | tf_op jit(solution)/shard_map/ppermute | solution.py:312
  64.9 0.6 copy-start.4

commit v2 on v1

--- a/solution.py
+++ b/solution.py
@@ -1,3 +1,4 @@
+import functools
 import math
 
 import jax
@@ -30,9 +31,9 @@
 
 
 def layers(
-    flags, vol, vol_lo, vol_hi, cot, cot_lo, cot_hi, w1, b1, w2, b2, w3,
+    flags, vol, below, above, cot, w1, b1, w2, b2, w3,
     act, pooled_grad, grads,
-    split, x1, x2, x3, slope, delta_one, cot_all, cot_below, cot_above, act_all, grad_all, band, thin,
+    split, x1, x2, x3, slope, delta_one, cot_all, act_all, grad_all, band, thin,
 ):
     row = lax.broadcasted_iota(jnp.int32, (256, 512), 0)
     col = lax.broadcasted_iota(jnp.int32, (256, 512), 1)
@@ -42,14 +43,14 @@
     for ci in range(4):
         planes = jnp.concatenate(
             [
-                vol_lo[ci].astype(F32),
-                vol[ci].astype(F32),
-                vol_hi[ci].astype(F32),
-                jnp.zeros((2, 8, 256), F32),
+                below[ci * 40 : ci * 40 + 40, :].astype(F32),
+                vol[ci].astype(F32).reshape(64, 256),
+                above[ci * 40 : ci * 40 + 40, :].astype(F32),
+                jnp.zeros((16, 256), F32),
             ],
             axis=0,
         )
-        parts = plain_dot(planes.reshape(160, 256).astype(BF16), pick)
+        parts = plain_dot(planes.astype(BF16), pick)
         for group in range(5):
             for kind_n in range(4):
                 split[kind_n, (group * 4 + ci) * 32 : (group * 4 + ci + 1) * 32, :] = parts[
@@ -109,8 +110,6 @@
                             row0 = plane * 144 + (kh * 3 + kw) * 16
                             x2[row0 : row0 + 16, out_h * 128 : out_h * 128 + 128] = moved
     cot_all[0:512, :] = cot[...].astype(F32)
-    cot_below[0:128, :] = cot_lo[...].astype(F32)
-    cot_above[0:128, :] = cot_hi[...].astype(F32)
     for plane in range(6):
         base = plane * 288
         x3[base : base + 96, 0:128] = jnp.zeros((96, 128), BF16)
@@ -124,10 +123,10 @@
         leaky = jnp.where(positive, linear, LEAK * linear)
         for high in range(4):
             lanes = slice(high * 128, high * 128 + 128)
-            if plane == 0:
-                target = cot_below[pl.ds(high, 32, stride=4), :]
-            elif plane == 5:
-                target = cot_above[pl.ds(high, 32, stride=4), :]
+            if plane in (0, 5):
+                outer = below if plane == 0 else above
+                row0, lane0 = 160 + high // 2 * 32, high % 2 * 128
+                target = outer[row0 : row0 + 32, lane0 : lane0 + 128].astype(F32)
             else:
                 at = (plane - 1) * 4 + high
                 target = cot_all[pl.ds(at, 32, stride=16), :]
@@ -140,7 +139,7 @@
                         row0 = plane * 288 + (kh * 3 + kw) * 32
                         x3[row0 : row0 + 32, out_h * 128 : out_h * 128 + 128] = moved
     act[...] = act_all[0:512, :].astype(BF16)
-    weights_three = w3[...]
+    weights_three = w3[:, 0:864]
     for plane in range(4):
         total = plain_dot(weights_three, x3[plane * 288 : plane * 288 + 864, :])
         for high in range(4):
@@ -198,9 +197,54 @@
     grads[136:144, :] = jnp.where(lane < 32, shift_two[0:8], ones)
 
 
-def unpack(scales, mine, other, grad_one, shift_one, grad_two, shift_two, whole):
-    scale_one, scale_two = scales[1], scales[2]
-    low = scales[0] > 0
+def edges(vol, cot, upward, downward, cot_all):
+    cot_all[0:512, :] = cot[...].astype(F32)
+    for out, first, plane in ((upward, PLANES - HALO, 3), (downward, 0, 0)):
+        for ci in range(4):
+            block = vol[ci, first : first + HALO].astype(F32).reshape(40, 256)
+            out[ci * 40 : ci * 40 + 40, :] = block.astype(BF16)
+        for high in range(4):
+            row0, lane0 = 160 + high // 2 * 32, high % 2 * 128
+            tile = cot_all[pl.ds(plane * 4 + high, 32, stride=16), :]
+            out[row0 : row0 + 32, lane0 : lane0 + 128] = tile.astype(BF16)
+
+
+def column(row, height):
+    count = row.shape[1]
+    at = lax.broadcasted_iota(jnp.int32, (height, count), 0) % count
+    lane = lax.broadcasted_iota(jnp.int32, (height, count), 1)
+    return jnp.sum(jnp.where(at == lane, row, 0.0), axis=1, keepdims=True)
+
+
+def prepare(first, bias_one, second, bias_two, w1, b1, w2, b2, w3, wide_one, wide_two, bands):
+    b1[...] = column(bias_one[...], 64)
+    b2[...] = column(bias_two[...], 32)
+    wide_one[...] = jnp.zeros((112, 128), F32)
+    wide_one[0:108, 0:16] = first[...].astype(F32)
+    bands[...] = jnp.zeros((384, 128), F32)
+    for at in range(6):
+        total = jnp.zeros((36, 128), F32)
+        for kd in range(3):
+            j = at - kd
+            if 0 <= j < 4:
+                piece = wide_one[kd * 36 : kd * 36 + 36, :]
+                total = total + (pltpu.roll(piece, 16 * j, 1) if j else piece)
+        bands[pl.ds(at // 4 * 144 + at % 4, 36, stride=4), :] = total
+    w1[...] = bands[...].T[0:64, 0:288].astype(BF16)
+    wide_two[...] = jnp.zeros((512, 128), F32)
+    wide_two[0:432, 0:32] = second[...].astype(F32)
+    w2[...] = wide_two[...].T[0:32, 0:432].astype(BF16)
+    for quad in range(7):
+        total = wide_two[(26 - quad * 4) * 16 : (26 - quad * 4) * 16 + 16, :]
+        for k in range(1, 4):
+            tap = 26 - quad * 4 - k
+            if tap >= 0:
+                total = total + pltpu.roll(wide_two[tap * 16 : tap * 16 + 16, :], 32 * k, 1)
+        w3[:, quad * 128 : quad * 128 + 128] = total.astype(BF16)
+
+
+def unpack(scale_one, scale_two, core, mine, other, grad_one, shift_one, grad_two, shift_two, whole):
+    low = core[0] == 0
     whole[0:72, :] = jnp.where(low, mine[...], other[...])
     whole[72:144, :] = jnp.where(low, other[...], mine[...])
     for group in range(4):
@@ -245,21 +289,53 @@
             pltpu.VMEM((128, 2048), F32),
             pltpu.VMEM((128, 2048), BF16),
             pltpu.VMEM((528, 128), F32),
-            pltpu.VMEM((136, 128), F32),
-            pltpu.VMEM((136, 128), F32),
             pltpu.VMEM((528, 128), F32),
             pltpu.VMEM((272, 128), F32),
             pltpu.VMEM((304, 128), F32),
             pltpu.VMEM((48, 128), F32),
         ],
-        compiler_params=pltpu.CompilerParams(vmem_limit_bytes=40 << 20),
+        compiler_params=pltpu.CompilerParams(vmem_limit_bytes=24 << 20),
         name="layers",
     )(flags, *arrays)
 
 
-def run_unpack(scales, mine, other):
+def run_edges(sample, target):
     return pl.pallas_call(
-        unpack,
+        edges,
+        out_shape=(jax.ShapeDtypeStruct((224, 256), BF16),) * 2,
+        in_specs=in_vmem(2),
+        out_specs=tuple(in_vmem(2)),
+        scratch_shapes=[pltpu.VMEM((528, 128), F32)],
+        compiler_params=pltpu.CompilerParams(vmem_limit_bytes=4 << 20),
+        name="edges",
+    )(sample, target)
+
+
+def run_prepare(*filters):
+    return pl.pallas_call(
+        prepare,
+        out_shape=(
+            jax.ShapeDtypeStruct((64, 288), BF16),
+            jax.ShapeDtypeStruct((64, 1), F32),
+            jax.ShapeDtypeStruct((32, 432), BF16),
+            jax.ShapeDtypeStruct((32, 1), F32),
+            jax.ShapeDtypeStruct((16, 896), BF16),
+        ),
+        in_specs=in_vmem(4),
+        out_specs=tuple(in_vmem(5)),
+        scratch_shapes=[
+            pltpu.VMEM((112, 128), F32),
+            pltpu.VMEM((512, 128), F32),
+            pltpu.VMEM((384, 128), F32),
+        ],
+        compiler_params=pltpu.CompilerParams(vmem_limit_bytes=4 << 20),
+        name="prepare",
+    )(*filters)
+
+
+def run_unpack(scales, core_index, mine, other):
+    return pl.pallas_call(
+        functools.partial(unpack, *scales),
         out_shape=(
             jax.ShapeDtypeStruct((27, 4, 16), F32),
             jax.ShapeDtypeStruct((1, 16), F32),
@@ -269,15 +345,9 @@
         in_specs=[pl.BlockSpec(memory_space=pltpu.SMEM)] + in_vmem(2),
         out_specs=tuple(in_vmem(4)),
         scratch_shapes=[pltpu.VMEM((144, 128), F32)],
+        compiler_params=pltpu.CompilerParams(vmem_limit_bytes=4 << 20),
         name="unpack",
-    )(scales, mine, other)
-
-
-def banded(first_filters):
-    taps = first_filters.transpose(2, 3, 4, 1, 0).reshape(3, 9, 4, 16)
-    shifted = [jnp.pad(taps, ((j, 5 - j), (0, 0), (0, 0), (0, 0))) for j in range(4)]
-    wide = jnp.stack(shifted, 0).reshape(4, 2, 4, 9, 4, 16)
-    return wide.transpose(0, 5, 1, 3, 4, 2).reshape(64, 288)
+    )(core_index, mine, other)
 
 
 def device_exchanges():
@@ -297,7 +367,7 @@
         return pairs
 
     core = pairing(0, 1)
-    others = [pairing(*step) for step in ((2, 1), (2, 3), (1, 1), (1, 3), (3, 1), (3, 2), (3, 7))]
+    others = [pairing(*step) for step in ((2, 1), (2, 2), (1, 1), (1, 2), (3, 1), (3, 2), (3, 7))]
     return core, others
 
 
@@ -312,38 +382,35 @@
     return mine, lax.ppermute(mine, axes, core)
 
 
+def as_rows(first_filters, first_biases, second_filters, second_biases):
+    return (
+        first_filters.transpose(2, 3, 4, 1, 0).reshape(108, 16),
+        first_biases[None],
+        second_filters.transpose(2, 3, 4, 1, 0).reshape(432, 32),
+        second_biases[None],
+    )
+
+
 def shards(volume, first_filters, first_biases, second_filters, second_biases, cotangent):
     sample, target = volume[0], cotangent[0]
     slabs = lax.axis_size("space")
     here = lax.axis_index("space")
     forward = [(i, i + 1) for i in range(slabs - 1)]
     backward = [(i + 1, i) for i in range(slabs - 1)]
-    vol_lo = lax.ppermute(sample[:, PLANES - HALO :], "space", forward)
-    vol_hi = lax.ppermute(sample[:, :HALO], "space", backward)
-    cot_lo = lax.ppermute(target[:, 3].reshape(128, 128), "space", forward)
-    cot_hi = lax.ppermute(target[:, 0].reshape(128, 128), "space", backward)
-    w1 = banded(first_filters)
-    b1 = jnp.tile(first_biases, 4)[:, None]
-    w2 = second_filters.transpose(0, 2, 3, 4, 1).reshape(32, 432)
-    w3 = jnp.flip(second_filters, (2, 3, 4)).transpose(1, 2, 3, 4, 0).reshape(16, 864)
+    target = target.reshape(512, 128)
+    upward, downward = run_edges(sample, target)
+    below = lax.ppermute(upward, "space", forward)
+    above = lax.ppermute(downward, "space", backward)
+    matrices = run_prepare(*as_rows(first_filters, first_biases, second_filters, second_biases))
     flags = jnp.stack([here > 0, here < slabs - 1]).astype(F32)
-    act, pooled_grad, grads = run_layers(
-        flags, sample, vol_lo, vol_hi, target.reshape(512, 128), cot_lo, cot_hi,
-        w1, b1, w2, second_biases[:, None], w3,
-    )
+    act, pooled_grad, grads = run_layers(flags, sample, below, above, target, *matrices)
     core_index = lax.axis_index("dp") % 2
     mine, other = add_up(grads, core_index)
     count_one = (
         lax.axis_size("dp") * slabs * PLANES * sample.shape[2] * sample.shape[3]
     )
-    scales = jnp.stack(
-        [
-            (core_index == 0).astype(F32),
-            jnp.float32(1.0 / math.sqrt(count_one)),
-            jnp.float32(1.0 / math.sqrt(count_one / 8)),
-        ]
-    )
-    grad_one, shift_one, grad_two, shift_two = run_unpack(scales, mine, other)
+    scales = (1.0 / math.sqrt(count_one), 1.0 / math.sqrt(count_one / 8))
+    grad_one, shift_one, grad_two, shift_two = run_unpack(scales, core_index[None], mine, other)
     return (
         act.reshape(1, 32, 4, 4, 128),
         pooled_grad.reshape(1, 16, 4, 4, 128),

time: 67.5 us -> 58.8 us (0.87)
  starting transfers between devices: 42.8 us -> 33.3 us
  waiting for transfers between devices: 11.2 us -> 15.8 us
  local copies, waits for them, and re-layouts: 4.58 us -> 1.86 us
  other arithmetic: 1.11 us -> 0.14 us
    ppermute x4 -> x2, starting transfers between devices: 10.6 us -> 5.46 us  [the longest x1 4.17 us: shards(): below = lax.ppermute(upward, 'space', forward)]
    ppermute x7, starting transfers between devices: 21.4 us -> 17.5 us  [add_up(): mine = mine + lax.ppermute(mine, axes, pairs)]
    ppermute x4 -> x2, waiting for transfers between devices: 0.01 us -> 3.69 us  [the longest x1 3.69 us: shards(): above = lax.ppermute(downward, 'space', backward)]
    slice x2 -> x0, local copies, waits for them, and re-layouts: 1.01 us -> none  [the longest x1 0.98 us: shards(): vol_hi = lax.ppermute(sample[:, :HALO], 'space', backward)]
    unnamed x16, local copies, waits for them, and re-layouts: 2.59 us -> 1.83 us
    pallas_call x1 -> x3, Pallas kernels: 1.61 us -> 1.25 us  [the longest x1 0.82 us: run_unpack(): pl.pallas_call(functools.partial(unpack, *scales), out_shape=(jax.ShapeDt...]
  transfers between devices with their start and end apart: 13 -> 11, of which waited for: 9 -> 10; matrix products, arithmetic and copies ran while one was open for 3% -> 0% of each run, Pallas kernels for 0% -> 1%
where the time goes in v2:
time: 58.8 us; the launch traced here: 58.1 us
  starting transfers between devices  33.3 us (57%)
  waiting for transfers between devices  15.8 us (27%)
  Pallas kernels  6.22 us (11%)
  local copies, waits for them, and re-layouts  1.86 us (3%)
  between operations  0.77 us (1%)
    ppermute x7, starting transfers between devices, add_up(): mine = mine + lax.ppermute(mine, axes, pairs)  17.5 us
    ppermute x7, waiting for transfers between devices, add_up(): mine = mine + lax.ppermute(mine, axes, pairs)  10.3 us
    ppermute x1, starting transfers between devices, add_up(): return (mine, lax.ppermute(mine, axes, core))  8.16 us
    pallas_call x1, Pallas kernels, run_layers(): pl.pallas_call(layers, out_shape=(jax.ShapeDtypeStruct((512, 128), BF16),...  4.97 us
    ppermute x1, starting transfers between devices, shards(): below = lax.ppermute(upward, 'space', forward)  4.17 us
    ppermute x1, waiting for transfers between devices, shards(): above = lax.ppermute(downward, 'space', backward)  3.69 us
    ppermute x1, starting transfers between devices, add_up(): lax.ppermute(jnp.where(low, bottom, top), axes, core)  2.19 us
    unnamed x16, local copies, waits for them, and re-layouts  1.83 us
  transfers between devices with their start and end apart: 11, of which 10 were waited for; matrix products, arithmetic and copies ran while one was open for 0% of the time, Pallas kernels for 1%

profile of v2, /device:TPU:1, one launch (start us, length us, event | category | flops | bytes accessed | tf_op | source)
XLA Modules:
  0.0 58.1 jit_solution(16145171248405157709)
XLA Ops:
  0.6 0.0 copy-start
  0.6 0.9 %copy-done = bf16[1,4,8,8,256]{4,3,2,1,0:T(8,128)(2,1)S(1)} copy-done((bf16[1,4,8,8,256]{4,3,2,1,0:T(8,128)(2,1)S(1)}, bf16[1,4,8,8,256]{4,3,2,1,0:T(8,128)(2,1)}, u32[]{:S(2)}) %copy-start) | copy-done | bytes 131096
  1.5 0.0 copy-start.2
  1.5 0.9 %copy-done.2 = bf16[1,32,4,4,128]{4,3,2,1,0:T(4,128)(2,1)S(1)} copy-done((bf16[1,32,4,4,128]{4,3,2,1,0:T(4,128)(2,1)S(1)}, bf16[1,32,4,4,128]{4,3,2,1,0:T(4,128)(2,1)}, u32[]{:S(2)}) %copy-start.2) | copy-done | bytes 131096
  2.4 0.0 copy-start.7
  2.4 0.0 copy-start.4
  2.4 0.0 copy-start.5
  2.5 0.0 copy-start.6
  2.5 0.1 edges.1
  2.5 0.0 copy-start.1
  2.5 0.0 copy-start.3
  2.6 4.2 %collective-permute-start = (bf16[224,256]{1,0:T(8,128)(2,1)S(1)}, bf16[224,256]{1,0:T(8,128)(2,1)S(1)}, u32[]{:S(2)}, u32[]{:S(2)}) collective-permute-start(bf16[224,256]{1,0:T(8,128)(2,1)S(1)} %get-tuple-element.20), channel_id=1, source_target_pairs={{0,1},{1,2},{2,3},{3,4},{4,5},{5,6},{6,7},{7,8},{8,9},{9,10},{10,1... | collective-permute-start | bytes 344072 | tf_op jit(solution)/shard_map/ppermute | solution.py:402
  6.7 1.3 %collective-permute-start.1 = (bf16[224,256]{1,0:T(8,128)(2,1)S(1)}, bf16[224,256]{1,0:T(8,128)(2,1)S(1)}, u32[]{:S(2)}, u32[]{:S(2)}) collective-permute-start(bf16[224,256]{1,0:T(8,128)(2,1)S(1)} %get-tuple-element.21), channel_id=1, source_target_pairs={{1,0},{2,1},{3,2},{4,3},{5,4},{6,5},{7,6},{8,7},{9,8},{10,9},{11,1... | collective-permute-start | bytes 344072 | tf_op jit(solution)/shard_map/ppermute | solution.py:403
  8.0 0.0 copy-done.7
  8.1 0.0 copy-done.4
  8.1 0.0 copy-done.5
  8.1 0.0 copy-done.6
  8.1 0.4 prepare.1
  8.5 0.1 add_convert_fusion.flags
  8.6 0.0 collective-permute-done.below
  8.6 3.7 %collective-permute-done.1.above = bf16[224,256]{1,0:T(8,128)(2,1)S(1)} collective-permute-done((bf16[224,256]{1,0:T(8,128)(2,1)S(1)}, bf16[224,256]{1,0:T(8,128)(2,1)S(1)}, u32[]{:S(2)}, u32[]{:S(2)}) %collective-permute-start.1) | collective-permute-done | bytes 114720 | tf_op jit(solution)/shard_map/ppermute | solution.py:403
  12.3 0.0 copy-done.1
  12.3 0.0 copy-done.3
  12.3 5.0 %layers.1 = (bf16[512,128]{1,0:T(8,128)(2,1)}, bf16[256,128]{1,0:T(8,128)(2,1)}, f32[144,128]{1,0:T(8,128)S(1)}) custom-call(f32[2]{0:T(128)S(1)} %add_convert_fusion.flags, bf16[4,8,8,256]{3,2,1,0:T(8,128)(2,1)S(1)} %bitcast.22, bf16[224,256]{1,0:T(8,128)(2,1)S(1)} %collective-permute-done.below, bf16[224,256]{1,0:T(8,128)(2,1)S(1)} %collective-permute-done.1.above, ...), custom_call_target="tpu_custom_call" | custom-call | tf_op jit(solution)/shard_map/layers/pallas_call | solution.py:275
  17.3 2.2 %collective-permute-start.2 = (f32[72,128]{1,0:T(8,128)S(1)}, f32[72,128]{1,0:T(8,128)S(1)}, u32[]{:S(2)}, u32[]{:S(2)}) collective-permute-start(f32[72,128]{1,0:T(8,128)S(1)} %slice_select_fusion), channel_id=1, source_target_pairs={{0,16},{1,17},{2,18},{3,19},{4,20},{5,21},{6,22},{7,23},{8,24},{9,... | collective-permute-start | bytes 110600 | tf_op jit(solution)/shard_map/ppermute | solution.py:379
  19.5 0.9 %collective-permute-done.2 = f32[72,128]{1,0:T(8,128)S(1)} collective-permute-done((f32[72,128]{1,0:T(8,128)S(1)}, f32[72,128]{1,0:T(8,128)S(1)}, u32[]{:S(2)}, u32[]{:S(2)}) %collective-permute-start.2) | collective-permute-done | bytes 36896 | tf_op jit(solution)/shard_map/ppermute | solution.py:379
  20.3 1.3 %collective-permute-start.3 = (f32[72,128]{1,0:T(8,128)S(1)}, f32[72,128]{1,0:T(8,128)S(1)}, u32[]{:S(2)}, u32[]{:S(2)}) collective-permute-start(f32[72,128]{1,0:T(8,128)S(1)} %select_add_fusion), channel_id=1, source_target_pairs={{0,1},{1,0},{2,3},{3,2},{4,5},{5,4},{6,7},{7,6},{8,9},{9,8},{10,11... | collective-permute-start | bytes 110600 | tf_op jit(solution)/shard_map/ppermute | solution.py:381
  21.7 1.5 %collective-permute-done.3 = f32[72,128]{1,0:T(8,128)S(1)} collective-permute-done((f32[72,128]{1,0:T(8,128)S(1)}, f32[72,128]{1,0:T(8,128)S(1)}, u32[]{:S(2)}, u32[]{:S(2)}) %collective-permute-start.3) | collective-permute-done | bytes 36896 | tf_op jit(solution)/shard_map/ppermute | solution.py:381
  23.2 4.6 %collective-permute-start.4 = (f32[72,128]{1,0:T(8,128)S(1)}, f32[72,128]{1,0:T(8,128)S(1)}, u32[]{:S(2)}, u32[]{:S(2)}) collective-permute-start(f32[72,128]{1,0:T(8,128)S(1)} %add.30), channel_id=1, source_target_pairs={{0,2},{1,3},{2,0},{3,1},{4,6},{5,7},{6,4},{7,5},{8,10},{9,11},{10,... | collective-permute-start | bytes 110600 | tf_op jit(solution)/shard_map/ppermute | solution.py:381
  27.7 1.3 %collective-permute-done.4 = f32[72,128]{1,0:T(8,128)S(1)} collective-permute-done((f32[72,128]{1,0:T(8,128)S(1)}, f32[72,128]{1,0:T(8,128)S(1)}, u32[]{:S(2)}, u32[]{:S(2)}) %collective-permute-start.4) | collective-permute-done | bytes 36896 | tf_op jit(solution)/shard_map/ppermute | solution.py:381
  29.1 1.2 %collective-permute-start.5 = (f32[72,128]{1,0:T(8,128)S(1)}, f32[72,128]{1,0:T(8,128)S(1)}, u32[]{:S(2)}, u32[]{:S(2)}) collective-permute-start(f32[72,128]{1,0:T(8,128)S(1)} %add.31), channel_id=1, source_target_pairs={{0,32},{1,33},{2,34},{3,35},{4,36},{5,37},{6,38},{7,39},{8,40},{9,... | collective-permute-start | bytes 110600 | tf_op jit(solution)/shard_map/ppermute | solution.py:381
  30.3 1.6 %collective-permute-done.5 = f32[72,128]{1,0:T(8,128)S(1)} collective-permute-done((f32[72,128]{1,0:T(8,128)S(1)}, f32[72,128]{1,0:T(8,128)S(1)}, u32[]{:S(2)}, u32[]{:S(2)}) %collective-permute-start.5) | collective-permute-done | bytes 36896 | tf_op jit(solution)/shard_map/ppermute | solution.py:381
  31.9 2.8 %collective-permute-start.6 = (f32[72,128]{1,0:T(8,128)S(1)}, f32[72,128]{1,0:T(8,128)S(1)}, u32[]{:S(2)}, u32[]{:S(2)}) collective-permute-start(f32[72,128]{1,0:T(8,128)S(1)} %add.32), channel_id=1, source_target_pairs={{0,64},{1,65},{2,66},{3,67},{4,68},{5,69},{6,70},{7,71},{8,72},{9,... | collective-permute-start | bytes 110600 | tf_op jit(solution)/shard_map/ppermute | solution.py:381
  34.7 1.6 %collective-permute-done.6 = f32[72,128]{1,0:T(8,128)S(1)} collective-permute-done((f32[72,128]{1,0:T(8,128)S(1)}, f32[72,128]{1,0:T(8,128)S(1)}, u32[]{:S(2)}, u32[]{:S(2)}) %collective-permute-start.6) | collective-permute-done | bytes 36896 | tf_op jit(solution)/shard_map/ppermute | solution.py:381
  36.2 1.6 %collective-permute-start.7 = (f32[72,128]{1,0:T(8,128)S(1)}, f32[72,128]{1,0:T(8,128)S(1)}, u32[]{:S(2)}, u32[]{:S(2)}) collective-permute-start(f32[72,128]{1,0:T(8,128)S(1)} %add.33), channel_id=1, source_target_pairs={{0,4},{1,5},{2,6},{3,7},{4,0},{5,1},{6,2},{7,3},{8,12},{9,13},{10,... | collective-permute-start | bytes 110600 | tf_op jit(solution)/shard_map/ppermute | solution.py:381
  37.9 1.6 %collective-permute-done.7 = f32[72,128]{1,0:T(8,128)S(1)} collective-permute-done((f32[72,128]{1,0:T(8,128)S(1)}, f32[72,128]{1,0:T(8,128)S(1)}, u32[]{:S(2)}, u32[]{:S(2)}) %collective-permute-start.7) | collective-permute-done | bytes 36896 | tf_op jit(solution)/shard_map/ppermute | solution.py:381
  39.5 2.8 %collective-permute-start.8 = (f32[72,128]{1,0:T(8,128)S(1)}, f32[72,128]{1,0:T(8,128)S(1)}, u32[]{:S(2)}, u32[]{:S(2)}) collective-permute-start(f32[72,128]{1,0:T(8,128)S(1)} %add.34), channel_id=1, source_target_pairs={{0,8},{1,9},{2,10},{3,11},{4,12},{5,13},{6,14},{7,15},{8,0},{9,1},... | collective-permute-start | bytes 110600 | tf_op jit(solution)/shard_map/ppermute | solution.py:381
  42.3 1.4 %collective-permute-done.8 = f32[72,128]{1,0:T(8,128)S(1)} collective-permute-done((f32[72,128]{1,0:T(8,128)S(1)}, f32[72,128]{1,0:T(8,128)S(1)}, u32[]{:S(2)}, u32[]{:S(2)}) %collective-permute-start.8) | collective-permute-done | bytes 36896 | tf_op jit(solution)/shard_map/ppermute | solution.py:381
  43.7 3.2 %collective-permute-start.9 = (f32[72,128]{1,0:T(8,128)S(1)}, f32[72,128]{1,0:T(8,128)S(1)}, u32[]{:S(2)}, u32[]{:S(2)}) collective-permute-start(f32[72,128]{1,0:T(8,128)S(1)} %add.35), channel_id=1, source_target_pairs={{0,140},{1,141},{2,142},{3,143},{4,136},{5,137},{6,138},{7,139},{8... | collective-permute-start | bytes 110600 | tf_op jit(solution)/shard_map/ppermute | solution.py:381
  46.9 1.3 %collective-permute-done.9 = f32[72,128]{1,0:T(8,128)S(1)} collective-permute-done((f32[72,128]{1,0:T(8,128)S(1)}, f32[72,128]{1,0:T(8,128)S(1)}, u32[]{:S(2)}, u32[]{:S(2)}) %collective-permute-start.9) | collective-permute-done | bytes 36896 | tf_op jit(solution)/shard_map/ppermute | solution.py:381
  48.2 8.2 %collective-permute-start.10 = (f32[72,128]{1,0:T(8,128)S(1)}, f32[72,128]{1,0:T(8,128)S(1)}, u32[]{:S(2)}, u32[]{:S(2)}) collective-permute-start(f32[72,128]{1,0:T(8,128)S(1)} %add.36.mine), channel_id=1, source_target_pairs={{0,16},{1,17},{2,18},{3,19},{4,20},{5,21},{6,22},{7,23},{8,24},{9,... | collective-permute-start | bytes 110600 | tf_op jit(solution)/shard_map/ppermute | solution.py:382
  56.4 0.9 %collective-permute-done.10.other = f32[72,128]{1,0:T(8,128)S(1)} collective-permute-done((f32[72,128]{1,0:T(8,128)S(1)}, f32[72,128]{1,0:T(8,128)S(1)}, u32[]{:S(2)}, u32[]{:S(2)}) %collective-permute-start.10) | collective-permute-done | bytes 36896 | tf_op jit(solution)/shard_map/ppermute | solution.py:382
  57.3 0.8 %unpack.1 = (f32[27,4,16]{2,1,0:T(4,128)}, f32[1,16]{1,0:T(1,128)}, f32[27,16,32]{2,1,0:T(8,128)}, f32[1,32]{1,0:T(1,128)}) custom-call(s32[1]{0:T(128)} %bitcast.11.core, f32[72,128]{1,0:T(8,128)S(1)} %add.36.mine, f32[72,128]{1,0:T(8,128)S(1)} %collective-permute-done.10.other), custom_call_target="tpu_custom_call" | custom-call | tf_op jit(solution)/shard_map/unpack/pallas_call | solution.py:337
  (10 shorter events, 0.1 us)
Async XLA Ops:
  0.6 0.9 %copy-start = (bf16[1,4,8,8,256]{4,3,2,1,0:T(8,128)(2,1)S(1)}, bf16[1,4,8,8,256]{4,3,2,1,0:T(8,128)(2,1)}, u32[]{:S(2)}) copy-start(bf16[1,4,8,8,256]{4,3,2,1,0:T(8,128)(2,1)} %param.6) | copy-start | bytes 393220
  1.5 0.9 %copy-start.2 = (bf16[1,32,4,4,128]{4,3,2,1,0:T(4,128)(2,1)S(1)}, bf16[1,32,4,4,128]{4,3,2,1,0:T(4,128)(2,1)}, u32[]{:S(2)}) copy-start(bf16[1,32,4,4,128]{4,3,2,1,0:T(4,128)(2,1)} %param.11) | copy-start | bytes 393220
  2.4 5.6 %copy-start.7 = (bf16[16,4,3,3,3]{0,1,4,3,2:T(4,128)(2,1)S(1)}, bf16[16,4,3,3,3]{0,1,4,3,2:T(4,128)(2,1)}, u32[]{:S(2)}) copy-start(bf16[16,4,3,3,3]{0,1,4,3,2:T(4,128)(2,1)} %param.7) | copy-start | bytes 10372
  2.4 5.7 %copy-start.4 = (bf16[32,16,3,3,3]{0,1,4,3,2:T(8,128)(2,1)S(1)}, bf16[32,16,3,3,3]{0,1,4,3,2:T(8,128)(2,1)}, u32[]{:S(2)}) copy-start(bf16[32,16,3,3,3]{0,1,4,3,2:T(8,128)(2,1)} %param.9) | copy-start | bytes 82948
  2.4 5.7 %copy-start.5 = (f32[16]{0:T(128)S(1)}, f32[16]{0:T(128)}, u32[]{:S(2)}) copy-start(f32[16]{0:T(128)} %param.8) | copy-start | bytes 196
  2.5 5.7 %copy-start.6 = (f32[32]{0:T(128)S(1)}, f32[32]{0:T(128)}, u32[]{:S(2)}) copy-start(f32[32]{0:T(128)} %param.10) | copy-start | bytes 388
  2.5 9.7 %copy-start.1 = (bf16[1,4,8,8,256]{4,3,2,1,0:T(8,128)(2,1)S(1)}, bf16[1,4,8,8,256]{4,3,2,1,0:T(8,128)(2,1)}, u32[]{:S(2)}) copy-start(bf16[1,4,8,8,256]{4,3,2,1,0:T(8,128)(2,1)} %param.6) | copy-start | bytes 393220
  2.5 9.7 %copy-start.3 = (bf16[1,32,4,4,128]{4,3,2,1,0:T(4,128)(2,1)S(1)}, bf16[1,32,4,4,128]{4,3,2,1,0:T(4,128)(2,1)}, u32[]{:S(2)}) copy-start(bf16[1,32,4,4,128]{4,3,2,1,0:T(4,128)(2,1)} %param.11) | copy-start | bytes 393220
  2.6 6.0 %collective-permute-start = (bf16[224,256]{1,0:T(8,128)(2,1)S(1)}, bf16[224,256]{1,0:T(8,128)(2,1)S(1)}, u32[]{:S(2)}, u32[]{:S(2)}) collective-permute-start(bf16[224,256]{1,0:T(8,128)(2,1)S(1)} %get-tuple-element.20), channel_id=1, source_target_pairs={{0,1},{1,2},{2,3},{3,4},{4,5},{5,6},{6,7},{7,8},{8,9},{9,10},{10,1... | collective-permute-start | bytes 344072 | tf_op jit(solution)/shard_map/ppermute | solution.py:402
  6.7 5.5 %collective-permute-start.1 = (bf16[224,256]{1,0:T(8,128)(2,1)S(1)}, bf16[224,256]{1,0:T(8,128)(2,1)S(1)}, u32[]{:S(2)}, u32[]{:S(2)}) collective-permute-start(bf16[224,256]{1,0:T(8,128)(2,1)S(1)} %get-tuple-element.21), channel_id=1, source_target_pairs={{1,0},{2,1},{3,2},{4,3},{5,4},{6,5},{7,6},{8,7},{9,8},{10,9},{11,1... | collective-permute-start | bytes 344072 | tf_op jit(solution)/shard_map/ppermute | solution.py:403
  17.3 3.1 %collective-permute-start.2 = (f32[72,128]{1,0:T(8,128)S(1)}, f32[72,128]{1,0:T(8,128)S(1)}, u32[]{:S(2)}, u32[]{:S(2)}) collective-permute-start(f32[72,128]{1,0:T(8,128)S(1)} %slice_select_fusion), channel_id=1, source_target_pairs={{0,16},{1,17},{2,18},{3,19},{4,20},{5,21},{6,22},{7,23},{8,24},{9,... | collective-permute-start | bytes 110600 | tf_op jit(solution)/shard_map/ppermute | solution.py:379
  20.3 2.9 %collective-permute-start.3 = (f32[72,128]{1,0:T(8,128)S(1)}, f32[72,128]{1,0:T(8,128)S(1)}, u32[]{:S(2)}, u32[]{:S(2)}) collective-permute-start(f32[72,128]{1,0:T(8,128)S(1)} %select_add_fusion), channel_id=1, source_target_pairs={{0,1},{1,0},{2,3},{3,2},{4,5},{5,4},{6,7},{7,6},{8,9},{9,8},{10,11... | collective-permute-start | bytes 110600 | tf_op jit(solution)/shard_map/ppermute | solution.py:381
  23.2 5.9 %collective-permute-start.4 = (f32[72,128]{1,0:T(8,128)S(1)}, f32[72,128]{1,0:T(8,128)S(1)}, u32[]{:S(2)}, u32[]{:S(2)}) collective-permute-start(f32[72,128]{1,0:T(8,128)S(1)} %add.30), channel_id=1, source_target_pairs={{0,2},{1,3},{2,0},{3,1},{4,6},{5,7},{6,4},{7,5},{8,10},{9,11},{10,... | collective-permute-start | bytes 110600 | tf_op jit(solution)/shard_map/ppermute | solution.py:381
  29.1 2.8 %collective-permute-start.5 = (f32[72,128]{1,0:T(8,128)S(1)}, f32[72,128]{1,0:T(8,128)S(1)}, u32[]{:S(2)}, u32[]{:S(2)}) collective-permute-start(f32[72,128]{1,0:T(8,128)S(1)} %add.31), channel_id=1, source_target_pairs={{0,32},{1,33},{2,34},{3,35},{4,36},{5,37},{6,38},{7,39},{8,40},{9,... | collective-permute-start | bytes 110600 | tf_op jit(solution)/shard_map/ppermute | solution.py:381
  31.9 4.3 %collective-permute-start.6 = (f32[72,128]{1,0:T(8,128)S(1)}, f32[72,128]{1,0:T(8,128)S(1)}, u32[]{:S(2)}, u32[]{:S(2)}) collective-permute-start(f32[72,128]{1,0:T(8,128)S(1)} %add.32), channel_id=1, source_target_pairs={{0,64},{1,65},{2,66},{3,67},{4,68},{5,69},{6,70},{7,71},{8,72},{9,... | collective-permute-start | bytes 110600 | tf_op jit(solution)/shard_map/ppermute | solution.py:381
  36.2 3.3 %collective-permute-start.7 = (f32[72,128]{1,0:T(8,128)S(1)}, f32[72,128]{1,0:T(8,128)S(1)}, u32[]{:S(2)}, u32[]{:S(2)}) collective-permute-start(f32[72,128]{1,0:T(8,128)S(1)} %add.33), channel_id=1, source_target_pairs={{0,4},{1,5},{2,6},{3,7},{4,0},{5,1},{6,2},{7,3},{8,12},{9,13},{10,... | collective-permute-start | bytes 110600 | tf_op jit(solution)/shard_map/ppermute | solution.py:381
  39.5 4.2 %collective-permute-start.8 = (f32[72,128]{1,0:T(8,128)S(1)}, f32[72,128]{1,0:T(8,128)S(1)}, u32[]{:S(2)}, u32[]{:S(2)}) collective-permute-start(f32[72,128]{1,0:T(8,128)S(1)} %add.34), channel_id=1, source_target_pairs={{0,8},{1,9},{2,10},{3,11},{4,12},{5,13},{6,14},{7,15},{8,0},{9,1},... | collective-permute-start | bytes 110600 | tf_op jit(solution)/shard_map/ppermute | solution.py:381
  43.7 4.5 %collective-permute-start.9 = (f32[72,128]{1,0:T(8,128)S(1)}, f32[72,128]{1,0:T(8,128)S(1)}, u32[]{:S(2)}, u32[]{:S(2)}) collective-permute-start(f32[72,128]{1,0:T(8,128)S(1)} %add.35), channel_id=1, source_target_pairs={{0,140},{1,141},{2,142},{3,143},{4,136},{5,137},{6,138},{7,139},{8... | collective-permute-start | bytes 110600 | tf_op jit(solution)/shard_map/ppermute | solution.py:381
  48.2 9.0 %collective-permute-start.10 = (f32[72,128]{1,0:T(8,128)S(1)}, f32[72,128]{1,0:T(8,128)S(1)}, u32[]{:S(2)}, u32[]{:S(2)}) collective-permute-start(f32[72,128]{1,0:T(8,128)S(1)} %add.36.mine), channel_id=1, source_target_pairs={{0,16},{1,17},{2,18},{3,19},{4,20},{5,21},{6,22},{7,23},{8,24},{9,... | collective-permute-start | bytes 110600 | tf_op jit(solution)/shard_map/ppermute | solution.py:382

commit v3 on v2

--- a/solution.py
+++ b/solution.py
@@ -43,9 +43,9 @@
     for ci in range(4):
         planes = jnp.concatenate(
             [
-                below[ci * 40 : ci * 40 + 40, :].astype(F32),
+                below[ci * HALO : ci * HALO + HALO].astype(F32).reshape(40, 256),
                 vol[ci].astype(F32).reshape(64, 256),
-                above[ci * 40 : ci * 40 + 40, :].astype(F32),
+                above[ci * HALO : ci * HALO + HALO].astype(F32).reshape(40, 256),
                 jnp.zeros((16, 256), F32),
             ],
             axis=0,
@@ -125,8 +125,9 @@
             lanes = slice(high * 128, high * 128 + 128)
             if plane in (0, 5):
                 outer = below if plane == 0 else above
-                row0, lane0 = 160 + high // 2 * 32, high % 2 * 128
-                target = outer[row0 : row0 + 32, lane0 : lane0 + 128].astype(F32)
+                block, lane0 = 20 + high // 2 * 4, high % 2 * 128
+                target = outer[block : block + 4, :, lane0 : lane0 + 128].astype(F32)
+                target = target.reshape(32, 128)
             else:
                 at = (plane - 1) * 4 + high
                 target = cot_all[pl.ds(at, 32, stride=16), :]
@@ -197,16 +198,28 @@
     grads[136:144, :] = jnp.where(lane < 32, shift_two[0:8], ones)
 
 
-def edges(vol, cot, upward, downward, cot_all):
-    cot_all[0:512, :] = cot[...].astype(F32)
-    for out, first, plane in ((upward, PLANES - HALO, 3), (downward, 0, 0)):
+def edges(vol, cot, upward, downward, cot_here, cot_all, sems):
+    moves = [pltpu.make_async_copy(cot, cot_here, sems.at[0])]
+    for side, (out, first) in enumerate(((upward, PLANES - HALO), (downward, 0))):
         for ci in range(4):
-            block = vol[ci, first : first + HALO].astype(F32).reshape(40, 256)
-            out[ci * 40 : ci * 40 + 40, :] = block.astype(BF16)
+            moves.append(
+                pltpu.make_async_copy(
+                    vol.at[ci, first : first + HALO],
+                    out.at[ci * HALO : ci * HALO + HALO],
+                    sems.at[1 + side * 4 + ci],
+                )
+            )
+    for move in moves:
+        move.start()
+    moves[0].wait()
+    cot_all[0:512, :] = cot_here[...].astype(F32)
+    for out, plane in ((upward, 3), (downward, 0)):
         for high in range(4):
-            row0, lane0 = 160 + high // 2 * 32, high % 2 * 128
+            block, lane0 = 20 + high // 2 * 4, high % 2 * 128
             tile = cot_all[pl.ds(plane * 4 + high, 32, stride=16), :]
-            out[row0 : row0 + 32, lane0 : lane0 + 128] = tile.astype(BF16)
+            out[block : block + 4, :, lane0 : lane0 + 128] = tile.reshape(4, 8, 128).astype(BF16)
+    for move in moves[1:]:
+        move.wait()
 
 
 def column(row, height):
@@ -302,10 +315,14 @@
 def run_edges(sample, target):
     return pl.pallas_call(
         edges,
-        out_shape=(jax.ShapeDtypeStruct((224, 256), BF16),) * 2,
-        in_specs=in_vmem(2),
+        out_shape=(jax.ShapeDtypeStruct((28, 8, 256), BF16),) * 2,
+        in_specs=[pl.BlockSpec(memory_space=pl.ANY)] * 2,
         out_specs=tuple(in_vmem(2)),
-        scratch_shapes=[pltpu.VMEM((528, 128), F32)],
+        scratch_shapes=[
+            pltpu.VMEM((512, 128), BF16),
+            pltpu.VMEM((528, 128), F32),
+            pltpu.SemaphoreType.DMA((9,)),
+        ],
         compiler_params=pltpu.CompilerParams(vmem_limit_bytes=4 << 20),
         name="edges",
     )(sample, target)
@@ -358,27 +375,31 @@
     def index_of(core, x, y, z):
         return ((z >> 2) * 8 + x * 2 + core) * 16 + (z & 3) * 4 + y
 
-    def pairing(which, mask):
+    def pairing(*masks):
         pairs = []
         for index in range(256):
-            spot = place(index)
-            spot[which] ^= mask
+            spot = [at ^ mask for at, mask in zip(place(index), masks)]
             pairs.append((index, index_of(*spot)))
         return pairs
 
-    core = pairing(0, 1)
-    others = [pairing(*step) for step in ((2, 1), (2, 2), (1, 1), (1, 2), (3, 1), (3, 2), (3, 7))]
-    return core, others
+    fours = (
+        (pairing(0, 0, 1, 0), pairing(0, 1, 0, 0), pairing(0, 1, 1, 0)),
+        (pairing(0, 0, 3, 0), pairing(0, 3, 0, 0), pairing(0, 3, 3, 0)),
+        (pairing(0, 0, 0, 1), pairing(0, 0, 0, 2), pairing(0, 0, 0, 3)),
+    )
+    return pairing(1, 0, 0, 0), fours, pairing(0, 0, 0, 7)
 
 
 def add_up(grads, core_index):
     axes = ("dp", "space")
-    core, others = device_exchanges()
+    core, fours, last = device_exchanges()
     low = core_index == 0
     top, bottom = grads[:72], grads[72:]
     mine = jnp.where(low, top, bottom) + lax.ppermute(jnp.where(low, bottom, top), axes, core)
-    for pairs in others:
-        mine = mine + lax.ppermute(mine, axes, pairs)
+    for first, second, third in fours:
+        one, two, three = (lax.ppermute(mine, axes, pairs) for pairs in (first, second, third))
+        mine = lax.optimization_barrier((mine + one) + (two + three))
+    mine = mine + lax.ppermute(mine, axes, last)
     return mine, lax.ppermute(mine, axes, core)
 
 

time: 58.8 us -> 57.2 us (0.973)
  starting transfers between devices: 33.3 us -> 29.8 us
  waiting for transfers between devices: 15.8 us -> 17.8 us
    ppermute x1, starting transfers between devices: 8.16 us -> 5.66 us  [add_up(): return (mine, lax.ppermute(mine, axes, core))]
    ppermute x7 -> x10, waiting for transfers between devices: 10.3 us -> 12.4 us  [the longest x9 11 us: add_up(): lax.ppermute(mine, axes, pairs)]
    ppermute x7 -> x10, starting transfers between devices: 17.5 us -> 16.5 us  [the longest x9 13.3 us: add_up(): lax.ppermute(mine, axes, pairs)]
  transfers between devices with their start and end apart: 11 -> 14, of which waited for: 10 -> 11; matrix products, arithmetic and copies ran while one was open for 0% -> 0% of each run, Pallas kernels for 1% -> 1%
where the time goes in v3:
time: 57.2 us; the launch traced here: 57.1 us
  starting transfers between devices  29.8 us (52%)
  waiting for transfers between devices  17.8 us (31%)
  Pallas kernels  6.69 us (12%)
  local copies, waits for them, and re-layouts  1.86 us (3%)
  between operations  0.79 us (1%)
    ppermute x9, starting transfers between devices, add_up(): lax.ppermute(mine, axes, pairs)  13.3 us
    ppermute x9, waiting for transfers between devices, add_up(): lax.ppermute(mine, axes, pairs)  11 us
    ppermute x1, starting transfers between devices, add_up(): return (mine, lax.ppermute(mine, axes, core))  5.66 us
    pallas_call x1, Pallas kernels, run_layers(): pl.pallas_call(layers, out_shape=(jax.ShapeDtypeStruct((512, 128), BF16),...  4.97 us
    ppermute x1, starting transfers between devices, shards(): below = lax.ppermute(upward, 'space', forward)  4.17 us
    ppermute x1, waiting for transfers between devices, shards(): above = lax.ppermute(downward, 'space', backward)  3.69 us
    ppermute x1, starting transfers between devices, add_up(): mine = mine + lax.ppermute(mine, axes, last)  3.2 us
    ppermute x1, starting transfers between devices, add_up(): lax.ppermute(jnp.where(low, bottom, top), axes, core)  2.19 us
  transfers between devices with their start and end apart: 14, of which 11 were waited for; matrix products, arithmetic and copies ran while one was open for 0% of the time, Pallas kernels for 1%

profile of v3, /device:TPU:1, one launch (start us, length us, event | category | flops | bytes accessed | tf_op | source)
XLA Modules:
  0.0 57.1 jit_solution(11865101903793349271)
XLA Ops:
  0.6 0.0 copy-start
  0.6 0.9 %copy-done = bf16[1,4,8,8,256]{4,3,2,1,0:T(8,128)(2,1)S(1)} copy-done((bf16[1,4,8,8,256]{4,3,2,1,0:T(8,128)(2,1)S(1)}, bf16[1,4,8,8,256]{4,3,2,1,0:T(8,128)(2,1)}, u32[]{:S(2)}) %copy-start) | copy-done | bytes 131096
  1.5 0.0 copy-start.2
  1.5 0.9 %copy-done.2 = bf16[1,32,4,4,128]{4,3,2,1,0:T(4,128)(2,1)S(1)} copy-done((bf16[1,32,4,4,128]{4,3,2,1,0:T(4,128)(2,1)S(1)}, bf16[1,32,4,4,128]{4,3,2,1,0:T(4,128)(2,1)}, u32[]{:S(2)}) %copy-start.2) | copy-done | bytes 131096
  2.4 0.0 copy-start.7
  2.4 0.0 copy-start.4
  2.4 0.0 copy-start.5
  2.5 0.5 edges.1
  3.0 0.0 copy-start.1
  3.0 0.0 copy-start.3
  3.0 4.2 %collective-permute-start = (bf16[28,8,256]{2,1,0:T(8,128)(2,1)S(1)}, bf16[28,8,256]{2,1,0:T(8,128)(2,1)S(1)}, u32[]{:S(2)}, u32[]{:S(2)}) collective-permute-start(bf16[28,8,256]{2,1,0:T(8,128)(2,1)S(1)} %get-tuple-element.20), channel_id=1, source_target_pairs={{0,1},{1,2},{2,3},{3,4},{4,5},{5,6},{6,7},{7,8},{8,9},{9,10},{10,1... | collective-permute-start | bytes 344072 | tf_op jit(solution)/shard_map/ppermute | solution.py:423
  7.2 1.3 %collective-permute-start.1 = (bf16[28,8,256]{2,1,0:T(8,128)(2,1)S(1)}, bf16[28,8,256]{2,1,0:T(8,128)(2,1)S(1)}, u32[]{:S(2)}, u32[]{:S(2)}) collective-permute-start(bf16[28,8,256]{2,1,0:T(8,128)(2,1)S(1)} %get-tuple-element.21), channel_id=1, source_target_pairs={{1,0},{2,1},{3,2},{4,3},{5,4},{6,5},{7,6},{8,7},{9,8},{10,9},{11,1... | collective-permute-start | bytes 344072 | tf_op jit(solution)/shard_map/ppermute | solution.py:424
  8.5 0.0 copy-done.7
  8.6 0.0 copy-done.4
  8.6 0.0 copy-done.5
  8.6 0.0 copy-done.6
  8.6 0.4 prepare.1
  9.0 0.1 add_convert_fusion.flags
  9.0 0.0 collective-permute-done.below
  9.1 3.7 %collective-permute-done.1.above = bf16[28,8,256]{2,1,0:T(8,128)(2,1)S(1)} collective-permute-done((bf16[28,8,256]{2,1,0:T(8,128)(2,1)S(1)}, bf16[28,8,256]{2,1,0:T(8,128)(2,1)S(1)}, u32[]{:S(2)}, u32[]{:S(2)}) %collective-permute-start.1) | collective-permute-done | bytes 114720 | tf_op jit(solution)/shard_map/ppermute | solution.py:424
  12.7 0.0 copy-done.1
  12.7 0.0 copy-done.3
  12.7 5.0 %layers.1 = (bf16[512,128]{1,0:T(8,128)(2,1)}, bf16[256,128]{1,0:T(8,128)(2,1)}, f32[144,128]{1,0:T(8,128)S(1)}) custom-call(f32[2]{0:T(128)S(1)} %add_convert_fusion.flags, bf16[4,8,8,256]{3,2,1,0:T(8,128)(2,1)S(1)} %bitcast.22, bf16[28,8,256]{2,1,0:T(8,128)(2,1)S(1)} %collective-permute-done.below, bf16[28,8,256]{2,1,0:T(8,128)(2,1)S(1)} %collective-permute-done.1.above, ...), custom_call_target="tpu_custom_call" | custom-call | tf_op jit(solution)/shard_map/layers/pallas_call | solution.py:288
  17.7 2.2 %collective-permute-start.2 = (f32[72,128]{1,0:T(8,128)S(1)}, f32[72,128]{1,0:T(8,128)S(1)}, u32[]{:S(2)}, u32[]{:S(2)}) collective-permute-start(f32[72,128]{1,0:T(8,128)S(1)} %slice_select_fusion), channel_id=1, source_target_pairs={{0,16},{1,17},{2,18},{3,19},{4,20},{5,21},{6,22},{7,23},{8,24},{9,... | collective-permute-start | bytes 110600 | tf_op jit(solution)/shard_map/ppermute | solution.py:398
  19.9 0.9 %collective-permute-done.2 = f32[72,128]{1,0:T(8,128)S(1)} collective-permute-done((f32[72,128]{1,0:T(8,128)S(1)}, f32[72,128]{1,0:T(8,128)S(1)}, u32[]{:S(2)}, u32[]{:S(2)}) %collective-permute-start.2) | collective-permute-done | bytes 36896 | tf_op jit(solution)/shard_map/ppermute | solution.py:398
  20.8 1.3 %collective-permute-start.4 = (f32[72,128]{1,0:T(8,128)S(1)}, f32[72,128]{1,0:T(8,128)S(1)}, u32[]{:S(2)}, u32[]{:S(2)}) collective-permute-start(f32[72,128]{1,0:T(8,128)S(1)} %select_add_fusion), channel_id=1, source_target_pairs={{0,32},{1,33},{2,34},{3,35},{4,36},{5,37},{6,38},{7,39},{8,40},{9,... | collective-permute-start | bytes 110600 | tf_op jit(solution)/shard_map/ppermute | solution.py:400
  22.1 1.2 %collective-permute-start.5 = (f32[72,128]{1,0:T(8,128)S(1)}, f32[72,128]{1,0:T(8,128)S(1)}, u32[]{:S(2)}, u32[]{:S(2)}) collective-permute-start(f32[72,128]{1,0:T(8,128)S(1)} %select_add_fusion), channel_id=1, source_target_pairs={{0,33},{1,32},{2,35},{3,34},{4,37},{5,36},{6,39},{7,38},{8,41},{9,... | collective-permute-start | bytes 110600 | tf_op jit(solution)/shard_map/ppermute | solution.py:400
  23.3 0.2 collective-permute-start.3
  23.5 0.2 collective-permute-done.4
  23.6 2.3 %collective-permute-done.5 = f32[72,128]{1,0:T(8,128)S(1)} collective-permute-done((f32[72,128]{1,0:T(8,128)S(1)}, f32[72,128]{1,0:T(8,128)S(1)}, u32[]{:S(2)}, u32[]{:S(2)}) %collective-permute-start.5) | collective-permute-done | bytes 36896 | tf_op jit(solution)/shard_map/ppermute | solution.py:400
  25.9 0.4 collective-permute-done.3
  26.3 2.8 %collective-permute-start.7 = (f32[72,128]{1,0:T(8,128)S(1)}, f32[72,128]{1,0:T(8,128)S(1)}, u32[]{:S(2)}, u32[]{:S(2)}) collective-permute-start(f32[72,128]{1,0:T(8,128)S(1)} %add_add_fusion.2), channel_id=1, source_target_pairs={{0,96},{1,97},{2,98},{3,99},{4,100},{5,101},{6,102},{7,103},{8,104... | collective-permute-start | bytes 110600 | tf_op jit(solution)/shard_map/ppermute | solution.py:400
  29.1 4.0 %collective-permute-start.8 = (f32[72,128]{1,0:T(8,128)S(1)}, f32[72,128]{1,0:T(8,128)S(1)}, u32[]{:S(2)}, u32[]{:S(2)}) collective-permute-start(f32[72,128]{1,0:T(8,128)S(1)} %add_add_fusion.2), channel_id=1, source_target_pairs={{0,99},{1,98},{2,97},{3,96},{4,103},{5,102},{6,101},{7,100},{8,107... | collective-permute-start | bytes 110600 | tf_op jit(solution)/shard_map/ppermute | solution.py:400
  33.1 0.0 collective-permute-start.6
  33.1 0.0 collective-permute-done.7
  33.1 2.1 %collective-permute-done.8 = f32[72,128]{1,0:T(8,128)S(1)} collective-permute-done((f32[72,128]{1,0:T(8,128)S(1)}, f32[72,128]{1,0:T(8,128)S(1)}, u32[]{:S(2)}, u32[]{:S(2)}) %collective-permute-start.8) | collective-permute-done | bytes 36896 | tf_op jit(solution)/shard_map/ppermute | solution.py:400
  35.2 2.2 %collective-permute-done.6 = f32[72,128]{1,0:T(8,128)S(1)} collective-permute-done((f32[72,128]{1,0:T(8,128)S(1)}, f32[72,128]{1,0:T(8,128)S(1)}, u32[]{:S(2)}, u32[]{:S(2)}) %collective-permute-start.6) | collective-permute-done | bytes 36896 | tf_op jit(solution)/shard_map/ppermute | solution.py:400
  37.4 3.1 %collective-permute-start.10 = (f32[72,128]{1,0:T(8,128)S(1)}, f32[72,128]{1,0:T(8,128)S(1)}, u32[]{:S(2)}, u32[]{:S(2)}) collective-permute-start(f32[72,128]{1,0:T(8,128)S(1)} %add_add_fusion.1), channel_id=1, source_target_pairs={{0,8},{1,9},{2,10},{3,11},{4,12},{5,13},{6,14},{7,15},{8,0},{9,1},... | collective-permute-start | bytes 110600 | tf_op jit(solution)/shard_map/ppermute | solution.py:400
  40.5 0.7 %collective-permute-start.11 = (f32[72,128]{1,0:T(8,128)S(1)}, f32[72,128]{1,0:T(8,128)S(1)}, u32[]{:S(2)}, u32[]{:S(2)}) collective-permute-start(f32[72,128]{1,0:T(8,128)S(1)} %add_add_fusion.1), channel_id=1, source_target_pairs={{0,12},{1,13},{2,14},{3,15},{4,8},{5,9},{6,10},{7,11},{8,4},{9,5},... | collective-permute-start | bytes 110600 | tf_op jit(solution)/shard_map/ppermute | solution.py:400
  41.2 0.0 collective-permute-start.9
  41.2 0.6 %collective-permute-done.10 = f32[72,128]{1,0:T(8,128)S(1)} collective-permute-done((f32[72,128]{1,0:T(8,128)S(1)}, f32[72,128]{1,0:T(8,128)S(1)}, u32[]{:S(2)}, u32[]{:S(2)}) %collective-permute-start.10) | collective-permute-done | bytes 36896 | tf_op jit(solution)/shard_map/ppermute | solution.py:400
  41.9 3.3 %collective-permute-done.11 = f32[72,128]{1,0:T(8,128)S(1)} collective-permute-done((f32[72,128]{1,0:T(8,128)S(1)}, f32[72,128]{1,0:T(8,128)S(1)}, u32[]{:S(2)}, u32[]{:S(2)}) %collective-permute-start.11) | collective-permute-done | bytes 36896 | tf_op jit(solution)/shard_map/ppermute | solution.py:400
  45.1 0.0 collective-permute-done.9
  45.2 3.2 %collective-permute-start.12 = (f32[72,128]{1,0:T(8,128)S(1)}, f32[72,128]{1,0:T(8,128)S(1)}, u32[]{:S(2)}, u32[]{:S(2)}) collective-permute-start(f32[72,128]{1,0:T(8,128)S(1)} %add_add_fusion), channel_id=1, source_target_pairs={{0,140},{1,141},{2,142},{3,143},{4,136},{5,137},{6,138},{7,139},{8... | collective-permute-start | bytes 110600 | tf_op jit(solution)/shard_map/ppermute | solution.py:402
  48.4 1.3 %collective-permute-done.12 = f32[72,128]{1,0:T(8,128)S(1)} collective-permute-done((f32[72,128]{1,0:T(8,128)S(1)}, f32[72,128]{1,0:T(8,128)S(1)}, u32[]{:S(2)}, u32[]{:S(2)}) %collective-permute-start.12) | collective-permute-done | bytes 36896 | tf_op jit(solution)/shard_map/ppermute | solution.py:402
  49.7 5.7 %collective-permute-start.13 = (f32[72,128]{1,0:T(8,128)S(1)}, f32[72,128]{1,0:T(8,128)S(1)}, u32[]{:S(2)}, u32[]{:S(2)}) collective-permute-start(f32[72,128]{1,0:T(8,128)S(1)} %add.48.mine), channel_id=1, source_target_pairs={{0,16},{1,17},{2,18},{3,19},{4,20},{5,21},{6,22},{7,23},{8,24},{9,... | collective-permute-start | bytes 110600 | tf_op jit(solution)/shard_map/ppermute | solution.py:403
  55.4 0.9 %collective-permute-done.13.other = f32[72,128]{1,0:T(8,128)S(1)} collective-permute-done((f32[72,128]{1,0:T(8,128)S(1)}, f32[72,128]{1,0:T(8,128)S(1)}, u32[]{:S(2)}, u32[]{:S(2)}) %collective-permute-start.13) | collective-permute-done | bytes 36896 | tf_op jit(solution)/shard_map/ppermute | solution.py:403
  56.3 0.8 %unpack.1 = (f32[27,4,16]{2,1,0:T(4,128)}, f32[1,16]{1,0:T(1,128)}, f32[27,16,32]{2,1,0:T(8,128)}, f32[1,32]{1,0:T(1,128)}) custom-call(s32[1]{0:T(128)} %bitcast.11.core, f32[72,128]{1,0:T(8,128)S(1)} %add.48.mine, f32[72,128]{1,0:T(8,128)S(1)} %collective-permute-done.13.other), custom_call_target="tpu_custom_call" | custom-call | tf_op jit(solution)/shard_map/unpack/pallas_call | solution.py:354
  (8 shorter events, 0.1 us)
Async XLA Ops:
  0.6 0.9 %copy-start = (bf16[1,4,8,8,256]{4,3,2,1,0:T(8,128)(2,1)S(1)}, bf16[1,4,8,8,256]{4,3,2,1,0:T(8,128)(2,1)}, u32[]{:S(2)}) copy-start(bf16[1,4,8,8,256]{4,3,2,1,0:T(8,128)(2,1)} %param.6) | copy-start | bytes 393220
  1.5 0.9 %copy-start.2 = (bf16[1,32,4,4,128]{4,3,2,1,0:T(4,128)(2,1)S(1)}, bf16[1,32,4,4,128]{4,3,2,1,0:T(4,128)(2,1)}, u32[]{:S(2)}) copy-start(bf16[1,32,4,4,128]{4,3,2,1,0:T(4,128)(2,1)} %param.11) | copy-start | bytes 393220
  2.4 6.1 %copy-start.7 = (bf16[16,4,3,3,3]{0,1,4,3,2:T(4,128)(2,1)S(1)}, bf16[16,4,3,3,3]{0,1,4,3,2:T(4,128)(2,1)}, u32[]{:S(2)}) copy-start(bf16[16,4,3,3,3]{0,1,4,3,2:T(4,128)(2,1)} %param.7) | copy-start | bytes 10372
  2.4 6.1 %copy-start.4 = (bf16[32,16,3,3,3]{0,1,4,3,2:T(8,128)(2,1)S(1)}, bf16[32,16,3,3,3]{0,1,4,3,2:T(8,128)(2,1)}, u32[]{:S(2)}) copy-start(bf16[32,16,3,3,3]{0,1,4,3,2:T(8,128)(2,1)} %param.9) | copy-start | bytes 82948
  2.4 6.1 %copy-start.5 = (f32[16]{0:T(128)S(1)}, f32[16]{0:T(128)}, u32[]{:S(2)}) copy-start(f32[16]{0:T(128)} %param.8) | copy-start | bytes 196
  2.5 6.1 %copy-start.6 = (f32[32]{0:T(128)S(1)}, f32[32]{0:T(128)}, u32[]{:S(2)}) copy-start(f32[32]{0:T(128)} %param.10) | copy-start | bytes 388
  3.0 9.7 %copy-start.1 = (bf16[1,4,8,8,256]{4,3,2,1,0:T(8,128)(2,1)S(1)}, bf16[1,4,8,8,256]{4,3,2,1,0:T(8,128)(2,1)}, u32[]{:S(2)}) copy-start(bf16[1,4,8,8,256]{4,3,2,1,0:T(8,128)(2,1)} %param.6) | copy-start | bytes 393220
  3.0 9.7 %copy-start.3 = (bf16[1,32,4,4,128]{4,3,2,1,0:T(4,128)(2,1)S(1)}, bf16[1,32,4,4,128]{4,3,2,1,0:T(4,128)(2,1)}, u32[]{:S(2)}) copy-start(bf16[1,32,4,4,128]{4,3,2,1,0:T(4,128)(2,1)} %param.11) | copy-start | bytes 393220
  3.0 6.0 %collective-permute-start = (bf16[28,8,256]{2,1,0:T(8,128)(2,1)S(1)}, bf16[28,8,256]{2,1,0:T(8,128)(2,1)S(1)}, u32[]{:S(2)}, u32[]{:S(2)}) collective-permute-start(bf16[28,8,256]{2,1,0:T(8,128)(2,1)S(1)} %get-tuple-element.20), channel_id=1, source_target_pairs={{0,1},{1,2},{2,3},{3,4},{4,5},{5,6},{6,7},{7,8},{8,9},{9,10},{10,1... | collective-permute-start | bytes 344072 | tf_op jit(solution)/shard_map/ppermute | solution.py:423
  7.2 5.5 %collective-permute-start.1 = (bf16[28,8,256]{2,1,0:T(8,128)(2,1)S(1)}, bf16[28,8,256]{2,1,0:T(8,128)(2,1)S(1)}, u32[]{:S(2)}, u32[]{:S(2)}) collective-permute-start(bf16[28,8,256]{2,1,0:T(8,128)(2,1)S(1)} %get-tuple-element.21), channel_id=1, source_target_pairs={{1,0},{2,1},{3,2},{4,3},{5,4},{6,5},{7,6},{8,7},{9,8},{10,9},{11,1... | collective-permute-start | bytes 344072 | tf_op jit(solution)/shard_map/ppermute | solution.py:424
  17.7 3.1 %collective-permute-start.2 = (f32[72,128]{1,0:T(8,128)S(1)}, f32[72,128]{1,0:T(8,128)S(1)}, u32[]{:S(2)}, u32[]{:S(2)}) collective-permute-start(f32[72,128]{1,0:T(8,128)S(1)} %slice_select_fusion), channel_id=1, source_target_pairs={{0,16},{1,17},{2,18},{3,19},{4,20},{5,21},{6,22},{7,23},{8,24},{9,... | collective-permute-start | bytes 110600 | tf_op jit(solution)/shard_map/ppermute | solution.py:398
  20.8 2.9 %collective-permute-start.4 = (f32[72,128]{1,0:T(8,128)S(1)}, f32[72,128]{1,0:T(8,128)S(1)}, u32[]{:S(2)}, u32[]{:S(2)}) collective-permute-start(f32[72,128]{1,0:T(8,128)S(1)} %select_add_fusion), channel_id=1, source_target_pairs={{0,32},{1,33},{2,34},{3,35},{4,36},{5,37},{6,38},{7,39},{8,40},{9,... | collective-permute-start | bytes 110600 | tf_op jit(solution)/shard_map/ppermute | solution.py:400
  22.1 3.9 %collective-permute-start.5 = (f32[72,128]{1,0:T(8,128)S(1)}, f32[72,128]{1,0:T(8,128)S(1)}, u32[]{:S(2)}, u32[]{:S(2)}) collective-permute-start(f32[72,128]{1,0:T(8,128)S(1)} %select_add_fusion), channel_id=1, source_target_pairs={{0,33},{1,32},{2,35},{3,34},{4,37},{5,36},{6,39},{7,38},{8,41},{9,... | collective-permute-start | bytes 110600 | tf_op jit(solution)/shard_map/ppermute | solution.py:400
  23.3 3.0 %collective-permute-start.3 = (f32[72,128]{1,0:T(8,128)S(1)}, f32[72,128]{1,0:T(8,128)S(1)}, u32[]{:S(2)}, u32[]{:S(2)}) collective-permute-start(f32[72,128]{1,0:T(8,128)S(1)} %select_add_fusion), channel_id=1, source_target_pairs={{0,1},{1,0},{2,3},{3,2},{4,5},{5,4},{6,7},{7,6},{8,9},{9,8},{10,11... | collective-permute-start | bytes 110600 | tf_op jit(solution)/shard_map/ppermute | solution.py:400
  26.3 6.8 %collective-permute-start.7 = (f32[72,128]{1,0:T(8,128)S(1)}, f32[72,128]{1,0:T(8,128)S(1)}, u32[]{:S(2)}, u32[]{:S(2)}) collective-permute-start(f32[72,128]{1,0:T(8,128)S(1)} %add_add_fusion.2), channel_id=1, source_target_pairs={{0,96},{1,97},{2,98},{3,99},{4,100},{5,101},{6,102},{7,103},{8,104... | collective-permute-start | bytes 110600 | tf_op jit(solution)/shard_map/ppermute | solution.py:400
  29.1 6.1 %collective-permute-start.8 = (f32[72,128]{1,0:T(8,128)S(1)}, f32[72,128]{1,0:T(8,128)S(1)}, u32[]{:S(2)}, u32[]{:S(2)}) collective-permute-start(f32[72,128]{1,0:T(8,128)S(1)} %add_add_fusion.2), channel_id=1, source_target_pairs={{0,99},{1,98},{2,97},{3,96},{4,103},{5,102},{6,101},{7,100},{8,107... | collective-permute-start | bytes 110600 | tf_op jit(solution)/shard_map/ppermute | solution.py:400
  33.1 4.3 %collective-permute-start.6 = (f32[72,128]{1,0:T(8,128)S(1)}, f32[72,128]{1,0:T(8,128)S(1)}, u32[]{:S(2)}, u32[]{:S(2)}) collective-permute-start(f32[72,128]{1,0:T(8,128)S(1)} %add_add_fusion.2), channel_id=1, source_target_pairs={{0,3},{1,2},{2,1},{3,0},{4,7},{5,6},{6,5},{7,4},{8,11},{9,10},{10,... | collective-permute-start | bytes 110600 | tf_op jit(solution)/shard_map/ppermute | solution.py:400
  37.4 4.4 %collective-permute-start.10 = (f32[72,128]{1,0:T(8,128)S(1)}, f32[72,128]{1,0:T(8,128)S(1)}, u32[]{:S(2)}, u32[]{:S(2)}) collective-permute-start(f32[72,128]{1,0:T(8,128)S(1)} %add_add_fusion.1), channel_id=1, source_target_pairs={{0,8},{1,9},{2,10},{3,11},{4,12},{5,13},{6,14},{7,15},{8,0},{9,1},... | collective-permute-start | bytes 110600 | tf_op jit(solution)/shard_map/ppermute | solution.py:400
  40.5 4.6 %collective-permute-start.11 = (f32[72,128]{1,0:T(8,128)S(1)}, f32[72,128]{1,0:T(8,128)S(1)}, u32[]{:S(2)}, u32[]{:S(2)}) collective-permute-start(f32[72,128]{1,0:T(8,128)S(1)} %add_add_fusion.1), channel_id=1, source_target_pairs={{0,12},{1,13},{2,14},{3,15},{4,8},{5,9},{6,10},{7,11},{8,4},{9,5},... | collective-permute-start | bytes 110600 | tf_op jit(solution)/shard_map/ppermute | solution.py:400
  41.2 3.9 %collective-permute-start.9 = (f32[72,128]{1,0:T(8,128)S(1)}, f32[72,128]{1,0:T(8,128)S(1)}, u32[]{:S(2)}, u32[]{:S(2)}) collective-permute-start(f32[72,128]{1,0:T(8,128)S(1)} %add_add_fusion.1), channel_id=1, source_target_pairs={{0,4},{1,5},{2,6},{3,7},{4,0},{5,1},{6,2},{7,3},{8,12},{9,13},{10,... | collective-permute-start | bytes 110600 | tf_op jit(solution)/shard_map/ppermute | solution.py:400
  45.2 4.6 %collective-permute-start.12 = (f32[72,128]{1,0:T(8,128)S(1)}, f32[72,128]{1,0:T(8,128)S(1)}, u32[]{:S(2)}, u32[]{:S(2)}) collective-permute-start(f32[72,128]{1,0:T(8,128)S(1)} %add_add_fusion), channel_id=1, source_target_pairs={{0,140},{1,141},{2,142},{3,143},{4,136},{5,137},{6,138},{7,139},{8... | collective-permute-start | bytes 110600 | tf_op jit(solution)/shard_map/ppermute | solution.py:402
  49.7 6.5 %collective-permute-start.13 = (f32[72,128]{1,0:T(8,128)S(1)}, f32[72,128]{1,0:T(8,128)S(1)}, u32[]{:S(2)}, u32[]{:S(2)}) collective-permute-start(f32[72,128]{1,0:T(8,128)S(1)} %add.48.mine), channel_id=1, source_target_pairs={{0,16},{1,17},{2,18},{3,19},{4,20},{5,21},{6,22},{7,23},{8,24},{9,... | collective-permute-start | bytes 110600 | tf_op jit(solution)/shard_map/ppermute | solution.py:403

commit v4 on v3

--- a/solution.py
+++ b/solution.py
@@ -32,8 +32,8 @@
 
 def layers(
     flags, vol, below, above, cot, w1, b1, w2, b2, w3,
-    act, pooled_grad, grads,
-    split, x1, x2, x3, slope, delta_one, cot_all, act_all, grad_all, band, thin,
+    act_out, pooled_grad_out, grads,
+    act, pooled_grad, sems, split, x1, x2, x3, slope, delta_one, cot_all, act_all, grad_all, band, thin,
 ):
     row = lax.broadcasted_iota(jnp.int32, (256, 512), 0)
     col = lax.broadcasted_iota(jnp.int32, (256, 512), 1)
@@ -81,11 +81,10 @@
         x2[base + 96 : base + 144, 384:512] = jnp.zeros((48, 128), BF16)
     weights_one = w1[...]
     bias_one = b1[...]
-    for group in range(4):
-        for high in range(4):
-            linear = plain_dot(
-                weights_one, x1[group * 144 : group * 144 + 288, high * 512 : high * 512 + 512]
-            )
+    for high in range(4):
+        everything = plain_dot(weights_one, x1[:, high * 512 : high * 512 + 512])
+        for group in range(4):
+            linear = everything[group * 64 : group * 64 + 64]
             linear = linear + bias_one
             positive = linear > 0
             if group in (1, 2):
@@ -116,8 +115,9 @@
         x3[base + 192 : base + 288, 384:512] = jnp.zeros((96, 128), BF16)
     weights_two = w2[...]
     bias_two = b2[...]
+    everything = plain_dot(weights_two, x2[...])
     for plane in range(6):
-        linear = plain_dot(weights_two, x2[plane * 144 : plane * 144 + 432, :]) + bias_two
+        linear = everything[plane * 32 : plane * 32 + 32] + bias_two
         positive = linear > 0
         factor = jnp.where(positive, 1.0, LEAK)
         leaky = jnp.where(positive, linear, LEAK * linear)
@@ -140,9 +140,11 @@
                         row0 = plane * 288 + (kh * 3 + kw) * 32
                         x3[row0 : row0 + 32, out_h * 128 : out_h * 128 + 128] = moved
     act[...] = act_all[0:512, :].astype(BF16)
-    weights_three = w3[:, 0:864]
+    act_move = pltpu.make_async_copy(act, act_out, sems.at[0])
+    act_move.start()
+    everything = plain_dot(w3[...], x3[...])
     for plane in range(4):
-        total = plain_dot(weights_three, x3[plane * 288 : plane * 288 + 864, :])
+        total = everything[plane * 16 : plane * 16 + 16]
         for high in range(4):
             tile = total[:, high * 128 : high * 128 + 128].astype(BF16).astype(F32)
             grad_all[pl.ds(plane * 4 + high, 16, stride=16), :] = tile
@@ -153,6 +155,8 @@
                         tile * slope[row0 : row0 + 16, lane0 : lane0 + 128]
                     ).astype(BF16)
     pooled_grad[...] = grad_all[0:256, :].astype(BF16)
+    pooled_grad_move = pltpu.make_async_copy(pooled_grad, pooled_grad_out, sems.at[1])
+    pooled_grad_move.start()
     second = jnp.zeros((432, 128), F32)
     shift_two = jnp.zeros((16, 128), F32)
     for plane in range(4):
@@ -196,6 +200,8 @@
     )
     ones = jnp.where((lane >= 32) & (lane < 48), pltpu.roll(ones, 32, 1), 0.0)
     grads[136:144, :] = jnp.where(lane < 32, shift_two[0:8], ones)
+    act_move.wait()
+    pooled_grad_move.wait()
 
 
 def edges(vol, cot, upward, downward, cot_here, cot_all, sems):
@@ -243,17 +249,28 @@
                 piece = wide_one[kd * 36 : kd * 36 + 36, :]
                 total = total + (pltpu.roll(piece, 16 * j, 1) if j else piece)
         bands[pl.ds(at // 4 * 144 + at % 4, 36, stride=4), :] = total
-    w1[...] = bands[...].T[0:64, 0:288].astype(BF16)
+    base = jnp.concatenate([bands[...].T[0:64], jnp.zeros((64, 384), F32)], axis=1)
+    for group in range(4):
+        moved = pltpu.roll(base, group * 144, 1) if group else base
+        w1[group * 64 : group * 64 + 64, :] = moved[:, 0:720].astype(BF16)
     wide_two[...] = jnp.zeros((512, 128), F32)
     wide_two[0:432, 0:32] = second[...].astype(F32)
-    w2[...] = wide_two[...].T[0:32, 0:432].astype(BF16)
+    base = jnp.concatenate([wide_two[...].T[0:32], jnp.zeros((32, 640), F32)], axis=1)
+    for plane in range(6):
+        moved = pltpu.roll(base, plane * 144, 1) if plane else base
+        w2[plane * 32 : plane * 32 + 32, :] = moved.astype(BF16)
+    quads = []
     for quad in range(7):
         total = wide_two[(26 - quad * 4) * 16 : (26 - quad * 4) * 16 + 16, :]
         for k in range(1, 4):
             tap = 26 - quad * 4 - k
             if tap >= 0:
                 total = total + pltpu.roll(wide_two[tap * 16 : tap * 16 + 16, :], 32 * k, 1)
-        w3[:, quad * 128 : quad * 128 + 128] = total.astype(BF16)
+        quads.append(total)
+    base = jnp.concatenate(quads + [jnp.zeros((16, 896), F32)], axis=1)
+    for plane in range(4):
+        moved = pltpu.roll(base, plane * 288, 1) if plane else base
+        w3[plane * 16 : plane * 16 + 16, :] = moved[:, 0:1728].astype(BF16)
 
 
 def unpack(scale_one, scale_two, core, mine, other, grad_one, shift_one, grad_two, shift_two, whole):
@@ -293,8 +310,15 @@
             jax.ShapeDtypeStruct((144, 128), F32),
         ),
         in_specs=[pl.BlockSpec(memory_space=pltpu.SMEM)] + in_vmem(len(arrays)),
-        out_specs=tuple(in_vmem(3)),
+        out_specs=(
+            pl.BlockSpec(memory_space=pl.ANY),
+            pl.BlockSpec(memory_space=pl.ANY),
+            pl.BlockSpec(memory_space=pltpu.VMEM),
+        ),
         scratch_shapes=[
+            pltpu.VMEM((512, 128), BF16),
+            pltpu.VMEM((256, 128), BF16),
+            pltpu.SemaphoreType.DMA((2,)),
             pltpu.VMEM((4, 648, 128), F32),
             pltpu.VMEM((720, 2048), BF16),
             pltpu.VMEM((1152, 512), BF16),
@@ -316,7 +340,7 @@
     return pl.pallas_call(
         edges,
         out_shape=(jax.ShapeDtypeStruct((28, 8, 256), BF16),) * 2,
-        in_specs=[pl.BlockSpec(memory_space=pl.ANY)] * 2,
+        in_specs=[pl.BlockSpec(memory_space=pltpu.HBM)] * 2,
         out_specs=tuple(in_vmem(2)),
         scratch_shapes=[
             pltpu.VMEM((512, 128), BF16),
@@ -325,18 +349,21 @@
         ],
         compiler_params=pltpu.CompilerParams(vmem_limit_bytes=4 << 20),
         name="edges",
-    )(sample, target)
+    )(
+        pltpu.with_memory_space_constraint(sample, pltpu.HBM),
+        pltpu.with_memory_space_constraint(target, pltpu.HBM),
+    )
 
 
 def run_prepare(*filters):
     return pl.pallas_call(
         prepare,
         out_shape=(
-            jax.ShapeDtypeStruct((64, 288), BF16),
+            jax.ShapeDtypeStruct((256, 720), BF16),
             jax.ShapeDtypeStruct((64, 1), F32),
-            jax.ShapeDtypeStruct((32, 432), BF16),
+            jax.ShapeDtypeStruct((192, 1152), BF16),
             jax.ShapeDtypeStruct((32, 1), F32),
-            jax.ShapeDtypeStruct((16, 896), BF16),
+            jax.ShapeDtypeStruct((64, 1728), BF16),
         ),
         in_specs=in_vmem(4),
         out_specs=tuple(in_vmem(5)),

time: 57.2 us -> 55.9 us (0.977)
  local copies, waits for them, and re-layouts: 1.86 us -> 0.06 us
  Pallas kernels: 6.69 us -> 7.29 us
    unnamed x16 -> x12, local copies, waits for them, and re-layouts: 1.83 us -> 0.03 us
    pallas_call x1, Pallas kernels: 0.54 us -> 1.12 us  [run_edges(): pl.pallas_call(edges, out_shape=(jax.ShapeDtypeStruct((28, 8, 256), BF16)...]
where the time goes in v4:
time: 55.9 us; the launch traced here: 55.7 us
  starting transfers between devices  29.8 us (53%)
  waiting for transfers between devices  17.6 us (31%)
  Pallas kernels  7.29 us (13%)
  between operations  0.82 us (1%)
    ppermute x9, starting transfers between devices, add_up(): lax.ppermute(mine, axes, pairs)  13.3 us
    ppermute x9, waiting for transfers between devices, add_up(): lax.ppermute(mine, axes, pairs)  11 us
    ppermute x1, starting transfers between devices, add_up(): return (mine, lax.ppermute(mine, axes, core))  5.62 us
    pallas_call x1, Pallas kernels, run_layers(): pl.pallas_call(layers, out_shape=(jax.ShapeDtypeStruct((512, 128), BF16),...  4.82 us
    ppermute x1, starting transfers between devices, shards(): below = lax.ppermute(upward, 'space', forward)  4.17 us
    ppermute x1, waiting for transfers between devices, shards(): above = lax.ppermute(downward, 'space', backward)  3.52 us
    ppermute x1, starting transfers between devices, add_up(): mine = mine + lax.ppermute(mine, axes, last)  3.26 us
    ppermute x1, starting transfers between devices, add_up(): lax.ppermute(jnp.where(low, bottom, top), axes, core)  2.19 us
  transfers between devices with their start and end apart: 14, of which 11 were waited for; matrix products, arithmetic and copies ran while one was open for 0% of the time, Pallas kernels for 1%

profile of v4, /device:TPU:1, one launch (start us, length us, event | category | flops | bytes accessed | tf_op | source)
XLA Modules:
  0.0 55.7 jit_solution(17743376017263524683)
XLA Ops:
  0.6 0.0 copy-start.5
  0.6 0.0 copy-start.2
  0.7 0.0 copy-start.3
  0.7 0.0 copy-start.4
  0.7 1.1 %edges.1 = (bf16[28,8,256]{2,1,0:T(8,128)(2,1)S(1)}, bf16[28,8,256]{2,1,0:T(8,128)(2,1)S(1)}) custom-call(bf16[4,8,8,256]{3,2,1,0:T(8,128)(2,1)} %bitcast.21, bf16[512,128]{1,0:T(8,128)(2,1)} %bitcast.23), custom_call_target="tpu_custom_call" | custom-call | tf_op jit(solution)/shard_map/edges/pallas_call | solution.py:340
  1.8 0.0 copy-start
  1.8 0.0 copy-start.1
  1.8 4.2 %collective-permute-start = (bf16[28,8,256]{2,1,0:T(8,128)(2,1)S(1)}, bf16[28,8,256]{2,1,0:T(8,128)(2,1)S(1)}, u32[]{:S(2)}, u32[]{:S(2)}) collective-permute-start(bf16[28,8,256]{2,1,0:T(8,128)(2,1)S(1)} %get-tuple-element.20), channel_id=1, source_target_pairs={{0,1},{1,2},{2,3},{3,4},{4,5},{5,6},{6,7},{7,8},{8,9},{9,10},{10,1... | collective-permute-start | bytes 344072 | tf_op jit(solution)/shard_map/ppermute | solution.py:450
  6.0 1.3 %collective-permute-start.1 = (bf16[28,8,256]{2,1,0:T(8,128)(2,1)S(1)}, bf16[28,8,256]{2,1,0:T(8,128)(2,1)S(1)}, u32[]{:S(2)}, u32[]{:S(2)}) collective-permute-start(bf16[28,8,256]{2,1,0:T(8,128)(2,1)S(1)} %get-tuple-element.21), channel_id=1, source_target_pairs={{1,0},{2,1},{3,2},{4,3},{5,4},{6,5},{7,6},{8,7},{9,8},{10,9},{11,1... | collective-permute-start | bytes 344072 | tf_op jit(solution)/shard_map/ppermute | solution.py:451
  7.3 0.0 copy-done.5
  7.4 0.0 copy-done.2
  7.4 0.0 copy-done.3
  7.4 0.0 copy-done.4
  7.4 0.5 prepare.1
  7.9 0.1 add_convert_fusion.flags
  8.0 0.0 collective-permute-done.below
  8.0 3.5 %collective-permute-done.1.above = bf16[28,8,256]{2,1,0:T(8,128)(2,1)S(1)} collective-permute-done((bf16[28,8,256]{2,1,0:T(8,128)(2,1)S(1)}, bf16[28,8,256]{2,1,0:T(8,128)(2,1)S(1)}, u32[]{:S(2)}, u32[]{:S(2)}) %collective-permute-start.1) | collective-permute-done | bytes 114720 | tf_op jit(solution)/shard_map/ppermute | solution.py:451
  11.5 0.0 copy-done
  11.5 0.0 copy-done.1
  11.5 4.8 %layers.1 = (bf16[512,128]{1,0:T(8,128)(2,1)}, bf16[256,128]{1,0:T(8,128)(2,1)}, f32[144,128]{1,0:T(8,128)S(1)}) custom-call(f32[2]{0:T(128)S(1)} %add_convert_fusion.flags, bf16[4,8,8,256]{3,2,1,0:T(8,128)(2,1)S(1)} %bitcast.22, bf16[28,8,256]{2,1,0:T(8,128)(2,1)S(1)} %collective-permute-done.below, bf16[28,8,256]{2,1,0:T(8,128)(2,1)S(1)} %collective-permute-done.1.above, ...), custom_call_target="tpu_custom_call" | custom-call | tf_op jit(solution)/shard_map/layers/pallas_call | solution.py:305
  16.4 2.2 %collective-permute-start.2 = (f32[72,128]{1,0:T(8,128)S(1)}, f32[72,128]{1,0:T(8,128)S(1)}, u32[]{:S(2)}, u32[]{:S(2)}) collective-permute-start(f32[72,128]{1,0:T(8,128)S(1)} %slice_select_fusion), channel_id=1, source_target_pairs={{0,16},{1,17},{2,18},{3,19},{4,20},{5,21},{6,22},{7,23},{8,24},{9,... | collective-permute-start | bytes 110600 | tf_op jit(solution)/shard_map/ppermute | solution.py:425
  18.6 0.9 %collective-permute-done.2 = f32[72,128]{1,0:T(8,128)S(1)} collective-permute-done((f32[72,128]{1,0:T(8,128)S(1)}, f32[72,128]{1,0:T(8,128)S(1)}, u32[]{:S(2)}, u32[]{:S(2)}) %collective-permute-start.2) | collective-permute-done | bytes 36896 | tf_op jit(solution)/shard_map/ppermute | solution.py:425
  19.5 1.3 %collective-permute-start.4 = (f32[72,128]{1,0:T(8,128)S(1)}, f32[72,128]{1,0:T(8,128)S(1)}, u32[]{:S(2)}, u32[]{:S(2)}) collective-permute-start(f32[72,128]{1,0:T(8,128)S(1)} %select_add_fusion), channel_id=1, source_target_pairs={{0,32},{1,33},{2,34},{3,35},{4,36},{5,37},{6,38},{7,39},{8,40},{9,... | collective-permute-start | bytes 110600 | tf_op jit(solution)/shard_map/ppermute | solution.py:427
  20.7 1.3 %collective-permute-start.5 = (f32[72,128]{1,0:T(8,128)S(1)}, f32[72,128]{1,0:T(8,128)S(1)}, u32[]{:S(2)}, u32[]{:S(2)}) collective-permute-start(f32[72,128]{1,0:T(8,128)S(1)} %select_add_fusion), channel_id=1, source_target_pairs={{0,33},{1,32},{2,35},{3,34},{4,37},{5,36},{6,39},{7,38},{8,41},{9,... | collective-permute-start | bytes 110600 | tf_op jit(solution)/shard_map/ppermute | solution.py:427
  22.0 0.2 collective-permute-start.3
  22.1 0.2 collective-permute-done.4
  22.3 2.3 %collective-permute-done.5 = f32[72,128]{1,0:T(8,128)S(1)} collective-permute-done((f32[72,128]{1,0:T(8,128)S(1)}, f32[72,128]{1,0:T(8,128)S(1)}, u32[]{:S(2)}, u32[]{:S(2)}) %collective-permute-start.5) | collective-permute-done | bytes 36896 | tf_op jit(solution)/shard_map/ppermute | solution.py:427
  24.6 0.4 collective-permute-done.3
  25.0 2.8 %collective-permute-start.7 = (f32[72,128]{1,0:T(8,128)S(1)}, f32[72,128]{1,0:T(8,128)S(1)}, u32[]{:S(2)}, u32[]{:S(2)}) collective-permute-start(f32[72,128]{1,0:T(8,128)S(1)} %add_add_fusion.2), channel_id=1, source_target_pairs={{0,96},{1,97},{2,98},{3,99},{4,100},{5,101},{6,102},{7,103},{8,104... | collective-permute-start | bytes 110600 | tf_op jit(solution)/shard_map/ppermute | solution.py:427
  27.8 4.0 %collective-permute-start.8 = (f32[72,128]{1,0:T(8,128)S(1)}, f32[72,128]{1,0:T(8,128)S(1)}, u32[]{:S(2)}, u32[]{:S(2)}) collective-permute-start(f32[72,128]{1,0:T(8,128)S(1)} %add_add_fusion.2), channel_id=1, source_target_pairs={{0,99},{1,98},{2,97},{3,96},{4,103},{5,102},{6,101},{7,100},{8,107... | collective-permute-start | bytes 110600 | tf_op jit(solution)/shard_map/ppermute | solution.py:427
  31.8 0.0 collective-permute-start.6
  31.8 0.0 collective-permute-done.7
  31.8 2.1 %collective-permute-done.8 = f32[72,128]{1,0:T(8,128)S(1)} collective-permute-done((f32[72,128]{1,0:T(8,128)S(1)}, f32[72,128]{1,0:T(8,128)S(1)}, u32[]{:S(2)}, u32[]{:S(2)}) %collective-permute-start.8) | collective-permute-done | bytes 36896 | tf_op jit(solution)/shard_map/ppermute | solution.py:427
  33.9 2.2 %collective-permute-done.6 = f32[72,128]{1,0:T(8,128)S(1)} collective-permute-done((f32[72,128]{1,0:T(8,128)S(1)}, f32[72,128]{1,0:T(8,128)S(1)}, u32[]{:S(2)}, u32[]{:S(2)}) %collective-permute-start.6) | collective-permute-done | bytes 36896 | tf_op jit(solution)/shard_map/ppermute | solution.py:427
  36.1 3.1 %collective-permute-start.10 = (f32[72,128]{1,0:T(8,128)S(1)}, f32[72,128]{1,0:T(8,128)S(1)}, u32[]{:S(2)}, u32[]{:S(2)}) collective-permute-start(f32[72,128]{1,0:T(8,128)S(1)} %add_add_fusion.1), channel_id=1, source_target_pairs={{0,8},{1,9},{2,10},{3,11},{4,12},{5,13},{6,14},{7,15},{8,0},{9,1},... | collective-permute-start | bytes 110600 | tf_op jit(solution)/shard_map/ppermute | solution.py:427
  39.2 0.7 %collective-permute-start.11 = (f32[72,128]{1,0:T(8,128)S(1)}, f32[72,128]{1,0:T(8,128)S(1)}, u32[]{:S(2)}, u32[]{:S(2)}) collective-permute-start(f32[72,128]{1,0:T(8,128)S(1)} %add_add_fusion.1), channel_id=1, source_target_pairs={{0,12},{1,13},{2,14},{3,15},{4,8},{5,9},{6,10},{7,11},{8,4},{9,5},... | collective-permute-start | bytes 110600 | tf_op jit(solution)/shard_map/ppermute | solution.py:427
  39.9 0.0 collective-permute-start.9
  39.9 0.6 %collective-permute-done.10 = f32[72,128]{1,0:T(8,128)S(1)} collective-permute-done((f32[72,128]{1,0:T(8,128)S(1)}, f32[72,128]{1,0:T(8,128)S(1)}, u32[]{:S(2)}, u32[]{:S(2)}) %collective-permute-start.10) | collective-permute-done | bytes 36896 | tf_op jit(solution)/shard_map/ppermute | solution.py:427
  40.5 3.3 %collective-permute-done.11 = f32[72,128]{1,0:T(8,128)S(1)} collective-permute-done((f32[72,128]{1,0:T(8,128)S(1)}, f32[72,128]{1,0:T(8,128)S(1)}, u32[]{:S(2)}, u32[]{:S(2)}) %collective-permute-start.11) | collective-permute-done | bytes 36896 | tf_op jit(solution)/shard_map/ppermute | solution.py:427
  43.8 0.0 collective-permute-done.9
  43.8 3.3 %collective-permute-start.12 = (f32[72,128]{1,0:T(8,128)S(1)}, f32[72,128]{1,0:T(8,128)S(1)}, u32[]{:S(2)}, u32[]{:S(2)}) collective-permute-start(f32[72,128]{1,0:T(8,128)S(1)} %add_add_fusion), channel_id=1, source_target_pairs={{0,140},{1,141},{2,142},{3,143},{4,136},{5,137},{6,138},{7,139},{8... | collective-permute-start | bytes 110600 | tf_op jit(solution)/shard_map/ppermute | solution.py:429
  47.1 1.3 %collective-permute-done.12 = f32[72,128]{1,0:T(8,128)S(1)} collective-permute-done((f32[72,128]{1,0:T(8,128)S(1)}, f32[72,128]{1,0:T(8,128)S(1)}, u32[]{:S(2)}, u32[]{:S(2)}) %collective-permute-start.12) | collective-permute-done | bytes 36896 | tf_op jit(solution)/shard_map/ppermute | solution.py:429
  48.4 5.6 %collective-permute-start.13 = (f32[72,128]{1,0:T(8,128)S(1)}, f32[72,128]{1,0:T(8,128)S(1)}, u32[]{:S(2)}, u32[]{:S(2)}) collective-permute-start(f32[72,128]{1,0:T(8,128)S(1)} %add.48.mine), channel_id=1, source_target_pairs={{0,16},{1,17},{2,18},{3,19},{4,20},{5,21},{6,22},{7,23},{8,24},{9,... | collective-permute-start | bytes 110600 | tf_op jit(solution)/shard_map/ppermute | solution.py:430
  54.1 0.9 %collective-permute-done.13.other = f32[72,128]{1,0:T(8,128)S(1)} collective-permute-done((f32[72,128]{1,0:T(8,128)S(1)}, f32[72,128]{1,0:T(8,128)S(1)}, u32[]{:S(2)}, u32[]{:S(2)}) %collective-permute-start.13) | collective-permute-done | bytes 36896 | tf_op jit(solution)/shard_map/ppermute | solution.py:430
  54.9 0.8 %unpack.1 = (f32[27,4,16]{2,1,0:T(4,128)}, f32[1,16]{1,0:T(1,128)}, f32[27,16,32]{2,1,0:T(8,128)}, f32[1,32]{1,0:T(1,128)}) custom-call(s32[1]{0:T(128)} %bitcast.11.core, f32[72,128]{1,0:T(8,128)S(1)} %add.48.mine, f32[72,128]{1,0:T(8,128)S(1)} %collective-permute-done.13.other), custom_call_target="tpu_custom_call" | custom-call | tf_op jit(solution)/shard_map/unpack/pallas_call | solution.py:381
  (7 shorter events, 0.1 us)
Async XLA Ops:
  0.6 6.7 %copy-start.5 = (bf16[16,4,3,3,3]{0,1,4,3,2:T(4,128)(2,1)S(1)}, bf16[16,4,3,3,3]{0,1,4,3,2:T(4,128)(2,1)}, u32[]{:S(2)}) copy-start(bf16[16,4,3,3,3]{0,1,4,3,2:T(4,128)(2,1)} %param.7) | copy-start | bytes 10372
  0.6 6.7 %copy-start.2 = (bf16[32,16,3,3,3]{0,1,4,3,2:T(8,128)(2,1)S(1)}, bf16[32,16,3,3,3]{0,1,4,3,2:T(8,128)(2,1)}, u32[]{:S(2)}) copy-start(bf16[32,16,3,3,3]{0,1,4,3,2:T(8,128)(2,1)} %param.9) | copy-start | bytes 82948
  0.7 6.7 %copy-start.3 = (f32[16]{0:T(128)S(1)}, f32[16]{0:T(128)}, u32[]{:S(2)}) copy-start(f32[16]{0:T(128)} %param.8) | copy-start | bytes 196
  0.7 6.7 %copy-start.4 = (f32[32]{0:T(128)S(1)}, f32[32]{0:T(128)}, u32[]{:S(2)}) copy-start(f32[32]{0:T(128)} %param.10) | copy-start | bytes 388
  1.8 9.7 %copy-start = (bf16[1,4,8,8,256]{4,3,2,1,0:T(8,128)(2,1)S(1)}, bf16[1,4,8,8,256]{4,3,2,1,0:T(8,128)(2,1)}, u32[]{:S(2)}) copy-start(bf16[1,4,8,8,256]{4,3,2,1,0:T(8,128)(2,1)} %param.6) | copy-start | bytes 393220
  1.8 9.7 %copy-start.1 = (bf16[1,32,4,4,128]{4,3,2,1,0:T(4,128)(2,1)S(1)}, bf16[1,32,4,4,128]{4,3,2,1,0:T(4,128)(2,1)}, u32[]{:S(2)}) copy-start(bf16[1,32,4,4,128]{4,3,2,1,0:T(4,128)(2,1)} %param.11) | copy-start | bytes 393220
  1.8 6.2 %collective-permute-start = (bf16[28,8,256]{2,1,0:T(8,128)(2,1)S(1)}, bf16[28,8,256]{2,1,0:T(8,128)(2,1)S(1)}, u32[]{:S(2)}, u32[]{:S(2)}) collective-permute-start(bf16[28,8,256]{2,1,0:T(8,128)(2,1)S(1)} %get-tuple-element.20), channel_id=1, source_target_pairs={{0,1},{1,2},{2,3},{3,4},{4,5},{5,6},{6,7},{7,8},{8,9},{9,10},{10,1... | collective-permute-start | bytes 344072 | tf_op jit(solution)/shard_map/ppermute | solution.py:450
  6.0 5.5 %collective-permute-start.1 = (bf16[28,8,256]{2,1,0:T(8,128)(2,1)S(1)}, bf16[28,8,256]{2,1,0:T(8,128)(2,1)S(1)}, u32[]{:S(2)}, u32[]{:S(2)}) collective-permute-start(bf16[28,8,256]{2,1,0:T(8,128)(2,1)S(1)} %get-tuple-element.21), channel_id=1, source_target_pairs={{1,0},{2,1},{3,2},{4,3},{5,4},{6,5},{7,6},{8,7},{9,8},{10,9},{11,1... | collective-permute-start | bytes 344072 | tf_op jit(solution)/shard_map/ppermute | solution.py:451
  16.4 3.1 %collective-permute-start.2 = (f32[72,128]{1,0:T(8,128)S(1)}, f32[72,128]{1,0:T(8,128)S(1)}, u32[]{:S(2)}, u32[]{:S(2)}) collective-permute-start(f32[72,128]{1,0:T(8,128)S(1)} %slice_select_fusion), channel_id=1, source_target_pairs={{0,16},{1,17},{2,18},{3,19},{4,20},{5,21},{6,22},{7,23},{8,24},{9,... | collective-permute-start | bytes 110600 | tf_op jit(solution)/shard_map/ppermute | solution.py:425
  19.5 2.9 %collective-permute-start.4 = (f32[72,128]{1,0:T(8,128)S(1)}, f32[72,128]{1,0:T(8,128)S(1)}, u32[]{:S(2)}, u32[]{:S(2)}) collective-permute-start(f32[72,128]{1,0:T(8,128)S(1)} %select_add_fusion), channel_id=1, source_target_pairs={{0,32},{1,33},{2,34},{3,35},{4,36},{5,37},{6,38},{7,39},{8,40},{9,... | collective-permute-start | bytes 110600 | tf_op jit(solution)/shard_map/ppermute | solution.py:427
  20.7 3.9 %collective-permute-start.5 = (f32[72,128]{1,0:T(8,128)S(1)}, f32[72,128]{1,0:T(8,128)S(1)}, u32[]{:S(2)}, u32[]{:S(2)}) collective-permute-start(f32[72,128]{1,0:T(8,128)S(1)} %select_add_fusion), channel_id=1, source_target_pairs={{0,33},{1,32},{2,35},{3,34},{4,37},{5,36},{6,39},{7,38},{8,41},{9,... | collective-permute-start | bytes 110600 | tf_op jit(solution)/shard_map/ppermute | solution.py:427
  22.0 3.0 %collective-permute-start.3 = (f32[72,128]{1,0:T(8,128)S(1)}, f32[72,128]{1,0:T(8,128)S(1)}, u32[]{:S(2)}, u32[]{:S(2)}) collective-permute-start(f32[72,128]{1,0:T(8,128)S(1)} %select_add_fusion), channel_id=1, source_target_pairs={{0,1},{1,0},{2,3},{3,2},{4,5},{5,4},{6,7},{7,6},{8,9},{9,8},{10,11... | collective-permute-start | bytes 110600 | tf_op jit(solution)/shard_map/ppermute | solution.py:427
  25.0 6.8 %collective-permute-start.7 = (f32[72,128]{1,0:T(8,128)S(1)}, f32[72,128]{1,0:T(8,128)S(1)}, u32[]{:S(2)}, u32[]{:S(2)}) collective-permute-start(f32[72,128]{1,0:T(8,128)S(1)} %add_add_fusion.2), channel_id=1, source_target_pairs={{0,96},{1,97},{2,98},{3,99},{4,100},{5,101},{6,102},{7,103},{8,104... | collective-permute-start | bytes 110600 | tf_op jit(solution)/shard_map/ppermute | solution.py:427
  27.8 6.1 %collective-permute-start.8 = (f32[72,128]{1,0:T(8,128)S(1)}, f32[72,128]{1,0:T(8,128)S(1)}, u32[]{:S(2)}, u32[]{:S(2)}) collective-permute-start(f32[72,128]{1,0:T(8,128)S(1)} %add_add_fusion.2), channel_id=1, source_target_pairs={{0,99},{1,98},{2,97},{3,96},{4,103},{5,102},{6,101},{7,100},{8,107... | collective-permute-start | bytes 110600 | tf_op jit(solution)/shard_map/ppermute | solution.py:427
  31.8 4.3 %collective-permute-start.6 = (f32[72,128]{1,0:T(8,128)S(1)}, f32[72,128]{1,0:T(8,128)S(1)}, u32[]{:S(2)}, u32[]{:S(2)}) collective-permute-start(f32[72,128]{1,0:T(8,128)S(1)} %add_add_fusion.2), channel_id=1, source_target_pairs={{0,3},{1,2},{2,1},{3,0},{4,7},{5,6},{6,5},{7,4},{8,11},{9,10},{10,... | collective-permute-start | bytes 110600 | tf_op jit(solution)/shard_map/ppermute | solution.py:427
  36.1 4.4 %collective-permute-start.10 = (f32[72,128]{1,0:T(8,128)S(1)}, f32[72,128]{1,0:T(8,128)S(1)}, u32[]{:S(2)}, u32[]{:S(2)}) collective-permute-start(f32[72,128]{1,0:T(8,128)S(1)} %add_add_fusion.1), channel_id=1, source_target_pairs={{0,8},{1,9},{2,10},{3,11},{4,12},{5,13},{6,14},{7,15},{8,0},{9,1},... | collective-permute-start | bytes 110600 | tf_op jit(solution)/shard_map/ppermute | solution.py:427
  39.2 4.6 %collective-permute-start.11 = (f32[72,128]{1,0:T(8,128)S(1)}, f32[72,128]{1,0:T(8,128)S(1)}, u32[]{:S(2)}, u32[]{:S(2)}) collective-permute-start(f32[72,128]{1,0:T(8,128)S(1)} %add_add_fusion.1), channel_id=1, source_target_pairs={{0,12},{1,13},{2,14},{3,15},{4,8},{5,9},{6,10},{7,11},{8,4},{9,5},... | collective-permute-start | bytes 110600 | tf_op jit(solution)/shard_map/ppermute | solution.py:427
  39.9 3.9 %collective-permute-start.9 = (f32[72,128]{1,0:T(8,128)S(1)}, f32[72,128]{1,0:T(8,128)S(1)}, u32[]{:S(2)}, u32[]{:S(2)}) collective-permute-start(f32[72,128]{1,0:T(8,128)S(1)} %add_add_fusion.1), channel_id=1, source_target_pairs={{0,4},{1,5},{2,6},{3,7},{4,0},{5,1},{6,2},{7,3},{8,12},{9,13},{10,... | collective-permute-start | bytes 110600 | tf_op jit(solution)/shard_map/ppermute | solution.py:427
  43.8 4.6 %collective-permute-start.12 = (f32[72,128]{1,0:T(8,128)S(1)}, f32[72,128]{1,0:T(8,128)S(1)}, u32[]{:S(2)}, u32[]{:S(2)}) collective-permute-start(f32[72,128]{1,0:T(8,128)S(1)} %add_add_fusion), channel_id=1, source_target_pairs={{0,140},{1,141},{2,142},{3,143},{4,136},{5,137},{6,138},{7,139},{8... | collective-permute-start | bytes 110600 | tf_op jit(solution)/shard_map/ppermute | solution.py:429
  48.4 6.5 %collective-permute-start.13 = (f32[72,128]{1,0:T(8,128)S(1)}, f32[72,128]{1,0:T(8,128)S(1)}, u32[]{:S(2)}, u32[]{:S(2)}) collective-permute-start(f32[72,128]{1,0:T(8,128)S(1)} %add.48.mine), channel_id=1, source_target_pairs={{0,16},{1,17},{2,18},{3,19},{4,20},{5,21},{6,22},{7,23},{8,24},{9,... | collective-permute-start | bytes 110600 | tf_op jit(solution)/shard_map/ppermute | solution.py:430

commit v5 on v4

--- a/solution.py
+++ b/solution.py
@@ -171,20 +171,14 @@
     )
     grads[0:96, :] = three[0:96] + pltpu.roll(second[336:432], 96, 1)
     grads[96:112, :] = three[96:112]
-    first = jnp.zeros((288, 128), F32)
-    shift_one = jnp.zeros((16, 128), F32)
-    for group in (1, 2):
-        delta = jnp.concatenate(
-            [delta_one[(group - 1) * 64 : group * 64, :], jnp.zeros((64, 2048), BF16)], axis=0
-        )
-        first = first + lanes_dot(x1[group * 144 : group * 144 + 288, :], delta)
-        shift_one = shift_one + lanes_dot(jnp.ones((16, 2048), BF16), delta)
-    band[0:288, :] = first
+    delta = delta_one[...]
+    band[0:432, :] = lanes_dot(x1[144:576, :], delta)
+    shift_one = lanes_dot(jnp.ones((16, 2048), BF16), delta)
     lane36 = lax.broadcasted_iota(jnp.int32, (36, 128), 1)
     packed = jnp.zeros((36, 128), F32)
     for kd in range(3):
         total = jnp.zeros((36, 128), F32)
-        for plane in range(4):
+        for plane in range(8):
             at = (plane + kd) // 4 * 144 + (plane + kd) % 4
             piece = band[pl.ds(at, 36, stride=4), :]
             lane0 = (128 + 16 * (kd - plane)) % 128
@@ -195,10 +189,9 @@
     grads[112:136, :] = thin[0:24, :] + pltpu.roll(thin[24:48, :], 48, 1)
     lane = lax.broadcasted_iota(jnp.int32, (8, 128), 1)
     ones = shift_one[0:8]
-    ones = (
-        ones + pltpu.roll(ones, 112, 1) + pltpu.roll(ones, 96, 1) + pltpu.roll(ones, 80, 1)
-    )
-    ones = jnp.where((lane >= 32) & (lane < 48), pltpu.roll(ones, 32, 1), 0.0)
+    for shift in (64, 32, 16):
+        ones = ones + pltpu.roll(ones, shift, 1)
+    ones = jnp.where((lane >= 32) & (lane < 48), ones, 0.0)
     grads[136:144, :] = jnp.where(lane < 32, shift_two[0:8], ones)
     act_move.wait()
     pooled_grad_move.wait()
@@ -328,7 +321,7 @@
             pltpu.VMEM((528, 128), F32),
             pltpu.VMEM((528, 128), F32),
             pltpu.VMEM((272, 128), F32),
-            pltpu.VMEM((304, 128), F32),
+            pltpu.VMEM((448, 128), F32),
             pltpu.VMEM((48, 128), F32),
         ],
         compiler_params=pltpu.CompilerParams(vmem_limit_bytes=24 << 20),

time: 55.9 us -> 56.3 us (level)
  no operation moved by 1% of the time
where the time goes in v5:
time: 56.3 us; the launch traced here: 56.2 us
  starting transfers between devices  29.8 us (53%)
  waiting for transfers between devices  17.6 us (31%)
  Pallas kernels  7.74 us (14%)
  between operations  0.82 us (1%)
    ppermute x9, starting transfers between devices, add_up(): lax.ppermute(mine, axes, pairs)  13.3 us
    ppermute x9, waiting for transfers between devices, add_up(): lax.ppermute(mine, axes, pairs)  11 us
    ppermute x1, starting transfers between devices, add_up(): return (mine, lax.ppermute(mine, axes, core))  5.57 us
    pallas_call x1, Pallas kernels, run_layers(): pl.pallas_call(layers, out_shape=(jax.ShapeDtypeStruct((512, 128), BF16),...  5.27 us
    ppermute x1, starting transfers between devices, shards(): below = lax.ppermute(upward, 'space', forward)  4.17 us
    ppermute x1, waiting for transfers between devices, shards(): above = lax.ppermute(downward, 'space', backward)  3.52 us
    ppermute x1, starting transfers between devices, add_up(): mine = mine + lax.ppermute(mine, axes, last)  3.31 us
    ppermute x1, starting transfers between devices, add_up(): lax.ppermute(jnp.where(low, bottom, top), axes, core)  2.19 us
  transfers between devices with their start and end apart: 14, of which 11 were waited for; matrix products, arithmetic and copies ran while one was open for 0% of the time, Pallas kernels for 1%

profile of v5, /device:TPU:1, one launch (start us, length us, event | category | flops | bytes accessed | tf_op | source)
XLA Modules:
  0.0 56.2 jit_solution(13835222024677245545)
XLA Ops:
  0.6 0.0 copy-start.5
  0.6 0.0 copy-start.2
  0.7 0.0 copy-start.3
  0.7 0.0 copy-start.4
  0.7 1.1 %edges.1 = (bf16[28,8,256]{2,1,0:T(8,128)(2,1)S(1)}, bf16[28,8,256]{2,1,0:T(8,128)(2,1)S(1)}) custom-call(bf16[4,8,8,256]{3,2,1,0:T(8,128)(2,1)} %bitcast.21, bf16[512,128]{1,0:T(8,128)(2,1)} %bitcast.23), custom_call_target="tpu_custom_call" | custom-call | tf_op jit(solution)/shard_map/edges/pallas_call | solution.py:333
  1.8 0.0 copy-start
  1.8 0.0 copy-start.1
  1.8 4.2 %collective-permute-start = (bf16[28,8,256]{2,1,0:T(8,128)(2,1)S(1)}, bf16[28,8,256]{2,1,0:T(8,128)(2,1)S(1)}, u32[]{:S(2)}, u32[]{:S(2)}) collective-permute-start(bf16[28,8,256]{2,1,0:T(8,128)(2,1)S(1)} %get-tuple-element.20), channel_id=1, source_target_pairs={{0,1},{1,2},{2,3},{3,4},{4,5},{5,6},{6,7},{7,8},{8,9},{9,10},{10,1... | collective-permute-start | bytes 344072 | tf_op jit(solution)/shard_map/ppermute | solution.py:443
  6.0 1.3 %collective-permute-start.1 = (bf16[28,8,256]{2,1,0:T(8,128)(2,1)S(1)}, bf16[28,8,256]{2,1,0:T(8,128)(2,1)S(1)}, u32[]{:S(2)}, u32[]{:S(2)}) collective-permute-start(bf16[28,8,256]{2,1,0:T(8,128)(2,1)S(1)} %get-tuple-element.21), channel_id=1, source_target_pairs={{1,0},{2,1},{3,2},{4,3},{5,4},{6,5},{7,6},{8,7},{9,8},{10,9},{11,1... | collective-permute-start | bytes 344072 | tf_op jit(solution)/shard_map/ppermute | solution.py:444
  7.3 0.0 copy-done.5
  7.4 0.0 copy-done.2
  7.4 0.0 copy-done.3
  7.4 0.0 copy-done.4
  7.4 0.5 prepare.1
  7.9 0.1 add_convert_fusion.flags
  8.0 0.0 collective-permute-done.below
  8.0 3.5 %collective-permute-done.1.above = bf16[28,8,256]{2,1,0:T(8,128)(2,1)S(1)} collective-permute-done((bf16[28,8,256]{2,1,0:T(8,128)(2,1)S(1)}, bf16[28,8,256]{2,1,0:T(8,128)(2,1)S(1)}, u32[]{:S(2)}, u32[]{:S(2)}) %collective-permute-start.1) | collective-permute-done | bytes 114720 | tf_op jit(solution)/shard_map/ppermute | solution.py:444
  11.5 0.0 copy-done
  11.5 0.0 copy-done.1
  11.5 5.3 %layers.1 = (bf16[512,128]{1,0:T(8,128)(2,1)}, bf16[256,128]{1,0:T(8,128)(2,1)}, f32[144,128]{1,0:T(8,128)S(1)}) custom-call(f32[2]{0:T(128)S(1)} %add_convert_fusion.flags, bf16[4,8,8,256]{3,2,1,0:T(8,128)(2,1)S(1)} %bitcast.22, bf16[28,8,256]{2,1,0:T(8,128)(2,1)S(1)} %collective-permute-done.below, bf16[28,8,256]{2,1,0:T(8,128)(2,1)S(1)} %collective-permute-done.1.above, ...), custom_call_target="tpu_custom_call" | custom-call | tf_op jit(solution)/shard_map/layers/pallas_call | solution.py:298
  16.8 2.2 %collective-permute-start.2 = (f32[72,128]{1,0:T(8,128)S(1)}, f32[72,128]{1,0:T(8,128)S(1)}, u32[]{:S(2)}, u32[]{:S(2)}) collective-permute-start(f32[72,128]{1,0:T(8,128)S(1)} %slice_select_fusion), channel_id=1, source_target_pairs={{0,16},{1,17},{2,18},{3,19},{4,20},{5,21},{6,22},{7,23},{8,24},{9,... | collective-permute-start | bytes 110600 | tf_op jit(solution)/shard_map/ppermute | solution.py:418
  19.0 0.9 %collective-permute-done.2 = f32[72,128]{1,0:T(8,128)S(1)} collective-permute-done((f32[72,128]{1,0:T(8,128)S(1)}, f32[72,128]{1,0:T(8,128)S(1)}, u32[]{:S(2)}, u32[]{:S(2)}) %collective-permute-start.2) | collective-permute-done | bytes 36896 | tf_op jit(solution)/shard_map/ppermute | solution.py:418
  19.9 1.3 %collective-permute-start.4 = (f32[72,128]{1,0:T(8,128)S(1)}, f32[72,128]{1,0:T(8,128)S(1)}, u32[]{:S(2)}, u32[]{:S(2)}) collective-permute-start(f32[72,128]{1,0:T(8,128)S(1)} %select_add_fusion), channel_id=1, source_target_pairs={{0,32},{1,33},{2,34},{3,35},{4,36},{5,37},{6,38},{7,39},{8,40},{9,... | collective-permute-start | bytes 110600 | tf_op jit(solution)/shard_map/ppermute | solution.py:420
  21.2 1.3 %collective-permute-start.5 = (f32[72,128]{1,0:T(8,128)S(1)}, f32[72,128]{1,0:T(8,128)S(1)}, u32[]{:S(2)}, u32[]{:S(2)}) collective-permute-start(f32[72,128]{1,0:T(8,128)S(1)} %select_add_fusion), channel_id=1, source_target_pairs={{0,33},{1,32},{2,35},{3,34},{4,37},{5,36},{6,39},{7,38},{8,41},{9,... | collective-permute-start | bytes 110600 | tf_op jit(solution)/shard_map/ppermute | solution.py:420
  22.4 0.2 collective-permute-start.3
  22.6 0.2 collective-permute-done.4
  22.8 2.3 %collective-permute-done.5 = f32[72,128]{1,0:T(8,128)S(1)} collective-permute-done((f32[72,128]{1,0:T(8,128)S(1)}, f32[72,128]{1,0:T(8,128)S(1)}, u32[]{:S(2)}, u32[]{:S(2)}) %collective-permute-start.5) | collective-permute-done | bytes 36896 | tf_op jit(solution)/shard_map/ppermute | solution.py:420
  25.0 0.4 collective-permute-done.3
  25.4 2.8 %collective-permute-start.7 = (f32[72,128]{1,0:T(8,128)S(1)}, f32[72,128]{1,0:T(8,128)S(1)}, u32[]{:S(2)}, u32[]{:S(2)}) collective-permute-start(f32[72,128]{1,0:T(8,128)S(1)} %add_add_fusion.2), channel_id=1, source_target_pairs={{0,96},{1,97},{2,98},{3,99},{4,100},{5,101},{6,102},{7,103},{8,104... | collective-permute-start | bytes 110600 | tf_op jit(solution)/shard_map/ppermute | solution.py:420
  28.2 4.0 %collective-permute-start.8 = (f32[72,128]{1,0:T(8,128)S(1)}, f32[72,128]{1,0:T(8,128)S(1)}, u32[]{:S(2)}, u32[]{:S(2)}) collective-permute-start(f32[72,128]{1,0:T(8,128)S(1)} %add_add_fusion.2), channel_id=1, source_target_pairs={{0,99},{1,98},{2,97},{3,96},{4,103},{5,102},{6,101},{7,100},{8,107... | collective-permute-start | bytes 110600 | tf_op jit(solution)/shard_map/ppermute | solution.py:420
  32.2 0.0 collective-permute-start.6
  32.2 0.0 collective-permute-done.7
  32.2 2.1 %collective-permute-done.8 = f32[72,128]{1,0:T(8,128)S(1)} collective-permute-done((f32[72,128]{1,0:T(8,128)S(1)}, f32[72,128]{1,0:T(8,128)S(1)}, u32[]{:S(2)}, u32[]{:S(2)}) %collective-permute-start.8) | collective-permute-done | bytes 36896 | tf_op jit(solution)/shard_map/ppermute | solution.py:420
  34.3 2.2 %collective-permute-done.6 = f32[72,128]{1,0:T(8,128)S(1)} collective-permute-done((f32[72,128]{1,0:T(8,128)S(1)}, f32[72,128]{1,0:T(8,128)S(1)}, u32[]{:S(2)}, u32[]{:S(2)}) %collective-permute-start.6) | collective-permute-done | bytes 36896 | tf_op jit(solution)/shard_map/ppermute | solution.py:420
  36.6 3.1 %collective-permute-start.10 = (f32[72,128]{1,0:T(8,128)S(1)}, f32[72,128]{1,0:T(8,128)S(1)}, u32[]{:S(2)}, u32[]{:S(2)}) collective-permute-start(f32[72,128]{1,0:T(8,128)S(1)} %add_add_fusion.1), channel_id=1, source_target_pairs={{0,8},{1,9},{2,10},{3,11},{4,12},{5,13},{6,14},{7,15},{8,0},{9,1},... | collective-permute-start | bytes 110600 | tf_op jit(solution)/shard_map/ppermute | solution.py:420
  39.6 0.7 %collective-permute-start.11 = (f32[72,128]{1,0:T(8,128)S(1)}, f32[72,128]{1,0:T(8,128)S(1)}, u32[]{:S(2)}, u32[]{:S(2)}) collective-permute-start(f32[72,128]{1,0:T(8,128)S(1)} %add_add_fusion.1), channel_id=1, source_target_pairs={{0,12},{1,13},{2,14},{3,15},{4,8},{5,9},{6,10},{7,11},{8,4},{9,5},... | collective-permute-start | bytes 110600 | tf_op jit(solution)/shard_map/ppermute | solution.py:420
  40.4 0.0 collective-permute-start.9
  40.4 0.6 %collective-permute-done.10 = f32[72,128]{1,0:T(8,128)S(1)} collective-permute-done((f32[72,128]{1,0:T(8,128)S(1)}, f32[72,128]{1,0:T(8,128)S(1)}, u32[]{:S(2)}, u32[]{:S(2)}) %collective-permute-start.10) | collective-permute-done | bytes 36896 | tf_op jit(solution)/shard_map/ppermute | solution.py:420
  41.0 3.3 %collective-permute-done.11 = f32[72,128]{1,0:T(8,128)S(1)} collective-permute-done((f32[72,128]{1,0:T(8,128)S(1)}, f32[72,128]{1,0:T(8,128)S(1)}, u32[]{:S(2)}, u32[]{:S(2)}) %collective-permute-start.11) | collective-permute-done | bytes 36896 | tf_op jit(solution)/shard_map/ppermute | solution.py:420
  44.2 0.0 collective-permute-done.9
  44.3 3.3 %collective-permute-start.12 = (f32[72,128]{1,0:T(8,128)S(1)}, f32[72,128]{1,0:T(8,128)S(1)}, u32[]{:S(2)}, u32[]{:S(2)}) collective-permute-start(f32[72,128]{1,0:T(8,128)S(1)} %add_add_fusion), channel_id=1, source_target_pairs={{0,140},{1,141},{2,142},{3,143},{4,136},{5,137},{6,138},{7,139},{8... | collective-permute-start | bytes 110600 | tf_op jit(solution)/shard_map/ppermute | solution.py:422
  47.6 1.3 %collective-permute-done.12 = f32[72,128]{1,0:T(8,128)S(1)} collective-permute-done((f32[72,128]{1,0:T(8,128)S(1)}, f32[72,128]{1,0:T(8,128)S(1)}, u32[]{:S(2)}, u32[]{:S(2)}) %collective-permute-start.12) | collective-permute-done | bytes 36896 | tf_op jit(solution)/shard_map/ppermute | solution.py:422
  48.9 5.6 %collective-permute-start.13 = (f32[72,128]{1,0:T(8,128)S(1)}, f32[72,128]{1,0:T(8,128)S(1)}, u32[]{:S(2)}, u32[]{:S(2)}) collective-permute-start(f32[72,128]{1,0:T(8,128)S(1)} %add.48.mine), channel_id=1, source_target_pairs={{0,16},{1,17},{2,18},{3,19},{4,20},{5,21},{6,22},{7,23},{8,24},{9,... | collective-permute-start | bytes 110600 | tf_op jit(solution)/shard_map/ppermute | solution.py:423
  54.5 0.9 %collective-permute-done.13.other = f32[72,128]{1,0:T(8,128)S(1)} collective-permute-done((f32[72,128]{1,0:T(8,128)S(1)}, f32[72,128]{1,0:T(8,128)S(1)}, u32[]{:S(2)}, u32[]{:S(2)}) %collective-permute-start.13) | collective-permute-done | bytes 36896 | tf_op jit(solution)/shard_map/ppermute | solution.py:423
  55.4 0.8 %unpack.1 = (f32[27,4,16]{2,1,0:T(4,128)}, f32[1,16]{1,0:T(1,128)}, f32[27,16,32]{2,1,0:T(8,128)}, f32[1,32]{1,0:T(1,128)}) custom-call(s32[1]{0:T(128)} %bitcast.11.core, f32[72,128]{1,0:T(8,128)S(1)} %add.48.mine, f32[72,128]{1,0:T(8,128)S(1)} %collective-permute-done.13.other), custom_call_target="tpu_custom_call" | custom-call | tf_op jit(solution)/shard_map/unpack/pallas_call | solution.py:374
  (7 shorter events, 0.1 us)
Async XLA Ops:
  0.6 6.7 %copy-start.5 = (bf16[16,4,3,3,3]{0,1,4,3,2:T(4,128)(2,1)S(1)}, bf16[16,4,3,3,3]{0,1,4,3,2:T(4,128)(2,1)}, u32[]{:S(2)}) copy-start(bf16[16,4,3,3,3]{0,1,4,3,2:T(4,128)(2,1)} %param.7) | copy-start | bytes 10372
  0.6 6.7 %copy-start.2 = (bf16[32,16,3,3,3]{0,1,4,3,2:T(8,128)(2,1)S(1)}, bf16[32,16,3,3,3]{0,1,4,3,2:T(8,128)(2,1)}, u32[]{:S(2)}) copy-start(bf16[32,16,3,3,3]{0,1,4,3,2:T(8,128)(2,1)} %param.9) | copy-start | bytes 82948
  0.7 6.7 %copy-start.3 = (f32[16]{0:T(128)S(1)}, f32[16]{0:T(128)}, u32[]{:S(2)}) copy-start(f32[16]{0:T(128)} %param.8) | copy-start | bytes 196
  0.7 6.7 %copy-start.4 = (f32[32]{0:T(128)S(1)}, f32[32]{0:T(128)}, u32[]{:S(2)}) copy-start(f32[32]{0:T(128)} %param.10) | copy-start | bytes 388
  1.8 9.7 %copy-start = (bf16[1,4,8,8,256]{4,3,2,1,0:T(8,128)(2,1)S(1)}, bf16[1,4,8,8,256]{4,3,2,1,0:T(8,128)(2,1)}, u32[]{:S(2)}) copy-start(bf16[1,4,8,8,256]{4,3,2,1,0:T(8,128)(2,1)} %param.6) | copy-start | bytes 393220
  1.8 9.7 %copy-start.1 = (bf16[1,32,4,4,128]{4,3,2,1,0:T(4,128)(2,1)S(1)}, bf16[1,32,4,4,128]{4,3,2,1,0:T(4,128)(2,1)}, u32[]{:S(2)}) copy-start(bf16[1,32,4,4,128]{4,3,2,1,0:T(4,128)(2,1)} %param.11) | copy-start | bytes 393220
  1.8 6.2 %collective-permute-start = (bf16[28,8,256]{2,1,0:T(8,128)(2,1)S(1)}, bf16[28,8,256]{2,1,0:T(8,128)(2,1)S(1)}, u32[]{:S(2)}, u32[]{:S(2)}) collective-permute-start(bf16[28,8,256]{2,1,0:T(8,128)(2,1)S(1)} %get-tuple-element.20), channel_id=1, source_target_pairs={{0,1},{1,2},{2,3},{3,4},{4,5},{5,6},{6,7},{7,8},{8,9},{9,10},{10,1... | collective-permute-start | bytes 344072 | tf_op jit(solution)/shard_map/ppermute | solution.py:443
  6.0 5.5 %collective-permute-start.1 = (bf16[28,8,256]{2,1,0:T(8,128)(2,1)S(1)}, bf16[28,8,256]{2,1,0:T(8,128)(2,1)S(1)}, u32[]{:S(2)}, u32[]{:S(2)}) collective-permute-start(bf16[28,8,256]{2,1,0:T(8,128)(2,1)S(1)} %get-tuple-element.21), channel_id=1, source_target_pairs={{1,0},{2,1},{3,2},{4,3},{5,4},{6,5},{7,6},{8,7},{9,8},{10,9},{11,1... | collective-permute-start | bytes 344072 | tf_op jit(solution)/shard_map/ppermute | solution.py:444
  16.8 3.1 %collective-permute-start.2 = (f32[72,128]{1,0:T(8,128)S(1)}, f32[72,128]{1,0:T(8,128)S(1)}, u32[]{:S(2)}, u32[]{:S(2)}) collective-permute-start(f32[72,128]{1,0:T(8,128)S(1)} %slice_select_fusion), channel_id=1, source_target_pairs={{0,16},{1,17},{2,18},{3,19},{4,20},{5,21},{6,22},{7,23},{8,24},{9,... | collective-permute-start | bytes 110600 | tf_op jit(solution)/shard_map/ppermute | solution.py:418
  19.9 2.9 %collective-permute-start.4 = (f32[72,128]{1,0:T(8,128)S(1)}, f32[72,128]{1,0:T(8,128)S(1)}, u32[]{:S(2)}, u32[]{:S(2)}) collective-permute-start(f32[72,128]{1,0:T(8,128)S(1)} %select_add_fusion), channel_id=1, source_target_pairs={{0,32},{1,33},{2,34},{3,35},{4,36},{5,37},{6,38},{7,39},{8,40},{9,... | collective-permute-start | bytes 110600 | tf_op jit(solution)/shard_map/ppermute | solution.py:420
  21.2 3.9 %collective-permute-start.5 = (f32[72,128]{1,0:T(8,128)S(1)}, f32[72,128]{1,0:T(8,128)S(1)}, u32[]{:S(2)}, u32[]{:S(2)}) collective-permute-start(f32[72,128]{1,0:T(8,128)S(1)} %select_add_fusion), channel_id=1, source_target_pairs={{0,33},{1,32},{2,35},{3,34},{4,37},{5,36},{6,39},{7,38},{8,41},{9,... | collective-permute-start | bytes 110600 | tf_op jit(solution)/shard_map/ppermute | solution.py:420
  22.4 3.0 %collective-permute-start.3 = (f32[72,128]{1,0:T(8,128)S(1)}, f32[72,128]{1,0:T(8,128)S(1)}, u32[]{:S(2)}, u32[]{:S(2)}) collective-permute-start(f32[72,128]{1,0:T(8,128)S(1)} %select_add_fusion), channel_id=1, source_target_pairs={{0,1},{1,0},{2,3},{3,2},{4,5},{5,4},{6,7},{7,6},{8,9},{9,8},{10,11... | collective-permute-start | bytes 110600 | tf_op jit(solution)/shard_map/ppermute | solution.py:420
  25.4 6.8 %collective-permute-start.7 = (f32[72,128]{1,0:T(8,128)S(1)}, f32[72,128]{1,0:T(8,128)S(1)}, u32[]{:S(2)}, u32[]{:S(2)}) collective-permute-start(f32[72,128]{1,0:T(8,128)S(1)} %add_add_fusion.2), channel_id=1, source_target_pairs={{0,96},{1,97},{2,98},{3,99},{4,100},{5,101},{6,102},{7,103},{8,104... | collective-permute-start | bytes 110600 | tf_op jit(solution)/shard_map/ppermute | solution.py:420
  28.2 6.1 %collective-permute-start.8 = (f32[72,128]{1,0:T(8,128)S(1)}, f32[72,128]{1,0:T(8,128)S(1)}, u32[]{:S(2)}, u32[]{:S(2)}) collective-permute-start(f32[72,128]{1,0:T(8,128)S(1)} %add_add_fusion.2), channel_id=1, source_target_pairs={{0,99},{1,98},{2,97},{3,96},{4,103},{5,102},{6,101},{7,100},{8,107... | collective-permute-start | bytes 110600 | tf_op jit(solution)/shard_map/ppermute | solution.py:420
  32.2 4.3 %collective-permute-start.6 = (f32[72,128]{1,0:T(8,128)S(1)}, f32[72,128]{1,0:T(8,128)S(1)}, u32[]{:S(2)}, u32[]{:S(2)}) collective-permute-start(f32[72,128]{1,0:T(8,128)S(1)} %add_add_fusion.2), channel_id=1, source_target_pairs={{0,3},{1,2},{2,1},{3,0},{4,7},{5,6},{6,5},{7,4},{8,11},{9,10},{10,... | collective-permute-start | bytes 110600 | tf_op jit(solution)/shard_map/ppermute | solution.py:420
  36.6 4.4 %collective-permute-start.10 = (f32[72,128]{1,0:T(8,128)S(1)}, f32[72,128]{1,0:T(8,128)S(1)}, u32[]{:S(2)}, u32[]{:S(2)}) collective-permute-start(f32[72,128]{1,0:T(8,128)S(1)} %add_add_fusion.1), channel_id=1, source_target_pairs={{0,8},{1,9},{2,10},{3,11},{4,12},{5,13},{6,14},{7,15},{8,0},{9,1},... | collective-permute-start | bytes 110600 | tf_op jit(solution)/shard_map/ppermute | solution.py:420
  39.6 4.6 %collective-permute-start.11 = (f32[72,128]{1,0:T(8,128)S(1)}, f32[72,128]{1,0:T(8,128)S(1)}, u32[]{:S(2)}, u32[]{:S(2)}) collective-permute-start(f32[72,128]{1,0:T(8,128)S(1)} %add_add_fusion.1), channel_id=1, source_target_pairs={{0,12},{1,13},{2,14},{3,15},{4,8},{5,9},{6,10},{7,11},{8,4},{9,5},... | collective-permute-start | bytes 110600 | tf_op jit(solution)/shard_map/ppermute | solution.py:420
  40.4 3.9 %collective-permute-start.9 = (f32[72,128]{1,0:T(8,128)S(1)}, f32[72,128]{1,0:T(8,128)S(1)}, u32[]{:S(2)}, u32[]{:S(2)}) collective-permute-start(f32[72,128]{1,0:T(8,128)S(1)} %add_add_fusion.1), channel_id=1, source_target_pairs={{0,4},{1,5},{2,6},{3,7},{4,0},{5,1},{6,2},{7,3},{8,12},{9,13},{10,... | collective-permute-start | bytes 110600 | tf_op jit(solution)/shard_map/ppermute | solution.py:420
  44.3 4.7 %collective-permute-start.12 = (f32[72,128]{1,0:T(8,128)S(1)}, f32[72,128]{1,0:T(8,128)S(1)}, u32[]{:S(2)}, u32[]{:S(2)}) collective-permute-start(f32[72,128]{1,0:T(8,128)S(1)} %add_add_fusion), channel_id=1, source_target_pairs={{0,140},{1,141},{2,142},{3,143},{4,136},{5,137},{6,138},{7,139},{8... | collective-permute-start | bytes 110600 | tf_op jit(solution)/shard_map/ppermute | solution.py:422
  48.9 6.4 %collective-permute-start.13 = (f32[72,128]{1,0:T(8,128)S(1)}, f32[72,128]{1,0:T(8,128)S(1)}, u32[]{:S(2)}, u32[]{:S(2)}) collective-permute-start(f32[72,128]{1,0:T(8,128)S(1)} %add.48.mine), channel_id=1, source_target_pairs={{0,16},{1,17},{2,18},{3,19},{4,20},{5,21},{6,22},{7,23},{8,24},{9,... | collective-permute-start | bytes 110600 | tf_op jit(solution)/shard_map/ppermute | solution.py:423
